TPU v7x, 32 devices: a whole 2x2x4 slice. The times are simulated.
32 devices in a mesh: ctx: 8 (over z, x), lat: 4 (over y, core).
Axes of the slice: x: 2, y: 2, z: 4, core: 2. Of those that a mesh axis runs over, the one named last changes fastest.
Arguments:
- token_ids: int32 [4096], P('ctx'), may hold values from 0 to 255
- latent_offset: int32 [1], replicated, may hold values from 2944 to 3072
- embed_table: bfloat16 [256, 2048], replicated, may hold values from -6 to 6
- cross_q: bfloat16 [2048, 2048], P('ctx', 'lat')
- cross_kv: bfloat16 [2, 2048, 2048], P(None, 'ctx', 'lat')
- cross_out: bfloat16 [2048, 2048], P('lat'), may hold values from -0.375 to 0.375
- self_qkv: bfloat16 [3, 2048, 2048], P(None, None, 'lat')
- self_out: bfloat16 [2048, 2048], P('lat'), may hold values from -0.25 to 0.25
- mlp_in: bfloat16 [2048, 8192], P(None, 'ctx'), may hold values from -0.125 to 0.125
- mlp_out: bfloat16 [8192, 2048], P('ctx'), may hold values from -0.0625 to 0.0625
Outputs:
- latent_out: bfloat16 [4, 256, 2048], P('lat', 'ctx')
Inputs may be any that keep to these rules, and one draw needn't show every extreme that they name: `latent_offset`: the latent rows lie inside the context.
All inputs are finite; a program needn't handle non-finite values.
Results may differ from a plain program's by a relative error of at most 0.014.
Values may be sent and summed in bfloat16 or wider, within the bound.
No kernel may reach another device: no remote copies, remote signals or barrier semaphores. Data moves between devices by JAX's collectives and lax.ppermute only.
A program may use at most 128 MiB of HBM per device.

v0:
```python
import math

import jax
import jax.numpy as jnp
from jax import lax
from jax.sharding import PartitionSpec as P

HD = 128
LATENTS = 1024


EPSILON = 1e-06
MASKED = -1e30


def rms_normalize(values):
    return values * lax.rsqrt(jnp.mean(values * values, axis=-1, keepdims=True) + EPSILON)


def sinusoid(places, width):
    index = jnp.arange(width // 2).astype(jnp.float32)
    rates = jnp.exp(index * (-2.0 * math.log(10000.0) / width))
    angles = places.astype(jnp.float32)[:, None] * rates[None, :]
    return jnp.stack([jnp.sin(angles), jnp.cos(angles)], axis=-1).reshape(places.shape[0], width)


def embed_rows(token_rows, table, places):
    vocab_range = jnp.arange(table.shape[0], dtype=jnp.int32)
    one_hot = (token_rows[:, None] == vocab_range[None, :]).astype(jnp.bfloat16)
    looked = jnp.dot(one_hot, table, preferred_element_type=jnp.float32)
    return rms_normalize(looked + sinusoid(places, table.shape[1])).astype(jnp.bfloat16)


def block_attention(queries, keys, values, blocked, head_size):
    scale = 1.0 / math.sqrt(head_size)
    head_count = queries.shape[1] // head_size
    query_rows = queries.shape[0]
    key_rows = keys.shape[0]
    query_heads = jnp.transpose(queries.reshape(query_rows, head_count, head_size), (1, 0, 2))
    key_heads = jnp.transpose(keys.reshape(key_rows, head_count, head_size), (1, 0, 2))
    value_heads = jnp.transpose(values.reshape(key_rows, head_count, head_size), (1, 0, 2))

    def one_head(operands):
        query, key, value = operands
        scores = (
            lax.dot_general(
                query, key, (((1,), (1,)), ((), ())), preferred_element_type=jnp.float32
            )
            * scale
        )
        scores = jnp.where(blocked, MASKED, scores)
        peak = jnp.max(scores, axis=1)
        weights = jnp.exp(scores - peak[:, None]).astype(jnp.bfloat16)
        total = jnp.sum(weights.astype(jnp.float32), axis=1)
        output = jnp.dot(weights, value, preferred_element_type=jnp.float32)
        return (peak, total, output)

    maxima, totals, outputs = lax.map(one_head, (query_heads, key_heads, value_heads))
    merged = jnp.transpose(outputs, (1, 0, 2)).reshape(query_rows, head_count * head_size)
    return (jnp.transpose(maxima), jnp.transpose(totals), merged)


def per_device(
    token_ids,
    latent_offset,
    embed_table,
    cross_q,
    cross_kv,
    cross_out,
    self_qkv,
    self_out,
    mlp_in,
    mlp_out,
):
    context_count = lax.axis_size("ctx")
    group_count = lax.axis_size("lat")
    context_index = lax.axis_index("ctx")
    group_index = lax.axis_index("lat")
    block_length = token_ids.shape[0]
    head_size = HD
    local_width = cross_q.shape[1]
    local_heads = local_width // head_size
    width = embed_table.shape[1]
    offset = latent_offset[0]
    latent_count = LATENTS
    row_count = latent_count // context_count
    group_rows = latent_count // group_count
    places = context_index * block_length + jnp.arange(block_length, dtype=jnp.int32)
    context = embed_rows(token_ids, embed_table, places)
    piece = lax.all_gather(cross_kv, "ctx", axis=1, tiled=True)
    columns = context
    key_sum = jnp.dot(columns, piece[0], preferred_element_type=jnp.float32)
    value_sum = jnp.dot(columns, piece[1], preferred_element_type=jnp.float32)
    keys = key_sum.astype(jnp.bfloat16)
    values = value_sum.astype(jnp.bfloat16)
    every_token = lax.all_gather(token_ids, "ctx", axis=0, tiled=True)
    latent_tokens = lax.dynamic_slice_in_dim(every_token, offset, latent_count, 0)
    latent_places = offset + jnp.arange(latent_count, dtype=jnp.int32)
    latent = embed_rows(latent_tokens, embed_table, latent_places)
    columns = latent
    query_sum = jnp.dot(
        columns,
        lax.all_gather(cross_q, "ctx", axis=0, tiled=True),
        preferred_element_type=jnp.float32,
    )
    queries = query_sum.astype(jnp.bfloat16)
    blocked = places[None, :] > latent_places[:, None]
    maxima, totals, outputs = block_attention(queries, keys, values, blocked, head_size)
    row_start = context_index * row_count
    came_max, came_total, came_out = (
        lax.all_to_all(maxima[:, None, :], "ctx", split_axis=0, concat_axis=1, tiled=True),
        lax.all_to_all(totals[:, None, :], "ctx", split_axis=0, concat_axis=1, tiled=True),
        lax.all_to_all(outputs[:, None, :], "ctx", split_axis=0, concat_axis=1, tiled=True),
    )
    peak = jnp.max(came_max, axis=1, keepdims=True)
    factor = jnp.exp(came_max - peak)
    own_totals = jnp.sum(came_total * factor, axis=1)
    spread = (
        came_out.reshape(row_count, context_count, local_heads, head_size) * factor[:, :, :, None]
    )
    own_outputs = jnp.sum(spread, axis=1).reshape(row_count, local_width)
    attended = (own_outputs / jnp.repeat(own_totals, head_size, axis=1)).astype(jnp.bfloat16)
    own_latent = lax.dynamic_slice_in_dim(latent, row_start, row_count, 0).astype(jnp.float32)
    first_stream = own_latent + lax.psum(
        jnp.dot(attended, cross_out, preferred_element_type=jnp.float32), "lat"
    )
    self_normed = rms_normalize(first_stream).astype(jnp.bfloat16)
    self_queries = jnp.dot(self_normed, self_qkv[0], preferred_element_type=jnp.float32).astype(
        jnp.bfloat16
    )
    self_keys = jnp.dot(self_normed, self_qkv[1], preferred_element_type=jnp.float32).astype(
        jnp.bfloat16
    )
    self_values = jnp.dot(self_normed, self_qkv[2], preferred_element_type=jnp.float32).astype(
        jnp.bfloat16
    )
    all_keys, all_values = (
        lax.all_gather(self_keys, "ctx", axis=0, tiled=True),
        lax.all_gather(self_values, "ctx", axis=0, tiled=True),
    )
    own_places = row_start + jnp.arange(row_count, dtype=jnp.int32)
    later = jnp.arange(latent_count, dtype=jnp.int32)[None, :] > own_places[:, None]
    self_peak, self_totals, self_outputs = block_attention(
        self_queries, all_keys, all_values, later, head_size
    )
    self_attended = (self_outputs / jnp.repeat(self_totals, head_size, axis=1)).astype(jnp.bfloat16)
    second_stream = first_stream + lax.psum(
        jnp.dot(self_attended, self_out, preferred_element_type=jnp.float32).astype(jnp.bfloat16),
        "lat",
    ).astype(jnp.float32)
    mlp_normed = rms_normalize(second_stream).astype(jnp.bfloat16)
    gathered = lax.all_gather(mlp_normed, "ctx", axis=0, tiled=True)
    group_input = lax.dynamic_slice_in_dim(gathered, group_index * group_rows, group_rows, 0)
    pre_hidden = jnp.dot(group_input, mlp_in, preferred_element_type=jnp.float32)
    hidden = jax.nn.gelu(pre_hidden, approximate=True).astype(jnp.bfloat16)
    place = context_index * row_count - group_index * group_rows
    inside = jnp.logical_and(place >= 0, place < group_rows)
    residual = jnp.zeros((group_rows, width), jnp.float32)
    residual = lax.dynamic_update_slice_in_dim(
        residual, second_stream, jnp.clip(place, 0, group_rows - row_count), 0
    )
    residual = jnp.where(inside, residual, 0.0)
    result = lax.psum_scatter(
        jnp.dot(hidden, mlp_out, preferred_element_type=jnp.float32) + residual,
        "ctx",
        scatter_dimension=0,
        tiled=True,
    )
    return result.astype(jnp.bfloat16)[None]


def solution(mesh):
    placed = (
        P("ctx"),
        P(),
        P(),
        P("ctx", "lat"),
        P(None, "ctx", "lat"),
        P("lat", None),
        P(None, None, "lat"),
        P("lat", None),
        P(None, "ctx"),
        P("ctx", None),
    )
    return jax.shard_map(
        per_device, mesh=mesh, in_specs=placed, out_specs=P("lat", "ctx", None), check_vma=False
    )
```

profile of v0, /device:TPU:0, one launch (start us, length us, event | category | flops | bytes accessed | tf_op | source)
XLA Modules:
  0.0 583.0 jit_solution(15255262971799882268)
XLA Ops:
  8.7 14.9 %multiply_sine_fusion = (f32[1024,1024,1]{1,0,2:T(8,128)S(1)}, f32[1024,1024,1]{1,0,2:T(8,128)S(1)}) fusion(f32[1024]{0:T(1024)S(1)} %multiply_exponential_fusion, f32[1024]{0:T(1024)S(1)} %get-tuple-element.182), kind=kLoop, calls=%fused_computation.36 | loop fusion | flops 1048576 | bytes 8396800 | tf_op jit(solution)/shard_map/sin | solution.py:24
  23.6 4.1 pad_maximum_fusion
  27.7 13.4 %copy.44 = f32[1024,1024,2]{0,2,1:T(2,128)} copy(f32[1024,1024,2]{1,0,2:T(8,128)} %pad_maximum_fusion) | data formatting | bytes 16777216 | tf_op jit(solution)/shard_map/stack | solution.py:24
  41.1 10.9 %reshape.288 = f32[1024,2048]{0,1:T(8,128)} reshape(f32[1024,1024,2]{0,2,1:T(2,128)} %copy.44) | data formatting | bytes 16777216 | tf_op jit(solution)/shard_map/reshape | solution.py:24
  52.0 9.3 %copy.45 = f32[1024,2048]{1,0:T(8,128)} copy(f32[1024,2048]{0,1:T(8,128)} %reshape.288) | data formatting | bytes 16777216 | tf_op jit(solution)/shard_map/reshape | solution.py:24
  61.3 7.3 %multiply_sine_fusion.1 = (f32[512,1024,1]{1,0,2:T(8,128)S(1)}, f32[512,1024,1]{1,0,2:T(8,128)S(1)}) fusion(f32[1024]{0:T(1024)S(1)} %multiply_exponential_fusion, f32[512]{0:T(512)S(1)} %get-tuple-element.184), kind=kLoop, calls=%fused_computation.43 | loop fusion | flops 524288 | bytes 4200448 | tf_op jit(solution)/shard_map/sin | solution.py:24
  68.7 2.3 pad_maximum_fusion.1
  70.9 7.3 %copy.47 = f32[512,1024,2]{0,2,1:T(2,128)} copy(f32[512,1024,2]{1,0,2:T(8,128)} %pad_maximum_fusion.1) | data formatting | bytes 8388608 | tf_op jit(solution)/shard_map/stack | solution.py:24
  78.2 6.1 %reshape.290 = f32[512,2048]{0,1:T(8,128)} reshape(f32[512,1024,2]{0,2,1:T(2,128)} %copy.47) | data formatting | bytes 8388608 | tf_op jit(solution)/shard_map/reshape | solution.py:24
  84.3 5.5 copy.48
  89.8 29.1 %all-gather = s32[8,1,512]{2,1,0:T(1,128)S(1)} all-gather(s32[1,1,512]{2,1,0:T(1,128)S(1)} %bitcast.206), channel_id=1, replica_groups=mesh['ctx'=8,'lat'=4] {'ctx'}, dimensions={0}, use_global_device_ids=true | all-gather | bytes 18432 | tf_op jit(solution)/shard_map/all_gather | solution.py:96
  119.1 4.9 multiply_reduce_fusion.1
  124.0 4.6 multiply_reduce_fusion
  128.6 2.4 multiply_convert_fusion
  131.1 5.2 convolution_convert_fusion.1
  136.3 1.3 copy.46
  137.6 4.2 fusion.38
  142.2 5.1 fusion.37
  147.2 1.3 copy.49
  148.5 13.4 %while.28 = (s32[]{:T(128)}, f32[4,1024]{1,0:T(4,128)S(1)}, f32[4,1024]{1,0:T(4,128)S(1)}, f32[4,1024,128]{1,2,0:T(8,128)}, bf16[4,1024,128]{2,1,0:T(8,128)(2,1)...) while((s32[]{:T(128)}, f32[4,1024]{1,0:T(4,128)S(1)}, ...), condition=%wide.region_5.6_spmd.clone, body=%wide.region_2.5_spmd.clone.sunk | while | flops 274200576 | bytes 7383157 | solution.py:58
  148.5 1.4 fusion.112
  151.9 1.4 fusion.112
  153.9 1.2 fusion.113
  155.2 1.4 fusion.112
  158.5 1.4 fusion.112
  162.6 1.9 reduce.4
  165.4 3.7 all-to-all-start.1
  169.3 1.9 reduce.2
  172.1 3.5 all-to-all-done.1
  175.7 3.6 all-to-all-start.2
  179.3 6.1 %copy.52 = f32[1024,1,512]{2,1,0:T(1,128)} copy(f32[1024,1,512]{0,2,1:T(8,128)} %bitcast.190) | data formatting | bytes 4194304 | tf_op jit(solution)/shard_map/broadcast_in_dim;reshape | solution.py:113
  185.8 5.5 all-to-all-start
  194.8 40.8 %all-to-all-done = f32[1024,1,512]{2,1,0:T(1,128)} async-done(((f32[1024,1,512]{2,1,0:T(1,128)}), f32[1024,1,512]{2,1,0:T(1,128)}, u32[]{:S(2)}, u32[]{:S(2)}) %all-to-all-start) | async-done | bytes 2097184 | tf_op jit(solution)/shard_map/all_to_all | solution.py:113
  235.7 4.1 copy.53
  239.9 2.5 fusion.33
  242.5 1.5 fusion.86
  244.1 35.2 %all-reduce.3.cloned.1.call-done = f32[128,2048]{1,0:T(8,128)} async-done(((f32[128,2048]{1,0:T(8,128)}), f32[128,2048]{1,0:T(8,128)}) %all-reduce.3.cloned.1.call-update) | async-done | bytes 1048592 | tf_op jit(solution)/shard_map/psum | solution.py:124
  279.2 1.6 multiply_reduce_fusion.3
  281.7 2.7 fusion.45
  284.5 2.9 fusion.42
  287.5 2.2 fusion.48
  289.7 35.6 %all-gather.13.cloned.1.call-done = bf16[1024,512]{1,0:T(8,128)(2,1)} async-done(((bf16[128,512]{1,0:T(8,128)(2,1)}), bf16[1024,512]{1,0:T(8,128)(2,1)}) %all-gather.13.cloned.1.call-update) | async-done | bytes 1048592 | tf_op jit(solution)/shard_map/all_gather | solution.py:139
  325.3 2.4 bitcast_bitcast_fusion
  327.7 38.6 %all-gather.11.cloned.1.call-done = bf16[1024,512]{1,0:T(8,128)(2,1)} async-done(((bf16[128,512]{1,0:T(8,128)(2,1)}), bf16[1024,512]{1,0:T(8,128)(2,1)}) %all-gather.11.cloned.1.call-update) | async-done | bytes 1048592 | tf_op jit(solution)/shard_map/all_gather | solution.py:138
  366.3 2.4 bitcast_bitcast_fusion.1
  368.8 11.3 %while.29 = (s32[]{:T(128)}, f32[4,128]{1,0:T(4,128)S(1)}, f32[4,128,128]{1,2,0:T(8,128)S(1)}, bf16[4,128,128]{2,1,0:T(8,128)(2,1)S(1)}, bf16[4,1024,128]{2,1,0:...) while((s32[]{:T(128)}, f32[4,128]{1,0:T(4,128)S(1)}, ...), condition=%wide.region_14.15_spmd.clone, body=%wide.region_11.14_spmd.clone.sunk | while | flops 68419328 | bytes 2201185 | solution.py:58
  368.8 1.3 fusion.115
  370.0 1.3 fusion.116
  371.6 1.3 fusion.115
  372.9 1.3 fusion.116
  374.4 1.3 fusion.115
  375.7 1.3 fusion.116
  377.3 1.3 fusion.115
  378.5 1.3 fusion.116
  380.1 2.9 convolution_convert_fusion
  383.1 32.2 %all-reduce.5.cloned.1.call-done = bf16[128,2048]{1,0:T(8,128)(2,1)} async-done(((bf16[128,2048]{1,0:T(8,128)(2,1)}), bf16[128,2048]{1,0:T(8,128)(2,1)}) %all-reduce.5.cloned.1.call-update) | async-done | bytes 524304 | tf_op jit(solution)/shard_map/psum | solution.py:147
  415.3 1.3 multiply_reduce_fusion.2
  416.6 2.0 multiply_convert_fusion.2
  418.6 73.0 %all-gather.15.cloned.1.call-done = bf16[1024,2048]{1,0:T(8,128)(2,1)} async-done(((bf16[128,2048]{1,0:T(8,128)(2,1)}), bf16[1024,2048]{1,0:T(8,128)(2,1)}) %all-gather.15.cloned.1.call-update) | async-done | bytes 4194320 | tf_op jit(solution)/shard_map/all_gather | solution.py:152
  491.6 7.7 %fusion.64 = f32[256,2048]{1,0:T(8,128)} fusion(bf16[1024,2048]{1,0:T(8,128)(2,1)} %param.23, bf16[2048,1024]{1,0:T(8,128)(2,1)} %param.22, bf16[1024,2048]{1,0:T(8,128)(2,1)} %all-gather.15.cloned.1.call-done, s32[]{:T(128)S(6)} %select_n.32), kind=kOutput, calls=%fused_computation.88 | convolution fusion | flops 2149842944 | bytes 11534340 | tf_op jit(solution)/shard_map/dot_general | solution.py:164
  499.3 2.6 select_add_fusion
  501.9 4.3 add.144
  506.2 67.9 %reduce-scatter.2.cloned.1.call-done = f32[32,2048]{1,0:T(8,128)} async-done(((f32[256,2048]{1,0:T(8,128)}), f32[32,2048]{1,0:T(8,128)}) %reduce-scatter.2.cloned.1.call-update) | async-done | bytes 262160 | tf_op jit(solution)/shard_map/reduce_scatter | solution.py:163
  574.1 1.6 convert_bitcast_fusion
  (83 shorter events, 17.4 us)
Async XLA Ops:
  6.5 235.9 %copy-start = (bf16[512,2048]{1,0:T(8,128)(2,1)S(1)}, bf16[512,2048]{1,0:T(8,128)(2,1)}, u32[]{:S(2)}) copy-start(bf16[512,2048]{1,0:T(8,128)(2,1)} %param.19) | copy-start | bytes 6291460
  6.5 124.5 %all-gather.7.cloned.1.call-start = ((), (), s32[]{:S(2)}) async-start(), calls=%async_computation.4 | async-start | bytes 2359296 | tf_op jit(solution)/shard_map/all_gather | solution.py:103
  7.3 130.4 %all-gather.9.cloned.1.call-start = ((), (), s32[]{:S(2)}) async-start(), calls=%async_computation.5 | async-start | bytes 4718592 | tf_op jit(solution)/shard_map/all_gather | solution.py:90
  84.3 5.5 copy-start.3
  84.3 34.8 %copy-start.1 = (bf16[256,2048]{1,0:T(8,128)(2,1)S(1)}, bf16[256,2048]{1,0:T(8,128)(2,1)}, u32[]{:S(2)}) copy-start(bf16[256,2048]{1,0:T(8,128)(2,1)} %param.16) | copy-start | bytes 3145732
  165.4 10.2 %all-to-all-start.1 = ((f32[8,1,512]{2,1,0:T(1,128)}), f32[8,1,512]{2,1,0:T(1,128)S(1)}, u32[]{:S(2)}, u32[]{:S(2)}) async-start(f32[8,1,512]{2,1,0:T(1,128)} %reshape.299), calls=%async_computation.1 | async-start | bytes 32768 | tf_op jit(solution)/shard_map/all_to_all | solution.py:111
  175.7 10.1 %all-to-all-start.2 = ((f32[8,1,512]{2,1,0:T(1,128)}), f32[8,1,512]{2,1,0:T(1,128)S(1)}, u32[]{:S(2)}, u32[]{:S(2)}) async-start(f32[8,1,512]{2,1,0:T(1,128)} %reshape.301), calls=%async_computation.2 | async-start | bytes 32768 | tf_op jit(solution)/shard_map/all_to_all | solution.py:112
  185.8 49.9 %all-to-all-start = ((f32[1024,1,512]{2,1,0:T(1,128)}), f32[1024,1,512]{2,1,0:T(1,128)}, u32[]{:S(2)}, u32[]{:S(2)}) async-start(f32[1024,1,512]{2,1,0:T(1,128)} %copy.52), calls=%async_computation | async-start | bytes 4194304 | tf_op jit(solution)/shard_map/all_to_all | solution.py:113
  191.3 87.9 %all-reduce.3.cloned.1.call-start = ((), (), s32[]{:S(2)}) async-start(), calls=%async_computation.6 | async-start | bytes 2097152 | tf_op jit(solution)/shard_map/psum | solution.py:124
  244.0 81.3 %all-gather.13.cloned.1.call-start = ((), (), s32[]{:S(2)}) async-start(), calls=%async_computation.8 | async-start | bytes 1179648 | tf_op jit(solution)/shard_map/all_gather | solution.py:139
  280.9 0.8 copy-start.2
  284.5 81.9 %all-gather.11.cloned.1.call-start = ((), (), s32[]{:S(2)}) async-start(), calls=%async_computation.7 | async-start | bytes 1179648 | tf_op jit(solution)/shard_map/all_gather | solution.py:138
  287.4 127.9 %all-reduce.5.cloned.1.call-start = ((), (), s32[]{:S(2)}) async-start(), calls=%async_computation.9 | async-start | bytes 1048576 | tf_op jit(solution)/shard_map/psum | solution.py:147
  383.0 108.6 %all-gather.15.cloned.1.call-start = ((), (), s32[]{:S(2)}) async-start(), calls=%async_computation.10 | async-start | bytes 4718592 | tf_op jit(solution)/shard_map/all_gather | solution.py:152
  418.6 155.5 %reduce-scatter.2.cloned.1.call-start = ((), (), s32[]{:S(2)}) async-start(), calls=%async_computation.11 | async-start | bytes 2359296 | tf_op jit(solution)/shard_map/reduce_scatter | solution.py:163
Sparse Core Ops, SparseCore 0:
  9.5 51.8 all-gather.6
  63.6 71.5 all-gather.8
  244.1 35.0 all-reduce.2
  284.6 40.7 all-gather.12
  327.3 38.9 all-gather.10
  383.1 32.1 all-reduce.4
  418.7 72.8 all-gather.14
  506.3 67.7 reduce-scatter.1
where the time goes:
time: 593 us; the launch traced here: 583 us
  waiting for transfers between devices  329 us (55%)
  local copies, waits for them, and re-layouts  81.4 us (14%)
  matrix products  64.4 us (11%)
  other arithmetic  51 us (9%)
  blocking collectives  29.1 us (5%)
  between operations  14.9 us (3%)
  starting transfers between devices  13.1 us (2%)
    all_gather x1, waiting for transfers between devices, per_device(): gathered = lax.all_gather(mlp_normed, 'ctx', axis=0, tiled=True)  73 us
    reduce_scatter x1, waiting for transfers between devices, per_device(): lax.psum_scatter(jnp.dot(hidden, mlp_out, preferred_element_type=jnp.floa...  67.9 us
    all_to_all x1, waiting for transfers between devices, per_device(): lax.all_to_all(outputs[:, None, :], 'ctx', split_axis=0, concat_axis=1, t...  40.8 us
    all_gather x1, waiting for transfers between devices, per_device(): lax.all_gather(self_keys, 'ctx', axis=0, tiled=True)  38.6 us
    all_gather x1, waiting for transfers between devices, per_device(): lax.all_gather(self_values, 'ctx', axis=0, tiled=True)  35.6 us
    psum x1, waiting for transfers between devices, per_device(): lax.psum(jnp.dot(attended, cross_out, preferred_element_type=jnp.float32)...  35.2 us
    psum x1, waiting for transfers between devices, per_device(): lax.psum(jnp.dot(self_attended, self_out, preferred_element_type=jnp.floa...  32.2 us
    reshape x4, local copies, waits for them, and re-layouts, sinusoid(): jnp.stack([jnp.sin(angles), jnp.cos(angles)], axis=-1)  31.8 us
  transfers between devices with their start and end apart: 11, of which 9 were waited for; matrix products, arithmetic and copies ran while one was open for 21% of the time, Pallas kernels for 0%

commit v1 on v0

--- a/solution.py
+++ b/solution.py
@@ -3,6 +3,8 @@
 import jax
 import jax.numpy as jnp
 from jax import lax
+from jax.experimental import pallas as pl
+from jax.experimental.pallas import tpu as pltpu
 from jax.sharding import PartitionSpec as P
 
 HD = 128
@@ -60,7 +62,7 @@
     return (jnp.transpose(maxima), jnp.transpose(totals), merged)
 
 
-def per_device(
+def general_device(
     token_ids,
     latent_offset,
     embed_table,
@@ -169,6 +171,303 @@
     return result.astype(jnp.bfloat16)[None]
 
 
+FINE = 16
+
+
+def rate_row(width):
+    index = (jnp.arange(width, dtype=jnp.int32) // 2).astype(jnp.float32)
+    return jnp.exp(index * (-2.0 * math.log(10000.0) / width))
+
+
+def context_kernel(halves, ids_ref, coarse_ref, fine_ref, table_ref, out_ref, cos_ref, sin_ref):
+    @pl.when(pl.program_id(0) == 0)
+    def _():
+        low_cos, low_sin = fine_ref[2], fine_ref[3]
+        for step in range(FINE):
+            high_cos, high_sin = fine_ref[0, step : step + 1, :], fine_ref[1, step : step + 1, :]
+            rows = pl.ds(step * FINE, FINE)
+            cos_ref[rows, :] = high_cos * low_cos - high_sin * low_sin
+            sin_ref[rows, :] = high_sin * low_cos + high_cos * low_sin
+
+    vocab, width = table_ref.shape
+    rows = out_ref.shape[0]
+    one_hot = (
+        lax.broadcasted_iota(jnp.int32, (vocab, rows), 0) == ids_ref[0]
+    ).astype(jnp.float32).astype(jnp.bfloat16)
+    looked = lax.dot_general(
+        one_hot, table_ref[...], (((0,), (0,)), ((), ())), preferred_element_type=jnp.float32
+    )
+    total = looked + coarse_ref[0, 0:1, :] * cos_ref[...] + coarse_ref[0, 1:2, :] * sin_ref[...]
+    power = jnp.mean(total * total, axis=1, keepdims=True)
+    normed = (total * lax.rsqrt(power + EPSILON)).astype(jnp.bfloat16)
+    part = width // (2 * halves)
+    for half in range(2):
+        for owner in range(halves):
+            source = (owner * 2 + half) * part
+            target = (half * halves + owner) * part
+            out_ref[:, target : target + part] = normed[:, source : source + part]
+
+
+def context_rows(ids, starts, table, owners):
+    count, rows = ids.shape[0], FINE * FINE
+    width = table.shape[1]
+    rates = rate_row(width)
+    odd = (jnp.arange(width, dtype=jnp.int32) % 2)[None, :] == 1
+    angles = starts.astype(jnp.float32)[:, None] * rates[None, :]
+    sines, cosines = jnp.sin(angles), jnp.cos(angles)
+    coarse = jnp.stack(
+        [jnp.where(odd, cosines, sines), jnp.where(odd, -sines, cosines)], axis=1
+    )
+    steps = jnp.arange(FINE, dtype=jnp.float32)
+    high = (steps * FINE)[:, None] * rates[None, :]
+    low = steps[:, None] * rates[None, :]
+    fine = jnp.stack([jnp.cos(high), jnp.sin(high), jnp.cos(low), jnp.sin(low)])
+    return pl.pallas_call(
+        lambda *refs: context_kernel(owners, *refs),
+        grid=(count,),
+        in_specs=[
+            pl.BlockSpec((1, 1, rows), lambda i: (i, 0, 0)),
+            pl.BlockSpec((1, 2, width), lambda i: (i, 0, 0)),
+            pl.BlockSpec((4, FINE, width), lambda i: (0, 0, 0)),
+            pl.BlockSpec(table.shape, lambda i: (0, 0)),
+        ],
+        out_specs=pl.BlockSpec((rows, width), lambda i: (i, 0)),
+        out_shape=jax.ShapeDtypeStruct((count * rows, width), jnp.bfloat16),
+        scratch_shapes=[pltpu.VMEM((rows, width), jnp.float32)] * 2,
+        cost_estimate=pl.CostEstimate(
+            flops=count * rows * width * table.shape[0] * 2,
+            bytes_accessed=count * rows * width * 2,
+            transcendentals=0,
+        ),
+        name="context_rows",
+    )(ids[:, None, :], coarse, fine, table)
+
+
+def attention_kernel(key_block, scale, starts_ref, query_ref, own_ref, other_ref, out_ref):
+    tile = pl.program_id(0)
+    query = query_ref[...]
+    rows, size = query.shape
+    query_place = starts_ref[0, tile] + lax.broadcasted_iota(jnp.int32, (rows, 1), 0)
+    peak = jnp.full((rows, 1), MASKED, jnp.float32)
+    total = jnp.zeros((rows, 1), jnp.float32)
+    output = jnp.zeros((rows, size), jnp.float32)
+    blocks = own_ref.shape[0] // key_block
+    for side, ref in enumerate((own_ref, other_ref)):
+        for block in range(blocks):
+            span = pl.ds(block * key_block, key_block)
+            key, value = ref[span, 0:size], ref[span, size : 2 * size]
+            scores = (
+                lax.dot_general(
+                    query, key, (((1,), (1,)), ((), ())), preferred_element_type=jnp.float32
+                )
+                * scale
+            )
+            key_place = starts_ref[1 + side, block] + lax.broadcasted_iota(
+                jnp.int32, (1, key_block), 1
+            )
+            scores = jnp.where(key_place > query_place, MASKED, scores)
+            new_peak = jnp.maximum(peak, jnp.max(scores, axis=1, keepdims=True))
+            factor = jnp.exp(peak - new_peak)
+            weights = jnp.exp(scores - new_peak).astype(jnp.bfloat16)
+            total = total * factor + jnp.sum(
+                weights.astype(jnp.float32), axis=1, keepdims=True
+            )
+            output = output * factor + jnp.dot(
+                weights, value, preferred_element_type=jnp.float32
+            )
+            peak = new_peak
+    out_ref[...] = (output / total).astype(jnp.bfloat16)
+
+
+def head_attention(query, own, other, query_starts, own_starts, other_starts, tile, key_block):
+    rows, size = query.shape
+    slots = max(query_starts.shape[0], own_starts.shape[0])
+    pad = lambda starts: jnp.pad(starts, (0, slots - starts.shape[0]))
+    starts = jnp.stack([pad(query_starts), pad(own_starts), pad(other_starts)]).astype(jnp.int32)
+    keys = own.shape[0] + other.shape[0]
+    return pl.pallas_call(
+        lambda *refs: attention_kernel(key_block, 1.0 / math.sqrt(size), *refs),
+        grid_spec=pltpu.PrefetchScalarGridSpec(
+            num_scalar_prefetch=1,
+            grid=(rows // tile,),
+            in_specs=[
+                pl.BlockSpec((tile, size), lambda i, s: (i, 0)),
+                pl.BlockSpec(own.shape, lambda i, s: (0, 0)),
+                pl.BlockSpec(other.shape, lambda i, s: (0, 0)),
+            ],
+            out_specs=pl.BlockSpec((tile, size), lambda i, s: (i, 0)),
+        ),
+        out_shape=jax.ShapeDtypeStruct((rows, size), jnp.bfloat16),
+        cost_estimate=pl.CostEstimate(
+            flops=4 * rows * keys * size, bytes_accessed=keys * size * 4, transcendentals=rows * keys
+        ),
+        name="head_attention",
+    )(starts, query, own, other)
+
+
+def dot32(left, right):
+    return jnp.dot(left, right, preferred_element_type=jnp.float32)
+
+
+def paired_device(
+    token_ids,
+    latent_offset,
+    embed_table,
+    cross_q,
+    cross_kv,
+    cross_out,
+    self_qkv,
+    self_out,
+    mlp_in,
+    mlp_out,
+):
+    owners = lax.axis_size("ctx")
+    groups = lax.axis_size("lat")
+    place = lax.axis_index("ctx")
+    group = lax.axis_index("lat")
+    core = group % 2
+    duo = group // 2
+    duos = groups // 2
+    first = core == 0
+    offset = latent_offset[0]
+    block = token_ids.shape[0]
+    width = embed_table.shape[1]
+    share, columns = cross_q.shape
+    heads = columns // HD
+    group_rows = LATENTS // groups
+    rows = group_rows // owners
+    duo_rows = duos * rows
+    half = share // 2
+
+    def swap(value):
+        return lax.ppermute(value, "lat", [(i, i ^ 1) for i in range(groups)])
+
+    def cross(value):
+        return lax.ppermute(value, "lat", [(i, i ^ 2) for i in range(groups)])
+
+    def exchange(value):
+        return lax.all_to_all(value, "ctx", 0, 0, tiled=True)
+
+    def ordered(mine, theirs):
+        return jnp.where(
+            first, jnp.concatenate([mine, theirs]), jnp.concatenate([theirs, mine])
+        )
+
+    every_token = exchange(jnp.broadcast_to(token_ids[None], (owners, block)))
+
+    stacked = jnp.concatenate([cross_q[None], cross_kv]).reshape(3, 2, half, heads, HD)
+    stacked = jnp.transpose(stacked, (1, 3, 2, 0, 4)).reshape(2, heads, half, 3 * HD)
+    mine = lax.dynamic_index_in_dim(stacked, core, 0, keepdims=False)
+    theirs = swap(lax.dynamic_index_in_dim(stacked, 1 - core, 0, keepdims=False))
+    arrived = exchange(ordered(mine, theirs)).reshape(owners * half, 3 * HD)
+    weights = ordered(arrived, swap(arrived))
+
+    cross_out_other = swap(cross_out)
+    self_qkv_other = swap(self_qkv)
+    self_out_other = swap(self_out)
+
+    step = FINE * FINE
+    latent_starts = (2 * jnp.arange(duos, dtype=jnp.int32) + core) * group_rows
+    pieces = block // step
+    half_blocks = owners // 2
+    token_blocks = every_token.reshape(half_blocks, 2, block)
+    own_ids = lax.dynamic_index_in_dim(token_blocks, core, 1, keepdims=False)
+    flat_tokens = every_token.reshape(owners * block)
+    latent_ids = jnp.stack(
+        [
+            lax.dynamic_slice_in_dim(
+                flat_tokens, offset + (2 * i + core) * group_rows, group_rows, 0
+            )
+            for i in range(duos)
+        ]
+    )
+    block_starts = (2 * jnp.arange(half_blocks, dtype=jnp.int32) + core) * block
+    other_starts = (2 * jnp.arange(half_blocks, dtype=jnp.int32) + 1 - core) * block
+    inner = jnp.arange(pieces, dtype=jnp.int32) * step
+    latent_inner = jnp.arange(group_rows // step, dtype=jnp.int32) * step
+    starts = jnp.concatenate(
+        [
+            (block_starts[:, None] + inner[None, :]).reshape(-1),
+            (offset + latent_starts[:, None] + latent_inner[None, :]).reshape(-1),
+        ]
+    )
+    ids = jnp.concatenate([own_ids.reshape(-1, step), latent_ids.reshape(-1, step)])
+    context = context_rows(ids, starts, embed_table, owners)
+    own_context = half_blocks * block
+    latent = context[own_context:]
+
+    pairs = dot32(context[:own_context], weights[:, HD:]).astype(jnp.bfloat16)
+    queries = dot32(latent, weights[:, :HD]).astype(jnp.bfloat16)
+    other_pairs = swap(pairs)
+    tile = group_rows
+    attended = head_attention(
+        queries,
+        pairs,
+        other_pairs,
+        offset + latent_starts,
+        block_starts,
+        other_starts,
+        tile,
+        block,
+    )
+
+    def to_rows(value):
+        value = jnp.transpose(value.reshape(duos, owners, rows, HD), (1, 0, 2, 3))
+        value = exchange(value.reshape(owners, duo_rows, HD))
+        return jnp.transpose(value, (1, 0, 2)).reshape(duo_rows, 2, heads * HD)
+
+    def project(value, mine, theirs):
+        value = jnp.where(first, value, value[:, ::-1])
+        product = dot32(value[:, 0], mine) + dot32(value[:, 1], theirs)
+        product = product.reshape(duos, rows, width)
+        kept = lax.dynamic_index_in_dim(product, duo, 0, keepdims=False)
+        given = lax.dynamic_index_in_dim(product, 1 - duo, 0, keepdims=False)
+        return kept + cross(given.astype(jnp.bfloat16)).astype(jnp.float32)
+
+    own_latent = lax.dynamic_slice_in_dim(latent, duo * group_rows + place * rows, rows, 0)
+    own_latent = jnp.transpose(own_latent.reshape(rows, 2, owners, half), (0, 2, 1, 3))
+    own_latent = own_latent.reshape(rows, width).astype(jnp.float32)
+    first_stream = own_latent + project(to_rows(attended), cross_out, cross_out_other)
+
+    normed = rms_normalize(first_stream).astype(jnp.bfloat16)
+    normed_other = cross(normed)
+    normed = jnp.where(
+        duo == 0,
+        jnp.concatenate([normed, normed_other]),
+        jnp.concatenate([normed_other, normed]),
+    )
+
+    def project_heads(matrices):
+        parts = [dot32(normed, matrices[i]).astype(jnp.bfloat16) for i in range(3)]
+        value = jnp.stack([part.reshape(duo_rows, heads, HD) for part in parts], axis=2)
+        return jnp.transpose(value, (1, 0, 2, 3)).reshape(heads, duo_rows, 3 * HD)
+
+    triples = exchange(ordered(project_heads(self_qkv), project_heads(self_qkv_other)))
+    triples = jnp.transpose(triples.reshape(owners, duos, rows, 3 * HD), (1, 0, 2, 3))
+    triples = triples.reshape(duos * group_rows, 3 * HD)
+    self_pairs = triples[:, HD:]
+    self_attended = head_attention(
+        triples[:, :HD],
+        self_pairs,
+        swap(self_pairs),
+        latent_starts,
+        latent_starts,
+        (2 * jnp.arange(duos, dtype=jnp.int32) + 1 - core) * group_rows,
+        tile,
+        group_rows,
+    )
+    second_stream = first_stream + project(to_rows(self_attended), self_out, self_out_other)
+
+    mlp_normed = rms_normalize(second_stream).astype(jnp.bfloat16)
+    gathered = exchange(jnp.broadcast_to(mlp_normed[None], (owners, rows, width)))
+    pre_hidden = dot32(gathered.reshape(group_rows, width), mlp_in)
+    hidden = jax.nn.gelu(pre_hidden, approximate=True).astype(jnp.bfloat16)
+    shares = dot32(hidden, mlp_out).astype(jnp.bfloat16).reshape(owners, rows, width)
+    shares = exchange(shares)
+    result = second_stream + jnp.sum(shares.astype(jnp.float32), axis=0)
+    return result.astype(jnp.bfloat16)[None]
+
+
 def solution(mesh):
     placed = (
         P("ctx"),
@@ -182,6 +481,13 @@
         P(None, "ctx"),
         P("ctx", None),
     )
+
+    def per_device(*arguments):
+        owners, groups = lax.axis_size("ctx"), lax.axis_size("lat")
+        local_heads = arguments[3].shape[1] // HD
+        paired = groups == 4 and owners == 2 * local_heads
+        return (paired_device if paired else general_device)(*arguments)
+
     return jax.shard_map(
         per_device, mesh=mesh, in_specs=placed, out_specs=P("lat", "ctx", None), check_vma=False
     )

time: 593 us -> 221 us (0.37); the launches traced: 583 us -> 220 us
  waiting for transfers between devices: 329 us -> 38 us
  local copies, waits for them, and re-layouts: 81.4 us -> 14.1 us
  blocking collectives: 29.1 us -> 79.6 us
  other arithmetic: 51 us -> 10.9 us
  matrix products: 64.4 us -> 30.8 us
  Pallas kernels: 0 us -> 24.6 us
  between operations: 14.9 us -> 1.28 us
  starting transfers between devices: 13.1 us -> 20.4 us
    all_gather x5 -> x0, waiting for transfers between devices: 147 us -> none  [the longest x1 73 us: per_device(): gathered = lax.all_gather(mlp_normed, 'ctx', axis=0, tiled=True)]
    all_to_all x0 -> x4, blocking collectives: none -> 79.6 us  [exchange(): return lax.all_to_all(value, 'ctx', 0, 0, tiled=True)]
    reduce_scatter x1 -> x0, waiting for transfers between devices: 67.9 us -> none  [per_device(): lax.psum_scatter(jnp.dot(hidden, mlp_out, preferred_element_type=jnp.floa...]
    psum x2 -> x0, waiting for transfers between devices: 67.4 us -> none  [the longest x1 35.2 us: per_device(): lax.psum(jnp.dot(attended, cross_out, preferred_element_type=jnp.float32)...]
    dot_general x27 -> x13, matrix products: 64.4 us -> 30.8 us  [dot32(): return jnp.dot(left, right, preferred_element_type=jnp.float32)]
    reshape x8, local copies, waits for them, and re-layouts: 34.7 us -> 2.96 us  [the longest x2 2.48 us: to_rows(): value = jnp.transpose(value.reshape(duos, owners, rows, HD), (1, 0, 2, 3))]
    all_gather x1 -> x0, blocking collectives: 29.1 us -> none  [per_device(): every_token = lax.all_gather(token_ids, 'ctx', axis=0, tiled=True)]
    another operation x3 -> x13, local copies, waits for them, and re-layouts: 26.8 us -> 0.75 us  [the longest x12 0.74 us: project_heads(): jnp.stack([part.reshape(duo_rows, heads, HD) for part in parts], axis=2)]
  transfers between devices with their start and end apart: 11 -> 13, of which waited for: 9 -> 9; matrix products, arithmetic and copies ran while one was open for 21% -> 18% of each run, Pallas kernels for 0% -> 11%
where the time goes in v1:
time: 221 us; the launch traced here: 220 us
  blocking collectives  79.6 us (36%)
  waiting for transfers between devices  38 us (17%)
  matrix products  30.8 us (14%)
  Pallas kernels  24.6 us (11%)
  starting transfers between devices  20.4 us (9%)
  local copies, waits for them, and re-layouts  14.1 us (6%)
  other arithmetic  10.9 us (5%)
    all_to_all x4, blocking collectives, exchange(): return lax.all_to_all(value, 'ctx', 0, 0, tiled=True)  79.6 us
    dot_general x13, matrix products, dot32(): return jnp.dot(left, right, preferred_element_type=jnp.float32)  30.8 us
    all_to_all x3, waiting for transfers between devices, exchange(): return lax.all_to_all(value, 'ctx', 0, 0, tiled=True)  28.2 us
    all_to_all x3, starting transfers between devices, exchange(): return lax.all_to_all(value, 'ctx', 0, 0, tiled=True)  14.3 us
    pallas_call x2, Pallas kernels, head_attention(): pl.pallas_call(lambda *refs: attention_kernel(key_block, 1.0 / math.sqrt(...  12.4 us
    pallas_call x1, Pallas kernels, context_rows(): pl.pallas_call(lambda *refs: context_kernel(owners, *refs), grid=(count,)...  12.2 us
    ppermute x3, waiting for transfers between devices, cross(): return lax.ppermute(value, 'lat', [(i, i ^ 2) for i in range(groups)])  8.32 us
    ppermute x3, starting transfers between devices, cross(): return lax.ppermute(value, 'lat', [(i, i ^ 2) for i in range(groups)])  4.74 us
  transfers between devices with their start and end apart: 13, of which 9 were waited for; matrix products, arithmetic and copies ran while one was open for 18% of the time, Pallas kernels for 11%

profile of v1, /device:TPU:0, one launch (start us, length us, event | category | flops | bytes accessed | tf_op | source)
XLA Modules:
  0.0 219.6 jit_solution(17576376696843290303)
XLA Ops:
  0.0 1.2 concatenate.45
  1.2 1.0 concatenate.44
  2.2 0.5 maximum_bitcast_fusion
  2.7 0.6 copy.51
  3.4 0.2 copy.53
  3.7 0.6 collective-permute-start
  4.3 0.2 copy.52
  4.6 0.9 collective-permute-done
  5.6 1.0 maximum_select_fusion.1
  6.6 7.2 %all-to-all-start.1 = ((bf16[8,128,384]{2,1,0:T(8,128)(2,1)}), bf16[8,128,384]{2,1,0:T(8,128)(2,1)S(1)}, u32[]{:S(2)}, u32[]{:S(2)}) async-start(bf16[8,128,384]{2,1,0:T(8,128)(2,1)} %maximum_select_fusion.1), calls=%async_computation.1 | async-start | bytes 1572864 | tf_op jit(solution)/shard_map/all_to_all | solution.py:349
  14.6 2.5 %broadcast_select_fusion.3 = (f32[10,1,2048]{2,1,0:T(1,128)S(1)}, f32[10,1,2048]{2,1,0:T(1,128)S(1)}) fusion(pred[2048]{0:T(1024)(128)(4,1)S(1)} %fusion.61, f32[2048]{0:T(1024)S(1)} %fusion.65, f32[10]{0:T(128)S(1)} %add_convert_fusion.1), kind=kLoop, calls=%fused_computation.70 | loop fusion | flops 81920 | bytes 174120 | tf_op jit(solution)/shard_map/jit(_where)/select_n | solution.py:219
  17.1 0.9 multiply_cosine_fusion
  18.1 16.1 %all-to-all-done.1 = bf16[8,128,384]{2,1,0:T(8,128)(2,1)S(1)} async-done(((bf16[8,128,384]{2,1,0:T(8,128)(2,1)}), bf16[8,128,384]{2,1,0:T(8,128)(2,1)S(1)}, u32[]{:S(2)}, u32[]{:S(2)}) %all-to-all-start.1) | async-done | bytes 786464 | tf_op jit(solution)/shard_map/all_to_all | solution.py:349
  34.2 0.6 broadcast_in_dim.21
  34.8 3.6 %all-to-all-start = ((s32[8,1,512]{2,1,0:T(1,128)}), s32[8,1,512]{2,1,0:T(1,128)S(1)}, u32[]{:S(2)}, u32[]{:S(2)}) async-start(s32[8,1,512]{2,1,0:T(1,128)} %broadcast_in_dim.21), calls=%async_computation | async-start | bytes 32768 | tf_op jit(solution)/shard_map/all_to_all | solution.py:349
  38.5 0.8 pad_maximum_fusion.refs_2_
  39.3 0.8 pad_maximum_fusion.1.refs_1_
  40.1 4.9 %all-to-all-done = s32[8,1,512]{2,1,0:T(1,128)S(1)} async-done(((s32[8,1,512]{2,1,0:T(1,128)}), s32[8,1,512]{2,1,0:T(1,128)S(1)}, u32[]{:S(2)}, u32[]{:S(2)}) %all-to-all-start) | async-done | bytes 16416 | tf_op jit(solution)/shard_map/all_to_all | solution.py:349
  45.2 0.6 broadcast_in_dim.22.refs_0_
  45.8 12.2 %context_rows.1 = bf16[2560,2048]{1,0:T(8,128)(2,1)} custom-call(s32[10,1,256]{2,1,0:T(1,128)} %broadcast_in_dim.22.refs_0_, f32[10,2,2048]{2,1,0:T(2,128)} %pad_maximum_fusion.1.refs_1_, f32[4,16,2048]{2,1,0:T(8,128)} %pad_maximum_fusion.refs_2_, bf16[256,2048]{1,0:T(8,128)(2,1)} %refs_3_.1), custom_call_target="tpu_custom_call" | custom-call | flops 2684354560 | bytes 10485760 | tf_op jit(solution)/shard_map/context_rows/pallas_call | solution.py:225
  58.0 0.4 maximum_select_fusion
  58.4 6.0 %fusion.2.refs_2_ = bf16[2048,256]{1,0:T(8,128)(2,1)S(1)} fusion(bf16[2560,2048]{1,0:T(8,128)(2,1)} %context_rows.1, bf16[2048,384]{1,0:T(8,128)(2,1)S(1)} %maximum_select_fusion), kind=kOutput, calls=%fused_computation.3 | convolution fusion | flops 2148007936 | bytes 10485760 | tf_op jit(solution)/shard_map/dot_general | solution.py:309
  64.5 0.5 collective-permute-start.3
  65.0 0.6 pad_add_fusion.1.refs_0_
  65.6 1.4 convolution_convert_fusion.1.refs_1_
  66.9 0.3 collective-permute-done.2.refs_3_
  67.2 8.2 %head_attention.2 = bf16[512,128]{1,0:T(8,128)(2,1)} custom-call(s32[3,4]{1,0:T(4,128)} %pad_add_fusion.1.refs_0_, bf16[512,128]{1,0:T(8,128)(2,1)} %convolution_convert_fusion.1.refs_1_, bf16[2048,256]{1,0:T(8,128)(2,1)} %copy-done.4, bf16[2048,256]{1,0:T(8,128)(2,1)} %collective-permute-done.2.refs_3_), custom_call_target="tpu_custom_call" | custom-call | flops 1073741824 | bytes 2097152 | tf_op jit(solution)/shard_map/head_attention/pallas_call | solution.py:288
  75.5 1.6 copy.54
  77.0 3.6 %all-to-all-start.2 = ((bf16[8,64,128]{2,1,0:T(8,128)(2,1)}), bf16[8,64,128]{2,1,0:T(8,128)(2,1)S(1)}, u32[]{:S(2)}, u32[]{:S(2)}) async-start(bf16[8,64,128]{2,1,0:T(8,128)(2,1)} %bitcast.13), calls=%async_computation.2 | async-start | bytes 262144 | tf_op jit(solution)/shard_map/all_to_all | solution.py:349
  80.7 7.3 %all-to-all-done.2 = bf16[8,64,128]{2,1,0:T(8,128)(2,1)S(1)} async-done(((bf16[8,64,128]{2,1,0:T(8,128)(2,1)}), bf16[8,64,128]{2,1,0:T(8,128)(2,1)S(1)}, u32[]{:S(2)}, u32[]{:S(2)}) %all-to-all-start.2) | async-done | bytes 131104 | tf_op jit(solution)/shard_map/all_to_all | solution.py:349
  88.1 0.7 rev.6
  89.0 0.5 fusion.58
  89.5 2.1 convolution_add_fusion.1
  91.7 1.6 collective-permute-start.4
  93.2 1.6 slice-done.3
  95.1 0.2 reshape.499
  95.3 1.4 collective-permute-done.4
  97.0 1.6 collective-permute-start.5
  98.5 3.4 %collective-permute-done.5 = bf16[32,2048]{1,0:T(8,128)(2,1)S(1)} collective-permute-done((bf16[32,2048]{1,0:T(8,128)(2,1)S(1)}, bf16[32,2048]{1,0:T(8,128)(2,1)S(1)}, u32[]{:S(2)}, u32[]{:S(2)}) %collective-permute-start.5) | collective-permute-done | bytes 131104 | tf_op jit(solution)/shard_map/ppermute | solution.py:346
  102.0 2.1 fusion.23
  104.2 2.1 fusion.20
  106.4 2.1 fusion.17
  108.6 0.5 maximum_bitcast_fusion.1
  109.2 2.1 fusion.28
  111.4 2.1 fusion.27
  113.6 2.1 fusion.26
  115.8 0.5 maximum_bitcast_fusion.2
  116.6 12.7 %all_to_all.36 = bf16[8,64,384]{2,1,0:T(8,128)(2,1)S(1)} all-to-all(bf16[8,64,384]{2,1,0:T(8,128)(2,1)S(1)} %maximum_select_fusion.2), channel_id=1, replica_groups=mesh['ctx'=8,'lat'=4] {'ctx'}, dimensions={0} | all-to-all | bytes 786432 | tf_op jit(solution)/shard_map/all_to_all | solution.py:349
  129.5 0.6 pad_add_fusion.2.refs_0_
  130.1 0.7 slice.73.refs_1_
  130.7 0.2 collective-permute-done.7.refs_3_
  131.0 0.7 copy-done.5
  131.7 4.1 %head_attention.3 = bf16[512,128]{1,0:T(8,128)(2,1)} custom-call(s32[3,2]{1,0:T(4,128)} %pad_add_fusion.2.refs_0_, bf16[512,128]{1,0:T(8,128)(2,1)} %slice.73.refs_1_, bf16[512,256]{1,0:T(8,128)(2,1)} %copy-done.2, bf16[512,256]{1,0:T(8,128)(2,1)} %copy-done.5), custom_call_target="tpu_custom_call" | custom-call | flops 268435456 | bytes 524288 | tf_op jit(solution)/shard_map/head_attention/pallas_call | solution.py:288
  135.8 0.9 copy.63
  136.7 10.5 %all_to_all.37 = bf16[8,64,128]{2,1,0:T(8,128)(2,1)S(1)} all-to-all(bf16[8,64,128]{2,1,0:T(8,128)(2,1)S(1)} %bitcast.137), channel_id=1, replica_groups=mesh['ctx'=8,'lat'=4] {'ctx'}, dimensions={0} | all-to-all | bytes 262144 | tf_op jit(solution)/shard_map/all_to_all | solution.py:349
  147.4 0.7 rev.7
  148.4 0.5 fusion.53
  148.9 2.1 convolution_add_fusion
  151.0 1.6 collective-permute-start.9
  152.5 3.5 %collective-permute-done.9 = bf16[32,2048]{1,0:T(8,128)(2,1)S(1)} collective-permute-done((bf16[32,2048]{1,0:T(8,128)(2,1)S(1)}, bf16[32,2048]{1,0:T(8,128)(2,1)S(1)}, u32[]{:S(2)}, u32[]{:S(2)}) %collective-permute-start.9) | collective-permute-done | bytes 131104 | tf_op jit(solution)/shard_map/ppermute | solution.py:346
  156.4 27.6 %all_to_all.38 = bf16[8,32,2048]{2,1,0:T(8,128)(2,1)S(1)} all-to-all(bf16[8,32,2048]{2,1,0:T(8,128)(2,1)S(1)} %broadcast_in_dim.24), channel_id=1, replica_groups=mesh['ctx'=8,'lat'=4] {'ctx'}, dimensions={0} | all-to-all | bytes 2097152 | tf_op jit(solution)/shard_map/all_to_all | solution.py:349
  184.0 6.0 %convolution_convert_fusion = bf16[256,2048]{1,0:T(8,128)(2,1)S(1)} fusion(bf16[1024,2048]{1,0:T(8,128)(2,1)} %param.19, bf16[256,2048]{1,0:T(8,128)(2,1)S(1)} %bitcast.131, bf16[2048,1024]{1,0:T(8,128)(2,1)} %param.18), kind=kOutput, calls=%fused_computation.2 | convolution fusion | flops 2150367232 | bytes 10485760 | tf_op jit(solution)/shard_map/dot_general | solution.py:309
  190.0 28.7 %all_to_all.39 = bf16[8,32,2048]{2,1,0:T(8,128)(2,1)S(1)} all-to-all(bf16[8,32,2048]{2,1,0:T(8,128)(2,1)S(1)} %bitcast.132), channel_id=1, replica_groups=mesh['ctx'=8,'lat'=4] {'ctx'}, dimensions={0} | all-to-all | bytes 2097152 | tf_op jit(solution)/shard_map/all_to_all | solution.py:349
  218.9 0.7 fusion.48
  (85 shorter events, 3.8 us)
Async XLA Ops:
  3.7 1.9 collective-permute-start
  4.2 105.0 %collective-permute-start.6 = (bf16[3,2048,512]{2,1,0:T(8,128)(2,1)}, bf16[3,2048,512]{2,1,0:T(8,128)(2,1)}, u32[]{:S(2)}, u32[]{:S(2)}) collective-permute-start(bf16[3,2048,512]{2,1,0:T(8,128)(2,1)} %param.16), channel_id=1, source_target_pairs={{0,1},{1,0},{2,3},{3,2},{4,5},{5,4},{6,7},{7,6},{8,9},{9,8},{10,11... | collective-permute-start | bytes 18874376 | tf_op jit(solution)/shard_map/ppermute | solution.py:343
  4.5 29.7 %copy-start.3 = (s32[512]{0:T(512)S(1)}, s32[512]{0:T(512)}, u32[]{:S(2)}) copy-start(s32[512]{0:T(512)} %param.10) | copy-start | bytes 6148
  6.6 27.6 %all-to-all-start.1 = ((bf16[8,128,384]{2,1,0:T(8,128)(2,1)}), bf16[8,128,384]{2,1,0:T(8,128)(2,1)S(1)}, u32[]{:S(2)}, u32[]{:S(2)}) async-start(bf16[8,128,384]{2,1,0:T(8,128)(2,1)} %maximum_select_fusion.1), calls=%async_computation.1 | async-start | bytes 1572864 | tf_op jit(solution)/shard_map/all_to_all | solution.py:349
  34.8 10.2 %all-to-all-start = ((s32[8,1,512]{2,1,0:T(1,128)}), s32[8,1,512]{2,1,0:T(1,128)S(1)}, u32[]{:S(2)}, u32[]{:S(2)}) async-start(s32[8,1,512]{2,1,0:T(1,128)} %broadcast_in_dim.21), calls=%async_computation | async-start | bytes 32768 | tf_op jit(solution)/shard_map/all_to_all | solution.py:349
  38.4 19.6 %collective-permute-start.1 = (bf16[1024,384]{1,0:T(8,128)(2,1)S(1)}, bf16[1024,384]{1,0:T(8,128)(2,1)S(1)}, u32[]{:S(2)}, u32[]{:S(2)}) collective-permute-start(bf16[1024,384]{1,0:T(8,128)(2,1)S(1)} %bitcast.117), channel_id=1, source_target_pairs={{0,1},{1,0},{2,3},{3,2},{4,5},{5,4},{6,7},{7,6},{8,9},{9,8},{10,11... | collective-permute-start | bytes 2359304 | tf_op jit(solution)/shard_map/ppermute | solution.py:343
  58.0 7.6 %slice-start = ((s8[10485760]{0:T(1024)(128)(4,1)}), s8[4194304]{0:T(1024)(128)(4,1)S(1)}, s32[]{:S(2)}) async-start(s8[10485760]{0:T(1024)(128)(4,1)} %bitcast.114), calls=%async_computation.7 | async-start | bytes 8388608
  58.4 6.1 %copy-start = (bf16[512,2048]{1,0:T(8,128)(2,1)S(1)}, bf16[512,2048]{1,0:T(8,128)(2,1)}, u32[]{:S(2)}) copy-start(bf16[512,2048]{1,0:T(8,128)(2,1)} %param.15) | copy-start | bytes 6291460
  58.4 7.2 %slice-start.1 = ((s8[10485760]{0:T(1024)(128)(4,1)}), s8[4194304]{0:T(1024)(128)(4,1)S(1)}, s32[]{:S(2)}) async-start(s8[10485760]{0:T(1024)(128)(4,1)} %bitcast.114), calls=%async_computation.8 | async-start | bytes 8388608
  58.4 7.2 %slice-start.2 = ((s8[10485760]{0:T(1024)(128)(4,1)}), s8[2097152]{0:T(1024)(128)(4,1)S(1)}, s32[]{:S(2)}) async-start(s8[10485760]{0:T(1024)(128)(4,1)} %bitcast.114), calls=%async_computation.9 | async-start | bytes 4194304
  64.4 2.9 %copy-start.4 = (bf16[2048,256]{1,0:T(8,128)(2,1)}, bf16[2048,256]{1,0:T(8,128)(2,1)S(1)}, u32[]{:S(2)}) copy-start(bf16[2048,256]{1,0:T(8,128)(2,1)S(1)} %fusion.2.refs_2_) | copy-start | bytes 3145732
  64.4 2.9 %collective-permute-start.2 = (bf16[2048,256]{1,0:T(8,128)(2,1)S(1)}, bf16[2048,256]{1,0:T(8,128)(2,1)}, u32[]{:S(2)}, u32[]{:S(2)}) collective-permute-start(bf16[2048,256]{1,0:T(8,128)(2,1)S(1)} %fusion.2.refs_2_), channel_id=1, source_target_pairs={{0,1},{1,0},{2,3},{3,2},{4,5},{5,4},{6,7},{7,6},{8,9},{9,8},{10,11... | collective-permute-start | bytes 3145736 | tf_op jit(solution)/shard_map/ppermute | solution.py:343
  64.5 25.1 %collective-permute-start.3 = (bf16[512,2048]{1,0:T(8,128)(2,1)S(1)}, bf16[512,2048]{1,0:T(8,128)(2,1)}, u32[]{:S(2)}, u32[]{:S(2)}) collective-permute-start(bf16[512,2048]{1,0:T(8,128)(2,1)S(1)} %copy-done), channel_id=1, source_target_pairs={{0,1},{1,0},{2,3},{3,2},{4,5},{5,4},{6,7},{7,6},{8,9},{9,8},{10,11... | collective-permute-start | bytes 6291464 | tf_op jit(solution)/shard_map/ppermute | solution.py:343
  77.0 10.9 %all-to-all-start.2 = ((bf16[8,64,128]{2,1,0:T(8,128)(2,1)}), bf16[8,64,128]{2,1,0:T(8,128)(2,1)S(1)}, u32[]{:S(2)}, u32[]{:S(2)}) async-start(bf16[8,64,128]{2,1,0:T(8,128)(2,1)} %bitcast.13), calls=%async_computation.2 | async-start | bytes 262144 | tf_op jit(solution)/shard_map/all_to_all | solution.py:349
  91.7 5.0 %collective-permute-start.4 = (bf16[32,2048]{1,0:T(8,128)(2,1)S(1)}, bf16[32,2048]{1,0:T(8,128)(2,1)S(1)}, u32[]{:S(2)}, u32[]{:S(2)}) collective-permute-start(bf16[32,2048]{1,0:T(8,128)(2,1)S(1)} %fusion.46), channel_id=1, source_target_pairs={{0,2},{1,3},{2,0},{3,1},{4,6},{5,7},{6,4},{7,5},{8,10},{9,11},{10,... | collective-permute-start | bytes 393224 | tf_op jit(solution)/shard_map/ppermute | solution.py:346
  93.2 1.6 slice-start.3
  94.8 3.7 %copy-start.1 = (bf16[512,2048]{1,0:T(8,128)(2,1)S(1)}, bf16[512,2048]{1,0:T(8,128)(2,1)}, u32[]{:S(2)}) copy-start(bf16[512,2048]{1,0:T(8,128)(2,1)} %param.17) | copy-start | bytes 6291460
  97.0 5.0 %collective-permute-start.5 = (bf16[32,2048]{1,0:T(8,128)(2,1)S(1)}, bf16[32,2048]{1,0:T(8,128)(2,1)S(1)}, u32[]{:S(2)}, u32[]{:S(2)}) collective-permute-start(bf16[32,2048]{1,0:T(8,128)(2,1)S(1)} %multiply_convert_fusion.1), channel_id=1, source_target_pairs={{0,2},{1,3},{2,0},{3,1},{4,6},{5,7},{6,4},{7,5},{8,10},{9,11},{10,... | collective-permute-start | bytes 393224 | tf_op jit(solution)/shard_map/ppermute | solution.py:346
  98.5 50.3 %collective-permute-start.8 = (bf16[512,2048]{1,0:T(8,128)(2,1)S(1)}, bf16[512,2048]{1,0:T(8,128)(2,1)}, u32[]{:S(2)}, u32[]{:S(2)}) collective-permute-start(bf16[512,2048]{1,0:T(8,128)(2,1)S(1)} %copy-done.1), channel_id=1, source_target_pairs={{0,1},{1,0},{2,3},{3,2},{4,5},{5,4},{6,7},{7,6},{8,9},{9,8},{10,11... | collective-permute-start | bytes 6291464 | tf_op jit(solution)/shard_map/ppermute | solution.py:343
  129.4 1.6 copy-start.2
  129.4 1.6 collective-permute-start.7
  131.0 0.7 copy-start.5
  151.0 5.0 %collective-permute-start.9 = (bf16[32,2048]{1,0:T(8,128)(2,1)S(1)}, bf16[32,2048]{1,0:T(8,128)(2,1)S(1)}, u32[]{:S(2)}, u32[]{:S(2)}) collective-permute-start(bf16[32,2048]{1,0:T(8,128)(2,1)S(1)} %fusion.47), channel_id=1, source_target_pairs={{0,2},{1,3},{2,0},{3,1},{4,6},{5,7},{6,4},{7,5},{8,10},{9,11},{10,... | collective-permute-start | bytes 393224 | tf_op jit(solution)/shard_map/ppermute | solution.py:346

commit v2 on v1

--- a/solution.py
+++ b/solution.py
@@ -142,7 +142,7 @@
     )
     own_places = row_start + jnp.arange(row_count, dtype=jnp.int32)
     later = jnp.arange(latent_count, dtype=jnp.int32)[None, :] > own_places[:, None]
-    self_peak, self_totals, self_outputs = block_attention(
+    _, self_totals, self_outputs = block_attention(
         self_queries, all_keys, all_values, later, head_size
     )
     self_attended = (self_outputs / jnp.repeat(self_totals, head_size, axis=1)).astype(jnp.bfloat16)
@@ -172,6 +172,8 @@
 
 
 FINE = 16
+MIB = 1 << 20
+BIG = 58 * MIB
 
 
 def rate_row(width):
@@ -208,9 +210,7 @@
             out_ref[:, target : target + part] = normed[:, source : source + part]
 
 
-def context_rows(ids, starts, table, owners):
-    count, rows = ids.shape[0], FINE * FINE
-    width = table.shape[1]
+def sinusoid_tables(starts, width):
     rates = rate_row(width)
     odd = (jnp.arange(width, dtype=jnp.int32) % 2)[None, :] == 1
     angles = starts.astype(jnp.float32)[:, None] * rates[None, :]
@@ -222,6 +222,13 @@
     high = (steps * FINE)[:, None] * rates[None, :]
     low = steps[:, None] * rates[None, :]
     fine = jnp.stack([jnp.cos(high), jnp.sin(high), jnp.cos(low), jnp.sin(low)])
+    return coarse, fine
+
+
+def context_rows(ids, starts, table, owners):
+    count, rows = ids.shape[0], FINE * FINE
+    width = table.shape[1]
+    coarse, fine = sinusoid_tables(starts, width)
     return pl.pallas_call(
         lambda *refs: context_kernel(owners, *refs),
         grid=(count,),
@@ -239,74 +246,303 @@
             bytes_accessed=count * rows * width * 2,
             transcendentals=0,
         ),
+        compiler_params=pltpu.CompilerParams(vmem_limit_bytes=20 * MIB),
         name="context_rows",
     )(ids[:, None, :], coarse, fine, table)
 
 
-def attention_kernel(key_block, scale, starts_ref, query_ref, own_ref, other_ref, out_ref):
+def attention_kernel(key_tile, places_ref, query_ref, own_ref, other_ref, out_ref):
     tile = pl.program_id(0)
-    query = query_ref[...]
-    rows, size = query.shape
-    query_place = starts_ref[0, tile] + lax.broadcasted_iota(jnp.int32, (rows, 1), 0)
+    parts, rows, size = query_ref.shape
+    query = query_ref[...].reshape(parts * rows, size)
+    rows = parts * rows
+    query_place = (
+        places_ref[0] + tile * places_ref[1] + lax.broadcasted_iota(jnp.int32, (rows, 1), 0)
+    )
     peak = jnp.full((rows, 1), MASKED, jnp.float32)
-    total = jnp.zeros((rows, 1), jnp.float32)
-    output = jnp.zeros((rows, size), jnp.float32)
-    blocks = own_ref.shape[0] // key_block
+    output = jnp.zeros((rows, 2 * size), jnp.float32)
+    outer, blocks, inner, columns = own_ref.shape
+    keys = outer * inner
     for side, ref in enumerate((own_ref, other_ref)):
         for block in range(blocks):
-            span = pl.ds(block * key_block, key_block)
-            key, value = ref[span, 0:size], ref[span, size : 2 * size]
-            scores = (
-                lax.dot_general(
+            pair = ref[:, block, :, columns - 2 * size :].reshape(keys, 2 * size)
+            for part in range(keys // key_tile):
+                span = slice(part * key_tile, (part + 1) * key_tile)
+                key, value = pair[span, :size], pair[span, size:]
+                scores = lax.dot_general(
                     query, key, (((1,), (1,)), ((), ())), preferred_element_type=jnp.float32
                 )
-                * scale
-            )
-            key_place = starts_ref[1 + side, block] + lax.broadcasted_iota(
-                jnp.int32, (1, key_block), 1
-            )
-            scores = jnp.where(key_place > query_place, MASKED, scores)
-            new_peak = jnp.maximum(peak, jnp.max(scores, axis=1, keepdims=True))
-            factor = jnp.exp(peak - new_peak)
-            weights = jnp.exp(scores - new_peak).astype(jnp.bfloat16)
-            total = total * factor + jnp.sum(
-                weights.astype(jnp.float32), axis=1, keepdims=True
-            )
-            output = output * factor + jnp.dot(
-                weights, value, preferred_element_type=jnp.float32
-            )
-            peak = new_peak
-    out_ref[...] = (output / total).astype(jnp.bfloat16)
-
-
-def head_attention(query, own, other, query_starts, own_starts, other_starts, tile, key_block):
-    rows, size = query.shape
-    slots = max(query_starts.shape[0], own_starts.shape[0])
-    pad = lambda starts: jnp.pad(starts, (0, slots - starts.shape[0]))
-    starts = jnp.stack([pad(query_starts), pad(own_starts), pad(other_starts)]).astype(jnp.int32)
-    keys = own.shape[0] + other.shape[0]
+                key_place = (
+                    places_ref[2 + 2 * side]
+                    + block * places_ref[3 + 2 * side]
+                    + part * key_tile
+                    + lax.broadcasted_iota(jnp.int32, (1, key_tile), 1)
+                )
+                scores = jnp.where(key_place > query_place, MASKED, scores)
+                new_peak = jnp.maximum(peak, jnp.max(scores, axis=1, keepdims=True))
+                weights = jnp.exp(scores - new_peak).astype(jnp.bfloat16)
+                output = output * jnp.exp(peak - new_peak) + jnp.dot(
+                    weights,
+                    jnp.concatenate([value, jnp.ones_like(value)], axis=1),
+                    preferred_element_type=jnp.float32,
+                )
+                peak = new_peak
+    final = (output[:, :size] / output[:, size:]).astype(jnp.bfloat16)
+    out_ref[...] = final.reshape(out_ref.shape)
+
+
+def head_attention(triples, own, other, places, key_tile):
+    owners, tiles, rows = triples.shape[:3]
+    keys = 2 * own.shape[0] * own.shape[1] * own.shape[2]
     return pl.pallas_call(
-        lambda *refs: attention_kernel(key_block, 1.0 / math.sqrt(size), *refs),
+        lambda *refs: attention_kernel(key_tile, *refs),
         grid_spec=pltpu.PrefetchScalarGridSpec(
             num_scalar_prefetch=1,
-            grid=(rows // tile,),
+            grid=(tiles,),
             in_specs=[
-                pl.BlockSpec((tile, size), lambda i, s: (i, 0)),
-                pl.BlockSpec(own.shape, lambda i, s: (0, 0)),
-                pl.BlockSpec(other.shape, lambda i, s: (0, 0)),
+                pl.BlockSpec((owners, None, rows, HD), lambda i, s: (0, i, 0, 0)),
+                pl.BlockSpec(own.shape, lambda i, s: (0, 0, 0, 0)),
+                pl.BlockSpec(other.shape, lambda i, s: (0, 0, 0, 0)),
             ],
-            out_specs=pl.BlockSpec((tile, size), lambda i, s: (i, 0)),
+            out_specs=pl.BlockSpec((owners, None, rows, HD), lambda i, s: (0, i, 0, 0)),
         ),
-        out_shape=jax.ShapeDtypeStruct((rows, size), jnp.bfloat16),
+        out_shape=jax.ShapeDtypeStruct((owners, tiles, rows, HD), jnp.bfloat16),
         cost_estimate=pl.CostEstimate(
-            flops=4 * rows * keys * size, bytes_accessed=keys * size * 4, transcendentals=rows * keys
+            flops=8 * owners * tiles * rows * keys * HD,
+            bytes_accessed=keys * HD * 4,
+            transcendentals=owners * tiles * rows * keys,
         ),
+        compiler_params=pltpu.CompilerParams(vmem_limit_bytes=14 * MIB),
         name="head_attention",
-    )(starts, query, own, other)
-
-
-def dot32(left, right):
-    return jnp.dot(left, right, preferred_element_type=jnp.float32)
+    )(places, triples, own, other)
+
+
+def prepare_kernel(core_ref, query_ref, pair_ref, mine_ref, theirs_ref):
+    heads, half, columns = mine_ref.shape
+    size = columns // 3
+    for target, core in ((mine_ref, core_ref[0]), (theirs_ref, 1 - core_ref[0])):
+        rows = pl.ds(pl.multiple_of(core * half, half), half)
+        for head in range(heads):
+            span = slice(head * size, (head + 1) * size)
+            target[head, :, 0:size] = query_ref[rows, span]
+            target[head, :, size : 2 * size] = pair_ref[0, rows, span]
+            target[head, :, 2 * size :] = pair_ref[1, rows, span]
+
+
+def prepare_weights(core, cross_q, cross_kv):
+    share, columns = cross_q.shape
+    shape = jax.ShapeDtypeStruct((columns // HD, share // 2, 3 * HD), jnp.bfloat16)
+    return pl.pallas_call(
+        prepare_kernel,
+        in_specs=[pl.BlockSpec(memory_space=pltpu.SMEM)]
+        + [pl.BlockSpec(memory_space=pltpu.VMEM)] * 2,
+        out_specs=[pl.BlockSpec(memory_space=pltpu.VMEM)] * 2,
+        out_shape=[shape, shape],
+        compiler_params=pltpu.CompilerParams(vmem_limit_bytes=4 * MIB),
+        name="prepare_weights",
+    )(core, cross_q, cross_kv)
+
+
+def project_kernel(scalars_ref, heads_ref, mine_ref, theirs_ref, kept_ref, given_ref):
+    core, duo = scalars_ref[0], scalars_ref[1]
+    half = heads_ref.shape[0] // 2
+    product = 0.0
+    for side, matrix in ((core, mine_ref), (1 - core, theirs_ref)):
+        left = jnp.concatenate([heads_ref[side * half + head] for head in range(half)], axis=1)
+        product += jnp.dot(left, matrix[...], preferred_element_type=jnp.float32)
+    kept_rows = kept_ref.shape[0]
+    low, high = product[:kept_rows], product[kept_rows:]
+    kept_ref[...] = jnp.where(duo == 0, low, high)
+    given_ref[...] = jnp.where(duo == 0, high, low).astype(jnp.bfloat16)
+
+
+IN_VMEM = pl.BlockSpec(memory_space=pltpu.VMEM)
+IN_SMEM = pl.BlockSpec(memory_space=pltpu.SMEM)
+ANYWHERE = pl.BlockSpec(memory_space=pl.ANY)
+
+
+def project_rows(scalars, heads, mine, theirs):
+    _, rows, _ = heads.shape
+    inner, width = mine.shape
+    return pl.pallas_call(
+        project_kernel,
+        in_specs=[IN_SMEM, IN_VMEM, IN_VMEM, IN_VMEM],
+        out_specs=[IN_VMEM, IN_VMEM],
+        out_shape=[
+            jax.ShapeDtypeStruct((rows // 2, width), jnp.float32),
+            jax.ShapeDtypeStruct((rows // 2, width), jnp.bfloat16),
+        ],
+        cost_estimate=pl.CostEstimate(
+            flops=4 * rows * inner * width, bytes_accessed=4 * inner * width, transcendentals=0
+        ),
+        compiler_params=pltpu.CompilerParams(vmem_limit_bytes=8 * MIB),
+        name="project_rows",
+    )(scalars, heads, mine, theirs)
+
+
+def triple_kernel(scale, scalars_ref, rows_ref, mine_ref, theirs_ref, out_ref):
+    core = scalars_ref[0]
+    heads = out_ref.shape[0] // 2
+    for side, matrix in ((core, mine_ref), (1 - core, theirs_ref)):
+        for kind in range(mine_ref.shape[0]):
+            product = jnp.dot(rows_ref[...], matrix[kind], preferred_element_type=jnp.float32)
+            product = (product * (scale if kind == 0 else 1.0)).astype(jnp.bfloat16)
+            for head in range(heads):
+                out_ref[side * heads + head, :, kind * HD : (kind + 1) * HD] = product[
+                    :, head * HD : (head + 1) * HD
+                ]
+
+
+def triple_heads(scalars, rows, mine, theirs):
+    count, _ = rows.shape
+    kinds, inner, columns = mine.shape
+    heads = columns // HD
+    return pl.pallas_call(
+        lambda *refs: triple_kernel(HD**-0.5, *refs),
+        in_specs=[IN_SMEM, IN_VMEM, IN_VMEM, IN_VMEM],
+        out_specs=IN_VMEM,
+        out_shape=jax.ShapeDtypeStruct((2 * heads, count, kinds * HD), jnp.bfloat16),
+        cost_estimate=pl.CostEstimate(
+            flops=4 * kinds * count * inner * columns,
+            bytes_accessed=4 * kinds * inner * columns,
+            transcendentals=0,
+        ),
+        compiler_params=pltpu.CompilerParams(vmem_limit_bytes=16 * MIB),
+        name="triple_heads",
+    )(scalars, rows, mine, theirs)
+
+
+def context_heads_kernel(
+    scale, scalars_ref, context_hbm, mine_hbm, theirs_hbm, pair_ref, query_ref, latent_ref,
+    context_ref, mine_ref, theirs_ref, loaded,
+):
+    core, duo, place = scalars_ref[0], scalars_ref[1], scalars_ref[2]
+    inner = mine_ref.shape[0]
+    size = mine_ref.shape[1] // 3
+    keys = pair_ref.shape[0]
+    owners, _, rows, _ = query_ref.shape
+    tile = owners * rows
+    count = context_ref.shape[0] // tile
+    own = pl.ds(pl.multiple_of(core * inner, inner), inner)
+    other = pl.ds(pl.multiple_of((1 - core) * inner, inner), inner)
+    loads = [
+        pltpu.make_async_copy(mine_hbm, mine_ref, loaded.at[count]),
+        pltpu.make_async_copy(theirs_hbm, theirs_ref, loaded.at[count + 1]),
+    ] + [
+        pltpu.make_async_copy(
+            context_hbm.at[pl.ds(i * tile, tile)], context_ref.at[pl.ds(i * tile, tile)], loaded.at[i]
+        )
+        for i in range(count)
+    ]
+    for load in loads:
+        load.start()
+    loads[0].wait()
+    loads[1].wait()
+
+    def product(span, columns):
+        return jnp.dot(
+            context_ref[span, own], mine_ref[:, columns], preferred_element_type=jnp.float32
+        ) + jnp.dot(
+            context_ref[span, other], theirs_ref[:, columns], preferred_element_type=jnp.float32
+        )
+
+    for index in range(count):
+        loads[2 + index].wait()
+        span = slice(index * tile, (index + 1) * tile)
+        if index * tile < keys:
+            pair_ref[span, :] = product(span, slice(size, 3 * size)).astype(jnp.bfloat16)
+        else:
+            query = (product(span, slice(0, size)) * scale).astype(jnp.bfloat16)
+            query_ref[:, index - keys // tile] = query.reshape(owners, rows, size)
+    start = pl.multiple_of(keys + duo * tile + place * rows, rows)
+    latent = context_ref[pl.ds(start, rows), :]
+    part = inner // owners
+    for half in range(2):
+        for owner in range(owners):
+            source = half * inner + owner * part
+            target = (owner * 2 + half) * part
+            latent_ref[:, target : target + part] = latent[:, source : source + part]
+
+
+def context_heads(scalars, context, mine, theirs, shape):
+    owners, tiles, rows = shape
+    count, width = context.shape
+    tile = owners * rows
+    keys = count - tiles * tile
+    inner, columns = mine.shape
+    size = columns // 3
+    return pl.pallas_call(
+        lambda *refs: context_heads_kernel(size**-0.5, *refs),
+        in_specs=[IN_SMEM] + [ANYWHERE] * 3,
+        out_specs=[IN_VMEM] * 3,
+        out_shape=[
+            jax.ShapeDtypeStruct((keys, 2 * size), jnp.bfloat16),
+            jax.ShapeDtypeStruct((owners, tiles, rows, size), jnp.bfloat16),
+            jax.ShapeDtypeStruct((rows, width), jnp.bfloat16),
+        ],
+        scratch_shapes=[
+            pltpu.VMEM(context.shape, jnp.bfloat16),
+            pltpu.VMEM(mine.shape, jnp.bfloat16),
+            pltpu.VMEM(mine.shape, jnp.bfloat16),
+            pltpu.SemaphoreType.DMA((count // tile + 2,)),
+        ],
+        cost_estimate=pl.CostEstimate(
+            flops=4 * count * inner * columns, bytes_accessed=context.size * 2, transcendentals=0
+        ),
+        compiler_params=pltpu.CompilerParams(vmem_limit_bytes=BIG),
+        name="context_heads",
+    )(scalars, context, mine, theirs)
+
+
+def mlp_kernel(scalars_ref, *refs):
+    group = scalars_ref[3]
+    *refs, hidden_ref = refs
+    count = (len(refs) - 10) // 2
+    blocks, (in_ref, out_ref), rest = refs[:count], refs[count : count + 2], refs[count + 2 :]
+    in_parts, out_parts, shares = rest[:4], rest[4:8], rest[8:]
+    rows = jnp.concatenate([block[...] for block in blocks])
+    depth, units = in_parts[0].shape[0], out_parts[0].shape[0]
+
+    def hidden_of(total):
+        return jax.nn.gelu(total, approximate=True).astype(jnp.bfloat16)
+
+    total = jnp.dot(rows, in_ref[...], preferred_element_type=jnp.float32)
+    share = jnp.dot(hidden_of(total), out_ref[...], preferred_element_type=jnp.float32)
+    quarters = [group, group ^ 2, group ^ 1, group ^ 3]
+    total = 0.0
+    for quarter, part in zip(quarters, in_parts):
+        span = pl.ds(pl.multiple_of(quarter * depth, depth), depth)
+        piece = jnp.concatenate([block[:, span] for block in blocks])
+        total += jnp.dot(piece, part[...], preferred_element_type=jnp.float32)
+    hidden_ref[...] = hidden_of(total)
+    for quarter, part in zip(quarters, out_parts):
+        span = pl.ds(pl.multiple_of(quarter * units, units), units)
+        share += jnp.dot(hidden_ref[:, span], part[...], preferred_element_type=jnp.float32)
+    each = blocks[0].shape[0]
+    for index, target in enumerate(shares):
+        target[...] = share[index * each : (index + 1) * each].astype(target.dtype)
+
+
+def mlp_shares(scalars, blocks, mlp_in, mlp_out, in_parts, out_parts):
+    first = jax.ShapeDtypeStruct(blocks[0].shape, jnp.float32)
+    other = jax.ShapeDtypeStruct(blocks[0].shape, jnp.bfloat16)
+    operands = [*blocks, mlp_in, mlp_out, *in_parts, *out_parts]
+    return pl.pallas_call(
+        mlp_kernel,
+        in_specs=[IN_SMEM] + [IN_VMEM] * len(operands),
+        out_specs=[IN_VMEM] * len(blocks),
+        out_shape=[first] + [other] * (len(blocks) - 1),
+        scratch_shapes=[
+            pltpu.VMEM((len(blocks) * blocks[0].shape[0], mlp_in.shape[1]), jnp.bfloat16)
+        ],
+        cost_estimate=pl.CostEstimate(
+            flops=8 * len(blocks) * blocks[0].size * mlp_in.shape[1],
+            bytes_accessed=8 * mlp_in.size,
+            transcendentals=0,
+        ),
+        compiler_params=pltpu.CompilerParams(vmem_limit_bytes=12 * MIB),
+        name="mlp_shares",
+    )(scalars, *operands)
 
 
 def paired_device(
@@ -331,13 +567,12 @@
     first = core == 0
     offset = latent_offset[0]
     block = token_ids.shape[0]
-    width = embed_table.shape[1]
-    share, columns = cross_q.shape
-    heads = columns // HD
+    share = cross_q.shape[0]
     group_rows = LATENTS // groups
     rows = group_rows // owners
     duo_rows = duos * rows
     half = share // 2
+    scalars = jnp.stack([core, duo, place, group]).astype(jnp.int32)
 
     def swap(value):
         return lax.ppermute(value, "lat", [(i, i ^ 1) for i in range(groups)])
@@ -347,24 +582,24 @@
 
     def exchange(value):
         return lax.all_to_all(value, "ctx", 0, 0, tiled=True)
+
+    def across(value, distance):
+        return lax.ppermute(value, "ctx", [(i, i ^ distance) for i in range(owners)])
+
+    def quarter(matrix):
+        size = matrix.shape[0] // groups
+        return lax.dynamic_slice_in_dim(matrix, group * size, size, 0)
 
     def ordered(mine, theirs):
         return jnp.where(
             first, jnp.concatenate([mine, theirs]), jnp.concatenate([theirs, mine])
         )
 
+    mine, theirs = prepare_weights(scalars, cross_q, cross_kv)
+    sent = ordered(mine, swap(theirs))
+
     every_token = exchange(jnp.broadcast_to(token_ids[None], (owners, block)))
-
-    stacked = jnp.concatenate([cross_q[None], cross_kv]).reshape(3, 2, half, heads, HD)
-    stacked = jnp.transpose(stacked, (1, 3, 2, 0, 4)).reshape(2, heads, half, 3 * HD)
-    mine = lax.dynamic_index_in_dim(stacked, core, 0, keepdims=False)
-    theirs = swap(lax.dynamic_index_in_dim(stacked, 1 - core, 0, keepdims=False))
-    arrived = exchange(ordered(mine, theirs)).reshape(owners * half, 3 * HD)
-    weights = ordered(arrived, swap(arrived))
-
-    cross_out_other = swap(cross_out)
-    self_qkv_other = swap(self_qkv)
-    self_out_other = swap(self_out)
+    arrived = exchange(sent).reshape(owners * half, 3 * HD)
 
     step = FINE * FINE
     latent_starts = (2 * jnp.arange(duos, dtype=jnp.int32) + core) * group_rows
@@ -381,8 +616,15 @@
             for i in range(duos)
         ]
     )
+    fetched = []
+    for matrix in (mlp_in, mlp_out):
+        one = across(quarter(matrix), 1)
+        two = cross(one)
+        three = swap(one)
+        four = swap(two)
+        fetched.append((one, two, three, four))
+
     block_starts = (2 * jnp.arange(half_blocks, dtype=jnp.int32) + core) * block
-    other_starts = (2 * jnp.arange(half_blocks, dtype=jnp.int32) + 1 - core) * block
     inner = jnp.arange(pieces, dtype=jnp.int32) * step
     latent_inner = jnp.arange(group_rows // step, dtype=jnp.int32) * step
     starts = jnp.concatenate(
@@ -393,41 +635,32 @@
     )
     ids = jnp.concatenate([own_ids.reshape(-1, step), latent_ids.reshape(-1, step)])
     context = context_rows(ids, starts, embed_table, owners)
-    own_context = half_blocks * block
-    latent = context[own_context:]
-
-    pairs = dot32(context[:own_context], weights[:, HD:]).astype(jnp.bfloat16)
-    queries = dot32(latent, weights[:, :HD]).astype(jnp.bfloat16)
+    pairs, queries, own_latent = context_heads(
+        scalars, context, arrived, swap(arrived), (owners, duos, rows)
+    )
     other_pairs = swap(pairs)
-    tile = group_rows
+    by_block = (1, half_blocks, block, 2 * HD)
+    places = jnp.stack(
+        [
+            offset + core * group_rows,
+            2 * group_rows,
+            core * block,
+            2 * block,
+            (1 - core) * block,
+            2 * block,
+        ]
+    ).astype(jnp.int32)
     attended = head_attention(
-        queries,
-        pairs,
-        other_pairs,
-        offset + latent_starts,
-        block_starts,
-        other_starts,
-        tile,
-        block,
-    )
-
-    def to_rows(value):
-        value = jnp.transpose(value.reshape(duos, owners, rows, HD), (1, 0, 2, 3))
-        value = exchange(value.reshape(owners, duo_rows, HD))
-        return jnp.transpose(value, (1, 0, 2)).reshape(duo_rows, 2, heads * HD)
-
-    def project(value, mine, theirs):
-        value = jnp.where(first, value, value[:, ::-1])
-        product = dot32(value[:, 0], mine) + dot32(value[:, 1], theirs)
-        product = product.reshape(duos, rows, width)
-        kept = lax.dynamic_index_in_dim(product, duo, 0, keepdims=False)
-        given = lax.dynamic_index_in_dim(product, 1 - duo, 0, keepdims=False)
-        return kept + cross(given.astype(jnp.bfloat16)).astype(jnp.float32)
-
-    own_latent = lax.dynamic_slice_in_dim(latent, duo * group_rows + place * rows, rows, 0)
-    own_latent = jnp.transpose(own_latent.reshape(rows, 2, owners, half), (0, 2, 1, 3))
-    own_latent = own_latent.reshape(rows, width).astype(jnp.float32)
-    first_stream = own_latent + project(to_rows(attended), cross_out, cross_out_other)
+        queries, pairs.reshape(by_block), other_pairs.reshape(by_block), places, block
+    )
+
+    def project(attended, mine, theirs):
+        heads = exchange(attended.reshape(owners, duo_rows, HD))
+        kept, given = project_rows(scalars, heads, mine, theirs)
+        return kept + cross(given).astype(jnp.float32)
+
+    projected = project(attended, cross_out, swap(cross_out))
+    first_stream = own_latent.astype(jnp.float32) + projected
 
     normed = rms_normalize(first_stream).astype(jnp.bfloat16)
     normed_other = cross(normed)
@@ -436,35 +669,30 @@
         jnp.concatenate([normed, normed_other]),
         jnp.concatenate([normed_other, normed]),
     )
-
-    def project_heads(matrices):
-        parts = [dot32(normed, matrices[i]).astype(jnp.bfloat16) for i in range(3)]
-        value = jnp.stack([part.reshape(duo_rows, heads, HD) for part in parts], axis=2)
-        return jnp.transpose(value, (1, 0, 2, 3)).reshape(heads, duo_rows, 3 * HD)
-
-    triples = exchange(ordered(project_heads(self_qkv), project_heads(self_qkv_other)))
-    triples = jnp.transpose(triples.reshape(owners, duos, rows, 3 * HD), (1, 0, 2, 3))
-    triples = triples.reshape(duos * group_rows, 3 * HD)
-    self_pairs = triples[:, HD:]
-    self_attended = head_attention(
-        triples[:, :HD],
-        self_pairs,
-        swap(self_pairs),
-        latent_starts,
-        latent_starts,
-        (2 * jnp.arange(duos, dtype=jnp.int32) + 1 - core) * group_rows,
-        tile,
-        group_rows,
-    )
-    second_stream = first_stream + project(to_rows(self_attended), self_out, self_out_other)
+    self_qkv_other = swap(self_qkv)
+    triples = exchange(triple_heads(scalars, normed, self_qkv, self_qkv_other))
+    triples = triples.reshape(owners, duos, rows, 3 * HD)
+    self_places = jnp.stack(
+        [
+            core * group_rows,
+            2 * group_rows,
+            core * group_rows,
+            2 * group_rows,
+            (1 - core) * group_rows,
+            2 * group_rows,
+        ]
+    ).astype(jnp.int32)
+    self_attended = head_attention(triples, triples, swap(triples), self_places, group_rows)
+    projected = project(self_attended, self_out, swap(self_out))
+    second_stream = first_stream + projected
 
     mlp_normed = rms_normalize(second_stream).astype(jnp.bfloat16)
-    gathered = exchange(jnp.broadcast_to(mlp_normed[None], (owners, rows, width)))
-    pre_hidden = dot32(gathered.reshape(group_rows, width), mlp_in)
-    hidden = jax.nn.gelu(pre_hidden, approximate=True).astype(jnp.bfloat16)
-    shares = dot32(hidden, mlp_out).astype(jnp.bfloat16).reshape(owners, rows, width)
-    shares = exchange(shares)
-    result = second_stream + jnp.sum(shares.astype(jnp.float32), axis=0)
+    distances = [2 * i for i in range(1, owners // 2)]
+    blocks = [mlp_normed] + [across(mlp_normed, distance) for distance in distances]
+    kept, *given = mlp_shares(scalars, blocks, mlp_in, mlp_out, *fetched)
+    result = second_stream + kept
+    for share, distance in zip(given, distances):
+        result = result + across(share, distance).astype(jnp.float32)
     return result.astype(jnp.bfloat16)[None]
 
 
@@ -485,7 +713,7 @@
     def per_device(*arguments):
         owners, groups = lax.axis_size("ctx"), lax.axis_size("lat")
         local_heads = arguments[3].shape[1] // HD
-        paired = groups == 4 and owners == 2 * local_heads
+        paired = groups == 4 and owners == 2 * local_heads and owners & (owners - 1) == 0
         return (paired_device if paired else general_device)(*arguments)
 
     return jax.shard_map(

time: 221 us -> 199 us (0.900)
  blocking collectives: 79.6 us -> 0 us
  waiting for transfers between devices: 38 us -> 82.7 us
  matrix products: 30.8 us -> 0 us
  starting transfers between devices: 20.4 us -> 43.3 us
  Pallas kernels: 24.6 us -> 42.6 us
  local copies, waits for them, and re-layouts: 14.1 us -> 19.5 us
    all_to_all x4 -> x0, blocking collectives: 79.6 us -> none  [exchange(): return lax.all_to_all(value, 'ctx', 0, 0, tiled=True)]
    ppermute x0 -> x8, waiting for transfers between devices: none -> 35.6 us  [across(): lax.ppermute(value, 'ctx', [(i, i ^ distance) for i in range(owners)])]
    dot_general x13 -> x0, matrix products: 30.8 us -> none  [dot32(): return jnp.dot(left, right, preferred_element_type=jnp.float32)]
    pallas_call x2 -> x8, Pallas kernels: 12.4 us -> 33.4 us  [the longest x1 9.56 us: context_heads(): pl.pallas_call(lambda *refs: context_heads_kernel(size ** (-0.5), *refs),...]
    unnamed x19 -> x36, local copies, waits for them, and re-layouts: 0.79 us -> 13.9 us
    ppermute x0 -> x8, starting transfers between devices: none -> 10.7 us  [across(): lax.ppermute(value, 'ctx', [(i, i ^ distance) for i in range(owners)])]
    all_to_all x3 -> x5, starting transfers between devices: 14.3 us -> 23.8 us  [exchange(): return lax.all_to_all(value, 'ctx', 0, 0, tiled=True)]
    all_to_all x3 -> x5, waiting for transfers between devices: 28.2 us -> 33.2 us  [exchange(): return lax.all_to_all(value, 'ctx', 0, 0, tiled=True)]
  transfers between devices with their start and end apart: 13 -> 29, of which waited for: 9 -> 16; matrix products, arithmetic and copies ran while one was open for 18% -> 7% of each run, Pallas kernels for 11% -> 19%
where the time goes in v2:
time: 199 us; the launch traced here: 198 us
  waiting for transfers between devices  82.7 us (42%)
  starting transfers between devices  43.3 us (22%)
  Pallas kernels  42.6 us (21%)
  local copies, waits for them, and re-layouts  19.5 us (10%)
  other arithmetic  9.13 us (5%)
    ppermute x8, waiting for transfers between devices, across(): lax.ppermute(value, 'ctx', [(i, i ^ distance) for i in range(owners)])  35.6 us
    all_to_all x5, waiting for transfers between devices, exchange(): return lax.all_to_all(value, 'ctx', 0, 0, tiled=True)  33.2 us
    all_to_all x5, starting transfers between devices, exchange(): return lax.all_to_all(value, 'ctx', 0, 0, tiled=True)  23.8 us
    unnamed x36, local copies, waits for them, and re-layouts  13.9 us
    ppermute x8, starting transfers between devices, across(): lax.ppermute(value, 'ctx', [(i, i ^ distance) for i in range(owners)])  10.7 us
    pallas_call x1, Pallas kernels, context_heads(): pl.pallas_call(lambda *refs: context_heads_kernel(size ** (-0.5), *refs),...  9.56 us
    pallas_call x1, Pallas kernels, context_rows(): pl.pallas_call(lambda *refs: context_kernel(owners, *refs), grid=(count,)...  9.22 us
    ppermute x5, waiting for transfers between devices, cross(): return lax.ppermute(value, 'lat', [(i, i ^ 2) for i in range(groups)])  8.38 us
  transfers between devices with their start and end apart: 29, of which 16 were waited for; matrix products, arithmetic and copies ran while one was open for 7% of the time, Pallas kernels for 19%

profile of v2, /device:TPU:0, one launch (start us, length us, event | category | flops | bytes accessed | tf_op | source)
XLA Modules:
  0.0 198.2 jit_solution(394725650315118685)
XLA Ops:
  0.1 1.1 copy-done.7
  1.2 0.9 copy-done.8
  2.2 0.7 prepare_weights.1
  2.8 0.6 collective-permute-start
  3.5 0.4 collective-permute-start.6
  4.0 0.8 collective-permute-done
  4.7 1.0 maximum_select_fusion
  5.8 7.2 %all-to-all-start.1 = ((bf16[8,128,384]{2,1,0:T(8,128)(2,1)}), bf16[8,128,384]{2,1,0:T(8,128)(2,1)S(1)}, u32[]{:S(2)}, u32[]{:S(2)}) async-start(bf16[8,128,384]{2,1,0:T(8,128)(2,1)} %maximum_select_fusion), calls=%async_computation.1 | async-start | bytes 1572864 | tf_op jit(solution)/shard_map/all_to_all | solution.py:584
  13.8 2.5 %broadcast_select_fusion.1 = (f32[10,1,2048]{2,1,0:T(1,128)S(1)}, f32[10,1,2048]{2,1,0:T(1,128)S(1)}) fusion(pred[2048]{0:T(1024)(128)(4,1)S(1)} %fusion.3, f32[2048]{0:T(1024)S(1)} %fusion.7, f32[10]{0:T(128)S(1)} %add_convert_fusion.1), kind=kLoop, calls=%fused_computation.14 | loop fusion | flops 81920 | bytes 174120 | tf_op jit(solution)/shard_map/jit(_where)/select_n | solution.py:219
  16.3 0.9 multiply_cosine_fusion
  17.3 16.1 %all-to-all-done.1 = bf16[8,128,384]{2,1,0:T(8,128)(2,1)S(1)} async-done(((bf16[8,128,384]{2,1,0:T(8,128)(2,1)}), bf16[8,128,384]{2,1,0:T(8,128)(2,1)S(1)}, u32[]{:S(2)}, u32[]{:S(2)}) %all-to-all-start.1) | async-done | bytes 786464 | tf_op jit(solution)/shard_map/all_to_all | solution.py:584
  33.4 0.7 broadcast_in_dim.19
  34.1 3.6 %all-to-all-start = ((s32[8,1,512]{2,1,0:T(1,128)}), s32[8,1,512]{2,1,0:T(1,128)S(1)}, u32[]{:S(2)}, u32[]{:S(2)}) async-start(s32[8,1,512]{2,1,0:T(1,128)} %broadcast_in_dim.19), calls=%async_computation | async-start | bytes 32768 | tf_op jit(solution)/shard_map/all_to_all | solution.py:584
  37.9 6.3 %all-to-all-done = s32[8,1,512]{2,1,0:T(1,128)S(1)} async-done(((s32[8,1,512]{2,1,0:T(1,128)}), s32[8,1,512]{2,1,0:T(1,128)S(1)}, u32[]{:S(2)}, u32[]{:S(2)}) %all-to-all-start) | async-done | bytes 16416 | tf_op jit(solution)/shard_map/all_to_all | solution.py:584
  44.5 9.2 %context_rows.1.refs_1_ = bf16[2560,2048]{1,0:T(8,128)(2,1)S(1)} custom-call(s32[10,1,256]{2,1,0:T(1,128)S(1)} %broadcast_in_dim.20.refs_0_, f32[10,2,2048]{2,1,0:T(2,128)S(1)} %pad_maximum_fusion.1.refs_1_, f32[4,16,2048]{2,1,0:T(8,128)S(1)} %pad_maximum_fusion.refs_2_, bf16[256,2048]{1,0:T(8,128)(2,1)S(1)} %copy-done.6), custom_call_target="tpu_custom_call" | custom-call | flops 2684354560 | bytes 10485760 | tf_op jit(solution)/shard_map/context_rows/pallas_call | solution.py:232
  53.7 4.0 %copy-done = bf16[2560,2048]{1,0:T(8,128)(2,1)} copy-done((bf16[2560,2048]{1,0:T(8,128)(2,1)}, bf16[2560,2048]{1,0:T(8,128)(2,1)S(1)}, u32[]{:S(2)}) %copy-start) | copy-done | bytes 10485784
  57.7 9.6 %context_heads.1 = (bf16[2048,256]{1,0:T(8,128)(2,1)}, bf16[8,2,32,128]{3,2,1,0:T(8,128)(2,1)}, bf16[32,2048]{1,0:T(8,128)(2,1)}) custom-call(s32[4]{0:T(128)} %copy-done.10, bf16[2560,2048]{1,0:T(8,128)(2,1)} %copy-done, bf16[1024,384]{1,0:T(8,128)(2,1)} %bitcast.28, bf16[1024,384]{1,0:T(8,128)(2,1)} %collective-permute-done.1.refs_3_), custom_call_target="tpu_custom_call" | custom-call | flops 4026531840 | bytes 10485760 | tf_op jit(solution)/shard_map/context_heads/pallas_call | solution.py:474
  67.5 2.8 %collective-permute-done.2 = bf16[2048,256]{1,0:T(8,128)(2,1)S(1)} collective-permute-done((bf16[2048,256]{1,0:T(8,128)(2,1)}, bf16[2048,256]{1,0:T(8,128)(2,1)S(1)}, u32[]{:S(2)}, u32[]{:S(2)}) %collective-permute-start.2) | collective-permute-done | bytes 1048608 | tf_op jit(solution)/shard_map/ppermute | solution.py:578
  70.2 1.2 copy-done.12
  71.5 0.9 copy-done.13
  72.4 4.6 %head_attention.2 = bf16[8,2,32,128]{3,2,1,0:T(8,128)(2,1)} custom-call(s32[6]{0:T(128)S(1)} %stack.67.refs_0_, bf16[8,2,32,128]{3,2,1,0:T(8,128)(2,1)S(1)} %copy-done.13, bf16[1,4,512,256]{3,2,1,0:T(8,128)(2,1)S(1)} %bitcast.25, bf16[1,4,512,256]{3,2,1,0:T(8,128)(2,1)S(1)} %bitcast.26), custom_call_target="tpu_custom_call" | custom-call | flops 2147483648 | bytes 2097152 | tf_op jit(solution)/shard_map/head_attention/pallas_call | solution.py:297
  77.0 3.6 %all-to-all-start.2 = ((bf16[8,64,128]{2,1,0:T(8,128)(2,1)}), bf16[8,64,128]{2,1,0:T(8,128)(2,1)S(1)}, u32[]{:S(2)}, u32[]{:S(2)}) async-start(bf16[8,64,128]{2,1,0:T(8,128)(2,1)} %bitcast.14), calls=%async_computation.2 | async-start | bytes 262144 | tf_op jit(solution)/shard_map/all_to_all | solution.py:584
  80.7 2.3 %constant_dynamic-slice_fusion.1 = bf16[512,1024]{1,0:T(8,128)(2,1)} fusion(bf16[2048,1024]{1,0:T(8,128)(2,1)} %refs_4_.1, s32[]{:T(128)S(6)} %select_n.106), kind=kLoop, calls=%fused_computation.39 | loop fusion | bytes 2097156 | tf_op jit(solution)/shard_map/dynamic_slice | solution.py:591
  83.0 1.5 collective-permute-start.13
  84.6 3.4 %all-to-all-done.2.heads_ref = bf16[8,64,128]{2,1,0:T(8,128)(2,1)S(1)} async-done(((bf16[8,64,128]{2,1,0:T(8,128)(2,1)}), bf16[8,64,128]{2,1,0:T(8,128)(2,1)S(1)}, u32[]{:S(2)}, u32[]{:S(2)}) %all-to-all-start.2) | async-done | bytes 131104 | tf_op jit(solution)/shard_map/all_to_all | solution.py:584
  88.0 2.4 %project_rows.2 = (f32[32,2048]{1,0:T(8,128)S(1)}, bf16[32,2048]{1,0:T(8,128)(2,1)S(1)}) custom-call(s32[4]{0:T(128)S(1)} %copy-done.11, bf16[8,64,128]{2,1,0:T(8,128)(2,1)S(1)} %all-to-all-done.2.heads_ref, bf16[512,2048]{1,0:T(8,128)(2,1)S(1)} %copy-done.4, bf16[512,2048]{1,0:T(8,128)(2,1)} %collective-permute-done.3.theirs_ref), custom_call_target="tpu_custom_call" | custom-call | flops 268435456 | bytes 4194304 | tf_op jit(solution)/shard_map/project_rows/pallas_call | solution.py:367
  90.4 1.6 collective-permute-start.4
  92.0 2.3 %constant_dynamic-slice_fusion = bf16[256,2048]{1,0:T(8,128)(2,1)} fusion(bf16[1024,2048]{1,0:T(8,128)(2,1)} %refs_5_.1, s32[]{:T(128)S(6)} %select_n.107), kind=kLoop, calls=%fused_computation.38 | loop fusion | bytes 2097156 | tf_op jit(solution)/shard_map/dynamic_slice | solution.py:591
  94.3 0.2 collective-permute-start.17
  94.5 0.9 collective-permute-done.4
  95.5 1.1 multiply_reduce_fusion.1
  96.6 1.0 multiply_convert_fusion.1
  97.6 1.6 collective-permute-start.5
  99.2 3.4 %collective-permute-done.5 = bf16[32,2048]{1,0:T(8,128)(2,1)S(1)} collective-permute-done((bf16[32,2048]{1,0:T(8,128)(2,1)S(1)}, bf16[32,2048]{1,0:T(8,128)(2,1)S(1)}, u32[]{:S(2)}, u32[]{:S(2)}) %collective-permute-start.5) | collective-permute-done | bytes 131104 | tf_op jit(solution)/shard_map/ppermute | solution.py:581
  102.7 2.8 %copy-done.3 = bf16[3,2048,512]{2,1,0:T(8,128)(2,1)S(1)} copy-done((bf16[3,2048,512]{2,1,0:T(8,128)(2,1)S(1)}, bf16[3,2048,512]{2,1,0:T(8,128)(2,1)}, u32[]{:S(2)}) %copy-start.3) | copy-done | bytes 6291480
  105.5 5.8 %triple_heads.1 = bf16[8,64,384]{2,1,0:T(8,128)(2,1)} custom-call(s32[4]{0:T(128)S(1)} %copy-done.11, bf16[64,2048]{1,0:T(8,128)(2,1)S(1)} %maximum_select_fusion.1.refs_1_, bf16[3,2048,512]{2,1,0:T(8,128)(2,1)S(1)} %copy-done.3, bf16[3,2048,512]{2,1,0:T(8,128)(2,1)} %collective-permute-done.6.refs_3_), custom_call_target="tpu_custom_call" | custom-call | flops 805306368 | bytes 12582912 | tf_op jit(solution)/shard_map/triple_heads/pallas_call | solution.py:400
  111.3 4.2 %all-to-all-start.3 = ((bf16[8,64,384]{2,1,0:T(8,128)(2,1)}), bf16[8,64,384]{2,1,0:T(8,128)(2,1)}, u32[]{:S(2)}, u32[]{:S(2)}) async-start(bf16[8,64,384]{2,1,0:T(8,128)(2,1)} %triple_heads.1), calls=%async_computation.3 | async-start | bytes 786432 | tf_op jit(solution)/shard_map/all_to_all | solution.py:584
  115.5 1.6 collective-permute-start.14
  117.1 18.1 %collective-permute-done.17.refs_10_ = bf16[256,2048]{1,0:T(8,128)(2,1)} collective-permute-done((bf16[256,2048]{1,0:T(8,128)(2,1)}, bf16[256,2048]{1,0:T(8,128)(2,1)}, u32[]{:S(2)}, u32[]{:S(2)}) %collective-permute-start.17) | collective-permute-done | bytes 1048608 | tf_op jit(solution)/shard_map/ppermute | solution.py:587
  135.3 1.5 collective-permute-start.18
  136.9 2.0 collective-permute-done.7.refs_3_
  138.9 3.1 %head_attention.3 = bf16[8,2,32,128]{3,2,1,0:T(8,128)(2,1)S(1)} custom-call(s32[6]{0:T(128)S(1)} %stack.70.refs_0_, bf16[8,2,32,384]{3,2,1,0:T(8,128)(2,1)} %bitcast.17.refs_1_.refs_2_, bf16[8,2,32,384]{3,2,1,0:T(8,128)(2,1)} %bitcast.17.refs_1_.refs_2_, bf16[8,2,32,384]{3,2,1,0:T(8,128)(2,1)} %collective-permute-done.7.refs_3_), custom_call_target="tpu_custom_call" | custom-call | flops 536870912 | bytes 524288 | tf_op jit(solution)/shard_map/head_attention/pallas_call | solution.py:297
  141.9 0.6 copy-done.9
  142.6 5.3 %all-to-all-start.4 = ((bf16[8,64,128]{2,1,0:T(8,128)(2,1)}), bf16[8,64,128]{2,1,0:T(8,128)(2,1)S(1)}, u32[]{:S(2)}, u32[]{:S(2)}) async-start(bf16[8,64,128]{2,1,0:T(8,128)(2,1)} %bitcast.24), calls=%async_computation.4 | async-start | bytes 262144 | tf_op jit(solution)/shard_map/all_to_all | solution.py:584
  147.9 7.3 %all-to-all-done.4.heads_ref = bf16[8,64,128]{2,1,0:T(8,128)(2,1)S(1)} async-done(((bf16[8,64,128]{2,1,0:T(8,128)(2,1)}), bf16[8,64,128]{2,1,0:T(8,128)(2,1)S(1)}, u32[]{:S(2)}, u32[]{:S(2)}) %all-to-all-start.4) | async-done | bytes 131104 | tf_op jit(solution)/shard_map/all_to_all | solution.py:584
  155.2 2.6 %project_rows.3 = (f32[32,2048]{1,0:T(8,128)S(1)}, bf16[32,2048]{1,0:T(8,128)(2,1)S(1)}) custom-call(s32[4]{0:T(128)S(1)} %copy-done.11, bf16[8,64,128]{2,1,0:T(8,128)(2,1)S(1)} %all-to-all-done.4.heads_ref, bf16[512,2048]{1,0:T(8,128)(2,1)S(1)} %copy-done.5, bf16[512,2048]{1,0:T(8,128)(2,1)} %collective-permute-done.8.theirs_ref), custom_call_target="tpu_custom_call" | custom-call | flops 268435456 | bytes 4194304 | tf_op jit(solution)/shard_map/project_rows/pallas_call | solution.py:367
  157.8 0.7 collective-permute-start.9
  158.5 0.5 collective-permute-start.19
  159.0 2.3 %collective-permute-done.18.refs_11_ = bf16[256,2048]{1,0:T(8,128)(2,1)} collective-permute-done((bf16[256,2048]{1,0:T(8,128)(2,1)}, bf16[256,2048]{1,0:T(8,128)(2,1)}, u32[]{:S(2)}, u32[]{:S(2)}) %collective-permute-start.18) | collective-permute-done | bytes 1048608 | tf_op jit(solution)/shard_map/ppermute | solution.py:581
  161.3 1.7 collective-permute-done.9
  163.0 1.1 multiply_reduce_fusion
  164.2 1.6 collective-permute-start.10
  165.8 2.4 %collective-permute-start.11 = (bf16[32,2048]{1,0:T(8,128)(2,1)S(1)}, bf16[32,2048]{1,0:T(8,128)(2,1)S(1)}, u32[]{:S(2)}, u32[]{:S(2)}) collective-permute-start(bf16[32,2048]{1,0:T(8,128)(2,1)S(1)} %multiply_convert_fusion.refs_0_), channel_id=1, source_target_pairs={{0,16},{4,20},{8,24},{12,28},{16,0},{20,4},{24,8},{28,12},{1,17},{... | collective-permute-start | bytes 393224 | tf_op jit(solution)/shard_map/ppermute | solution.py:587
  168.2 0.4 collective-permute-start.12
  168.7 2.1 %collective-permute-done.10.refs_1_ = bf16[32,2048]{1,0:T(8,128)(2,1)S(1)} collective-permute-done((bf16[32,2048]{1,0:T(8,128)(2,1)S(1)}, bf16[32,2048]{1,0:T(8,128)(2,1)S(1)}, u32[]{:S(2)}, u32[]{:S(2)}) %collective-permute-start.10) | collective-permute-done | bytes 131104 | tf_op jit(solution)/shard_map/ppermute | solution.py:587
  170.8 7.2 %collective-permute-done.11.refs_2_ = bf16[32,2048]{1,0:T(8,128)(2,1)S(1)} collective-permute-done((bf16[32,2048]{1,0:T(8,128)(2,1)S(1)}, bf16[32,2048]{1,0:T(8,128)(2,1)S(1)}, u32[]{:S(2)}, u32[]{:S(2)}) %collective-permute-start.11) | collective-permute-done | bytes 131104 | tf_op jit(solution)/shard_map/ppermute | solution.py:587
  178.0 2.2 %copy-done.2 = bf16[1024,2048]{1,0:T(8,128)(2,1)S(1)} copy-done((bf16[1024,2048]{1,0:T(8,128)(2,1)S(1)}, bf16[1024,2048]{1,0:T(8,128)(2,1)}, u32[]{:S(2)}) %copy-start.2) | copy-done | bytes 4194328
  180.2 4.6 %mlp_shares.1 = (f32[32,2048]{1,0:T(8,128)S(1)}, bf16[32,2048]{1,0:T(8,128)(2,1)S(1)}, bf16[32,2048]{1,0:T(8,128)(2,1)S(1)}, bf16[32,2048]{1,0:T(8,128)(2,1)S(1)}) custom-call(s32[4]{0:T(128)S(1)} %copy-done.11, bf16[32,2048]{1,0:T(8,128)(2,1)S(1)} %multiply_convert_fusion.refs_0_, bf16[32,2048]{1,0:T(8,128)(2,1)S(1)} %collective-permute-done.10.refs_1_, ...), custom_call_target="tpu_custom_call" | custom-call | flops 2147483648 | bytes 16777216 | tf_op jit(solution)/shard_map/mlp_shares/pallas_call | solution.py:530
  184.8 2.4 %collective-permute-start.23 = (bf16[32,2048]{1,0:T(8,128)(2,1)S(1)}, bf16[32,2048]{1,0:T(8,128)(2,1)S(1)}, u32[]{:S(2)}, u32[]{:S(2)}) collective-permute-start(bf16[32,2048]{1,0:T(8,128)(2,1)S(1)} %get-tuple-element.30), channel_id=1, source_target_pairs={{0,24},{4,28},{8,16},{12,20},{16,8},{20,12},{24,0},{28,4},{1,25},{... | collective-permute-start | bytes 393224 | tf_op jit(solution)/shard_map/ppermute | solution.py:587
  187.2 1.1 collective-permute-start.22
  188.3 0.9 collective-permute-start.21
  189.3 3.8 %collective-permute-done.23 = bf16[32,2048]{1,0:T(8,128)(2,1)S(1)} collective-permute-done((bf16[32,2048]{1,0:T(8,128)(2,1)S(1)}, bf16[32,2048]{1,0:T(8,128)(2,1)S(1)}, u32[]{:S(2)}, u32[]{:S(2)}) %collective-permute-start.23) | collective-permute-done | bytes 131104 | tf_op jit(solution)/shard_map/ppermute | solution.py:587
  193.0 4.4 %collective-permute-done.22 = bf16[32,2048]{1,0:T(8,128)(2,1)S(1)} collective-permute-done((bf16[32,2048]{1,0:T(8,128)(2,1)S(1)}, bf16[32,2048]{1,0:T(8,128)(2,1)S(1)}, u32[]{:S(2)}, u32[]{:S(2)}) %collective-permute-start.22) | collective-permute-done | bytes 131104 | tf_op jit(solution)/shard_map/ppermute | solution.py:587
  197.5 0.7 fusion
  (74 shorter events, 1.5 us)
Async XLA Ops:
  0.0 44.5 %copy-start.6 = (bf16[256,2048]{1,0:T(8,128)(2,1)S(1)}, bf16[256,2048]{1,0:T(8,128)(2,1)}, u32[]{:S(2)}) copy-start(bf16[256,2048]{1,0:T(8,128)(2,1)} %refs_3_.1) | copy-start | bytes 3145732
  0.1 1.1 copy-start.7
  1.2 0.9 copy-start.8
  2.1 51.6 %copy-start.10 = (s32[4]{0:T(128)}, s32[4]{0:T(128)S(1)}, u32[]{:S(2)}) copy-start(s32[4]{0:T(128)S(1)} %pad_add_fusion.1.core_ref.refs_0_.scalars_ref) | copy-start | bytes 52
  2.1 31.2 %copy-start.17 = (s32[512]{0:T(512)S(1)}, s32[512]{0:T(512)}, u32[]{:S(2)}) copy-start(s32[512]{0:T(512)} %param.10) | copy-start | bytes 6148
  2.8 1.9 collective-permute-start
  3.4 81.2 %collective-permute-start.3 = (bf16[512,2048]{1,0:T(8,128)(2,1)}, bf16[512,2048]{1,0:T(8,128)(2,1)}, u32[]{:S(2)}, u32[]{:S(2)}) collective-permute-start(bf16[512,2048]{1,0:T(8,128)(2,1)} %mine_ref.2), channel_id=1, source_target_pairs={{0,1},{1,0},{2,3},{3,2},{4,5},{5,4},{6,7},{7,6},{8,9},{9,8},{10,11... | collective-permute-start | bytes 6291464 | tf_op jit(solution)/shard_map/ppermute | solution.py:578
  3.5 99.2 %collective-permute-start.6 = (bf16[3,2048,512]{2,1,0:T(8,128)(2,1)}, bf16[3,2048,512]{2,1,0:T(8,128)(2,1)}, u32[]{:S(2)}, u32[]{:S(2)}) collective-permute-start(bf16[3,2048,512]{2,1,0:T(8,128)(2,1)} %refs_2_.1), channel_id=1, source_target_pairs={{0,1},{1,0},{2,3},{3,2},{4,5},{5,4},{6,7},{7,6},{8,9},{9,8},{10,11... | collective-permute-start | bytes 18874376 | tf_op jit(solution)/shard_map/ppermute | solution.py:578
  5.8 27.6 %all-to-all-start.1 = ((bf16[8,128,384]{2,1,0:T(8,128)(2,1)}), bf16[8,128,384]{2,1,0:T(8,128)(2,1)S(1)}, u32[]{:S(2)}, u32[]{:S(2)}) async-start(bf16[8,128,384]{2,1,0:T(8,128)(2,1)} %maximum_select_fusion), calls=%async_computation.1 | async-start | bytes 1572864 | tf_op jit(solution)/shard_map/all_to_all | solution.py:584
  33.4 20.3 %copy-start.16 = (bf16[8,128,384]{2,1,0:T(8,128)(2,1)}, bf16[8,128,384]{2,1,0:T(8,128)(2,1)S(1)}, u32[]{:S(2)}) copy-start(bf16[8,128,384]{2,1,0:T(8,128)(2,1)S(1)} %all-to-all-done.1) | copy-start | bytes 2359300
  34.1 10.2 %all-to-all-start = ((s32[8,1,512]{2,1,0:T(1,128)}), s32[8,1,512]{2,1,0:T(1,128)S(1)}, u32[]{:S(2)}, u32[]{:S(2)}) async-start(s32[8,1,512]{2,1,0:T(1,128)} %broadcast_in_dim.19), calls=%async_computation | async-start | bytes 32768 | tf_op jit(solution)/shard_map/all_to_all | solution.py:584
  37.7 20.1 %collective-permute-start.1 = (bf16[1024,384]{1,0:T(8,128)(2,1)S(1)}, bf16[1024,384]{1,0:T(8,128)(2,1)}, u32[]{:S(2)}, u32[]{:S(2)}) collective-permute-start(bf16[1024,384]{1,0:T(8,128)(2,1)S(1)} %bitcast.27), channel_id=1, source_target_pairs={{0,1},{1,0},{2,3},{3,2},{4,5},{5,4},{6,7},{7,6},{8,9},{9,8},{10,11... | collective-permute-start | bytes 2359304 | tf_op jit(solution)/shard_map/ppermute | solution.py:578
  53.7 4.0 %copy-start = (bf16[2560,2048]{1,0:T(8,128)(2,1)}, bf16[2560,2048]{1,0:T(8,128)(2,1)S(1)}, u32[]{:S(2)}) copy-start(bf16[2560,2048]{1,0:T(8,128)(2,1)S(1)} %context_rows.1.refs_1_) | copy-start | bytes 31457284
  67.3 2.9 %collective-permute-start.2 = (bf16[2048,256]{1,0:T(8,128)(2,1)}, bf16[2048,256]{1,0:T(8,128)(2,1)S(1)}, u32[]{:S(2)}, u32[]{:S(2)}) collective-permute-start(bf16[2048,256]{1,0:T(8,128)(2,1)} %get-tuple-element.22), channel_id=1, source_target_pairs={{0,1},{1,0},{2,3},{3,2},{4,5},{5,4},{6,7},{7,6},{8,9},{9,8},{10,11... | collective-permute-start | bytes 3145736 | tf_op jit(solution)/shard_map/ppermute | solution.py:578
  70.2 1.2 copy-start.12
  71.5 0.9 copy-start.13
  72.4 15.6 %copy-start.4 = (bf16[512,2048]{1,0:T(8,128)(2,1)S(1)}, bf16[512,2048]{1,0:T(8,128)(2,1)}, u32[]{:S(2)}) copy-start(bf16[512,2048]{1,0:T(8,128)(2,1)} %mine_ref.2) | copy-start | bytes 6291460
  72.4 15.6 %copy-start.11 = (s32[4]{0:T(128)S(1)}, s32[4]{0:T(128)}, u32[]{:S(2)}) copy-start(s32[4]{0:T(128)} %copy-done.10) | copy-start | bytes 52
  77.0 11.0 %all-to-all-start.2 = ((bf16[8,64,128]{2,1,0:T(8,128)(2,1)}), bf16[8,64,128]{2,1,0:T(8,128)(2,1)S(1)}, u32[]{:S(2)}, u32[]{:S(2)}) async-start(bf16[8,64,128]{2,1,0:T(8,128)(2,1)} %bitcast.14), calls=%async_computation.2 | async-start | bytes 262144 | tf_op jit(solution)/shard_map/all_to_all | solution.py:584
  80.5 67.3 %collective-permute-start.8 = (bf16[512,2048]{1,0:T(8,128)(2,1)}, bf16[512,2048]{1,0:T(8,128)(2,1)}, u32[]{:S(2)}, u32[]{:S(2)}) collective-permute-start(bf16[512,2048]{1,0:T(8,128)(2,1)} %mine_ref.3), channel_id=1, source_target_pairs={{0,1},{1,0},{2,3},{3,2},{4,5},{5,4},{6,7},{7,6},{8,9},{9,8},{10,11... | collective-permute-start | bytes 6291464 | tf_op jit(solution)/shard_map/ppermute | solution.py:578
  83.0 32.5 %collective-permute-start.13 = (bf16[512,1024]{1,0:T(8,128)(2,1)}, bf16[512,1024]{1,0:T(8,128)(2,1)S(1)}, u32[]{:S(2)}, u32[]{:S(2)}) collective-permute-start(bf16[512,1024]{1,0:T(8,128)(2,1)} %constant_dynamic-slice_fusion.1), channel_id=1, source_target_pairs={{0,4},{4,0},{8,12},{12,8},{16,20},{20,16},{24,28},{28,24},{1,5},{5... | collective-permute-start | bytes 3145736 | tf_op jit(solution)/shard_map/ppermute | solution.py:587
  90.4 5.0 %collective-permute-start.4 = (bf16[32,2048]{1,0:T(8,128)(2,1)S(1)}, bf16[32,2048]{1,0:T(8,128)(2,1)S(1)}, u32[]{:S(2)}, u32[]{:S(2)}) collective-permute-start(bf16[32,2048]{1,0:T(8,128)(2,1)S(1)} %get-tuple-element.24), channel_id=1, source_target_pairs={{0,2},{1,3},{2,0},{3,1},{4,6},{5,7},{6,4},{7,5},{8,10},{9,11},{10,... | collective-permute-start | bytes 393224 | tf_op jit(solution)/shard_map/ppermute | solution.py:581
  94.3 40.9 %collective-permute-start.17 = (bf16[256,2048]{1,0:T(8,128)(2,1)}, bf16[256,2048]{1,0:T(8,128)(2,1)}, u32[]{:S(2)}, u32[]{:S(2)}) collective-permute-start(bf16[256,2048]{1,0:T(8,128)(2,1)} %constant_dynamic-slice_fusion), channel_id=1, source_target_pairs={{0,4},{4,0},{8,12},{12,8},{16,20},{20,16},{24,28},{28,24},{1,5},{5... | collective-permute-start | bytes 3145736 | tf_op jit(solution)/shard_map/ppermute | solution.py:587
  95.5 7.2 %copy-start.15 = (bf16[32,2048]{1,0:T(8,128)(2,1)}, bf16[32,2048]{1,0:T(8,128)(2,1)S(1)}, u32[]{:S(2)}) copy-start(bf16[32,2048]{1,0:T(8,128)(2,1)S(1)} %collective-permute-done.4) | copy-start | bytes 393220
  97.6 5.0 %collective-permute-start.5 = (bf16[32,2048]{1,0:T(8,128)(2,1)S(1)}, bf16[32,2048]{1,0:T(8,128)(2,1)S(1)}, u32[]{:S(2)}, u32[]{:S(2)}) collective-permute-start(bf16[32,2048]{1,0:T(8,128)(2,1)S(1)} %multiply_convert_fusion.1), channel_id=1, source_target_pairs={{0,2},{1,3},{2,0},{3,1},{4,6},{5,7},{6,4},{7,5},{8,10},{9,11},{10,... | collective-permute-start | bytes 393224 | tf_op jit(solution)/shard_map/ppermute | solution.py:581
  102.7 2.8 %copy-start.3 = (bf16[3,2048,512]{2,1,0:T(8,128)(2,1)S(1)}, bf16[3,2048,512]{2,1,0:T(8,128)(2,1)}, u32[]{:S(2)}) copy-start(bf16[3,2048,512]{2,1,0:T(8,128)(2,1)} %refs_2_.1) | copy-start | bytes 18874372
  111.3 43.9 %copy-start.5 = (bf16[512,2048]{1,0:T(8,128)(2,1)S(1)}, bf16[512,2048]{1,0:T(8,128)(2,1)}, u32[]{:S(2)}) copy-start(bf16[512,2048]{1,0:T(8,128)(2,1)} %mine_ref.3) | copy-start | bytes 6291460
  111.3 25.5 %all-to-all-start.3 = ((bf16[8,64,384]{2,1,0:T(8,128)(2,1)}), bf16[8,64,384]{2,1,0:T(8,128)(2,1)}, u32[]{:S(2)}, u32[]{:S(2)}) async-start(bf16[8,64,384]{2,1,0:T(8,128)(2,1)} %triple_heads.1), calls=%async_computation.3 | async-start | bytes 786432 | tf_op jit(solution)/shard_map/all_to_all | solution.py:584
  115.5 43.4 %collective-permute-start.14 = (bf16[512,1024]{1,0:T(8,128)(2,1)S(1)}, bf16[512,1024]{1,0:T(8,128)(2,1)}, u32[]{:S(2)}, u32[]{:S(2)}) collective-permute-start(bf16[512,1024]{1,0:T(8,128)(2,1)S(1)} %collective-permute-done.13.refs_6_), channel_id=1, source_target_pairs={{0,2},{1,3},{2,0},{3,1},{4,6},{5,7},{6,4},{7,5},{8,10},{9,11},{10,... | collective-permute-start | bytes 3145736 | tf_op jit(solution)/shard_map/ppermute | solution.py:581
  135.3 26.0 %collective-permute-start.18 = (bf16[256,2048]{1,0:T(8,128)(2,1)}, bf16[256,2048]{1,0:T(8,128)(2,1)}, u32[]{:S(2)}, u32[]{:S(2)}) collective-permute-start(bf16[256,2048]{1,0:T(8,128)(2,1)} %collective-permute-done.17.refs_10_), channel_id=1, source_target_pairs={{0,2},{1,3},{2,0},{3,1},{4,6},{5,7},{6,4},{7,5},{8,10},{9,11},{10,... | collective-permute-start | bytes 3145736 | tf_op jit(solution)/shard_map/ppermute | solution.py:581
  136.8 2.1 %collective-permute-start.7 = (bf16[8,2,32,384]{3,2,1,0:T(8,128)(2,1)}, bf16[8,2,32,384]{3,2,1,0:T(8,128)(2,1)}, u32[]{:S(2)}, u32[]{:S(2)}) collective-permute-start(bf16[8,2,32,384]{3,2,1,0:T(8,128)(2,1)} %bitcast.17.refs_1_.refs_2_), channel_id=1, source_target_pairs={{0,1},{1,0},{2,3},{3,2},{4,5},{5,4},{6,7},{7,6},{8,9},{9,8},{10,11... | collective-permute-start | bytes 1179656 | tf_op jit(solution)/shard_map/ppermute | solution.py:578
  141.9 0.7 copy-start.9
  142.6 12.6 %all-to-all-start.4 = ((bf16[8,64,128]{2,1,0:T(8,128)(2,1)}), bf16[8,64,128]{2,1,0:T(8,128)(2,1)S(1)}, u32[]{:S(2)}, u32[]{:S(2)}) async-start(bf16[8,64,128]{2,1,0:T(8,128)(2,1)} %bitcast.24), calls=%async_computation.4 | async-start | bytes 262144 | tf_op jit(solution)/shard_map/all_to_all | solution.py:584
  155.2 7.8 %copy-start.14 = (bf16[32,2048]{1,0:T(8,128)(2,1)S(1)}, bf16[32,2048]{1,0:T(8,128)(2,1)}, u32[]{:S(2)}) copy-start(bf16[32,2048]{1,0:T(8,128)(2,1)} %get-tuple-element.20) | copy-start | bytes 393220
  155.2 22.8 %copy-start.1 = (bf16[2048,1024]{1,0:T(8,128)(2,1)S(1)}, bf16[2048,1024]{1,0:T(8,128)(2,1)}, u32[]{:S(2)}) copy-start(bf16[2048,1024]{1,0:T(8,128)(2,1)} %refs_4_.1) | copy-start | bytes 12582916
  157.8 5.2 %collective-permute-start.9 = (bf16[32,2048]{1,0:T(8,128)(2,1)S(1)}, bf16[32,2048]{1,0:T(8,128)(2,1)S(1)}, u32[]{:S(2)}, u32[]{:S(2)}) collective-permute-start(bf16[32,2048]{1,0:T(8,128)(2,1)S(1)} %get-tuple-element.26), channel_id=1, source_target_pairs={{0,2},{1,3},{2,0},{3,1},{4,6},{5,7},{6,4},{7,5},{8,10},{9,11},{10,... | collective-permute-start | bytes 393224 | tf_op jit(solution)/shard_map/ppermute | solution.py:581
  158.5 7.4 %collective-permute-start.15 = (bf16[512,1024]{1,0:T(8,128)(2,1)S(1)}, bf16[512,1024]{1,0:T(8,128)(2,1)S(1)}, u32[]{:S(2)}, u32[]{:S(2)}) collective-permute-start(bf16[512,1024]{1,0:T(8,128)(2,1)S(1)} %collective-permute-done.13.refs_6_), channel_id=1, source_target_pairs={{0,1},{1,0},{2,3},{3,2},{4,5},{5,4},{6,7},{7,6},{8,9},{9,8},{10,11... | collective-permute-start | bytes 3145736 | tf_op jit(solution)/shard_map/ppermute | solution.py:578
  158.5 9.8 %collective-permute-start.19 = (bf16[256,2048]{1,0:T(8,128)(2,1)}, bf16[256,2048]{1,0:T(8,128)(2,1)S(1)}, u32[]{:S(2)}, u32[]{:S(2)}) collective-permute-start(bf16[256,2048]{1,0:T(8,128)(2,1)} %collective-permute-done.17.refs_10_), channel_id=1, source_target_pairs={{0,1},{1,0},{2,3},{3,2},{4,5},{5,4},{6,7},{7,6},{8,9},{9,8},{10,11... | collective-permute-start | bytes 3145736 | tf_op jit(solution)/shard_map/ppermute | solution.py:578
  159.0 9.7 %collective-permute-start.16 = (bf16[512,1024]{1,0:T(8,128)(2,1)}, bf16[512,1024]{1,0:T(8,128)(2,1)S(1)}, u32[]{:S(2)}, u32[]{:S(2)}) collective-permute-start(bf16[512,1024]{1,0:T(8,128)(2,1)} %collective-permute-done.14.refs_7_), channel_id=1, source_target_pairs={{0,1},{1,0},{2,3},{3,2},{4,5},{5,4},{6,7},{7,6},{8,9},{9,8},{10,11... | collective-permute-start | bytes 3145736 | tf_op jit(solution)/shard_map/ppermute | solution.py:578
  161.3 7.4 %collective-permute-start.20 = (bf16[256,2048]{1,0:T(8,128)(2,1)}, bf16[256,2048]{1,0:T(8,128)(2,1)S(1)}, u32[]{:S(2)}, u32[]{:S(2)}) collective-permute-start(bf16[256,2048]{1,0:T(8,128)(2,1)} %collective-permute-done.18.refs_11_), channel_id=1, source_target_pairs={{0,1},{1,0},{2,3},{3,2},{4,5},{5,4},{6,7},{7,6},{8,9},{9,8},{10,11... | collective-permute-start | bytes 3145736 | tf_op jit(solution)/shard_map/ppermute | solution.py:578
  164.2 6.6 %collective-permute-start.10 = (bf16[32,2048]{1,0:T(8,128)(2,1)S(1)}, bf16[32,2048]{1,0:T(8,128)(2,1)S(1)}, u32[]{:S(2)}, u32[]{:S(2)}) collective-permute-start(bf16[32,2048]{1,0:T(8,128)(2,1)S(1)} %multiply_convert_fusion.refs_0_), channel_id=1, source_target_pairs={{0,8},{4,12},{8,0},{12,4},{16,24},{20,28},{24,16},{28,20},{1,9},{5... | collective-permute-start | bytes 393224 | tf_op jit(solution)/shard_map/ppermute | solution.py:587
  165.8 12.1 %collective-permute-start.11 = (bf16[32,2048]{1,0:T(8,128)(2,1)S(1)}, bf16[32,2048]{1,0:T(8,128)(2,1)S(1)}, u32[]{:S(2)}, u32[]{:S(2)}) collective-permute-start(bf16[32,2048]{1,0:T(8,128)(2,1)S(1)} %multiply_convert_fusion.refs_0_), channel_id=1, source_target_pairs={{0,16},{4,20},{8,24},{12,28},{16,0},{20,4},{24,8},{28,12},{1,17},{... | collective-permute-start | bytes 393224 | tf_op jit(solution)/shard_map/ppermute | solution.py:587
  168.2 9.7 %collective-permute-start.12 = (bf16[32,2048]{1,0:T(8,128)(2,1)S(1)}, bf16[32,2048]{1,0:T(8,128)(2,1)S(1)}, u32[]{:S(2)}, u32[]{:S(2)}) collective-permute-start(bf16[32,2048]{1,0:T(8,128)(2,1)S(1)} %multiply_convert_fusion.refs_0_), channel_id=1, source_target_pairs={{0,24},{4,28},{8,16},{12,20},{16,8},{20,12},{24,0},{28,4},{1,25},{... | collective-permute-start | bytes 393224 | tf_op jit(solution)/shard_map/ppermute | solution.py:587
  178.0 2.2 %copy-start.2 = (bf16[1024,2048]{1,0:T(8,128)(2,1)S(1)}, bf16[1024,2048]{1,0:T(8,128)(2,1)}, u32[]{:S(2)}) copy-start(bf16[1024,2048]{1,0:T(8,128)(2,1)} %refs_5_.1) | copy-start | bytes 12582916
  184.8 8.2 %collective-permute-start.23 = (bf16[32,2048]{1,0:T(8,128)(2,1)S(1)}, bf16[32,2048]{1,0:T(8,128)(2,1)S(1)}, u32[]{:S(2)}, u32[]{:S(2)}) collective-permute-start(bf16[32,2048]{1,0:T(8,128)(2,1)S(1)} %get-tuple-element.30), channel_id=1, source_target_pairs={{0,24},{4,28},{8,16},{12,20},{16,8},{20,12},{24,0},{28,4},{1,25},{... | collective-permute-start | bytes 393224 | tf_op jit(solution)/shard_map/ppermute | solution.py:587
  187.2 10.2 %collective-permute-start.22 = (bf16[32,2048]{1,0:T(8,128)(2,1)S(1)}, bf16[32,2048]{1,0:T(8,128)(2,1)S(1)}, u32[]{:S(2)}, u32[]{:S(2)}) collective-permute-start(bf16[32,2048]{1,0:T(8,128)(2,1)S(1)} %get-tuple-element.29), channel_id=1, source_target_pairs={{0,16},{4,20},{8,24},{12,28},{16,0},{20,4},{24,8},{28,12},{1,17},{... | collective-permute-start | bytes 393224 | tf_op jit(solution)/shard_map/ppermute | solution.py:587
  188.3 9.1 %collective-permute-start.21 = (bf16[32,2048]{1,0:T(8,128)(2,1)S(1)}, bf16[32,2048]{1,0:T(8,128)(2,1)S(1)}, u32[]{:S(2)}, u32[]{:S(2)}) collective-permute-start(bf16[32,2048]{1,0:T(8,128)(2,1)S(1)} %get-tuple-element.28), channel_id=1, source_target_pairs={{0,8},{4,12},{8,0},{12,4},{16,24},{20,28},{24,16},{28,20},{1,9},{5... | collective-permute-start | bytes 393224 | tf_op jit(solution)/shard_map/ppermute | solution.py:587

commit v3 on v2

--- a/solution.py
+++ b/solution.py
@@ -225,10 +225,9 @@
     return coarse, fine
 
 
-def context_rows(ids, starts, table, owners):
+def context_rows(ids, coarse, fine, table, owners):
     count, rows = ids.shape[0], FINE * FINE
     width = table.shape[1]
-    coarse, fine = sinusoid_tables(starts, width)
     return pl.pallas_call(
         lambda *refs: context_kernel(owners, *refs),
         grid=(count,),
@@ -251,13 +250,14 @@
     )(ids[:, None, :], coarse, fine, table)
 
 
-def attention_kernel(key_tile, places_ref, query_ref, own_ref, other_ref, out_ref):
-    tile = pl.program_id(0)
+def attention_kernel(key_tile, shifted, scalars_ref, query_ref, own_ref, other_ref, out_ref):
+    tile, core = pl.program_id(0), scalars_ref[0]
+    offset = scalars_ref[4] if shifted else 0
     parts, rows, size = query_ref.shape
     query = query_ref[...].reshape(parts * rows, size)
     rows = parts * rows
     query_place = (
-        places_ref[0] + tile * places_ref[1] + lax.broadcasted_iota(jnp.int32, (rows, 1), 0)
+        offset + (2 * tile + core) * rows + lax.broadcasted_iota(jnp.int32, (rows, 1), 0)
     )
     peak = jnp.full((rows, 1), MASKED, jnp.float32)
     output = jnp.zeros((rows, 2 * size), jnp.float32)
@@ -273,8 +273,7 @@
                     query, key, (((1,), (1,)), ((), ())), preferred_element_type=jnp.float32
                 )
                 key_place = (
-                    places_ref[2 + 2 * side]
-                    + block * places_ref[3 + 2 * side]
+                    (2 * block + (1 - core if side else core)) * keys
                     + part * key_tile
                     + lax.broadcasted_iota(jnp.int32, (1, key_tile), 1)
                 )
@@ -291,11 +290,11 @@
     out_ref[...] = final.reshape(out_ref.shape)
 
 
-def head_attention(triples, own, other, places, key_tile):
+def head_attention(scalars, triples, own, other, shifted, key_tile):
     owners, tiles, rows = triples.shape[:3]
     keys = 2 * own.shape[0] * own.shape[1] * own.shape[2]
     return pl.pallas_call(
-        lambda *refs: attention_kernel(key_tile, *refs),
+        lambda *refs: attention_kernel(key_tile, shifted, *refs),
         grid_spec=pltpu.PrefetchScalarGridSpec(
             num_scalar_prefetch=1,
             grid=(tiles,),
@@ -314,7 +313,7 @@
         ),
         compiler_params=pltpu.CompilerParams(vmem_limit_bytes=14 * MIB),
         name="head_attention",
-    )(places, triples, own, other)
+    )(scalars, triples, own, other)
 
 
 def prepare_kernel(core_ref, query_ref, pair_ref, mine_ref, theirs_ref):
@@ -380,83 +379,107 @@
     )(scalars, heads, mine, theirs)
 
 
-def triple_kernel(scale, scalars_ref, rows_ref, mine_ref, theirs_ref, out_ref):
-    core = scalars_ref[0]
+def triple_kernel(scale, scalars_ref, own_ref, other_ref, mine_hbm, theirs_hbm, out_ref, matrices, loaded):
+    core, duo = scalars_ref[0], scalars_ref[1]
     heads = out_ref.shape[0] // 2
-    for side, matrix in ((core, mine_ref), (1 - core, theirs_ref)):
-        for kind in range(mine_ref.shape[0]):
-            product = jnp.dot(rows_ref[...], matrix[kind], preferred_element_type=jnp.float32)
-            product = (product * (scale if kind == 0 else 1.0)).astype(jnp.bfloat16)
-            for head in range(heads):
-                out_ref[side * heads + head, :, kind * HD : (kind + 1) * HD] = product[
-                    :, head * HD : (head + 1) * HD
-                ]
-
-
-def triple_heads(scalars, rows, mine, theirs):
-    count, _ = rows.shape
+    kinds = mine_hbm.shape[0]
+    loads = [
+        pltpu.make_async_copy(source.at[kind], matrices.at[base + kind], loaded.at[base + kind])
+        for base, source in ((0, mine_hbm), (kinds, theirs_hbm))
+        for kind in range(kinds)
+    ]
+    ahead = 3
+    for load in loads[:ahead]:
+        load.start()
+    own, other = own_ref[...], other_ref[...]
+    rows = jnp.concatenate([jnp.where(duo == 0, own, other), jnp.where(duo == 0, other, own)])
+    for index, load in enumerate(loads):
+        load.wait()
+        for later in loads[index + ahead : index + ahead + 1]:
+            later.start()
+        kind = index % kinds
+        side = core if index < kinds else 1 - core
+        product = jnp.dot(rows, matrices[index], preferred_element_type=jnp.float32)
+        product = (product * (scale if kind == 0 else 1.0)).astype(jnp.bfloat16)
+        for head in range(heads):
+            out_ref[side * heads + head, :, kind * HD : (kind + 1) * HD] = product[
+                :, head * HD : (head + 1) * HD
+            ]
+
+
+def triple_heads(scalars, own, other, mine, theirs):
+    count, _ = own.shape
     kinds, inner, columns = mine.shape
     heads = columns // HD
     return pl.pallas_call(
         lambda *refs: triple_kernel(HD**-0.5, *refs),
-        in_specs=[IN_SMEM, IN_VMEM, IN_VMEM, IN_VMEM],
+        in_specs=[IN_SMEM, IN_VMEM, IN_VMEM, ANYWHERE, ANYWHERE],
         out_specs=IN_VMEM,
-        out_shape=jax.ShapeDtypeStruct((2 * heads, count, kinds * HD), jnp.bfloat16),
+        out_shape=jax.ShapeDtypeStruct((2 * heads, 2 * count, kinds * HD), jnp.bfloat16),
+        scratch_shapes=[
+            pltpu.VMEM((2 * kinds, inner, columns), jnp.bfloat16),
+            pltpu.SemaphoreType.DMA((2 * kinds,)),
+        ],
         cost_estimate=pl.CostEstimate(
-            flops=4 * kinds * count * inner * columns,
+            flops=8 * kinds * count * inner * columns,
             bytes_accessed=4 * kinds * inner * columns,
             transcendentals=0,
         ),
-        compiler_params=pltpu.CompilerParams(vmem_limit_bytes=16 * MIB),
+        compiler_params=pltpu.CompilerParams(vmem_limit_bytes=BIG),
         name="triple_heads",
-    )(scalars, rows, mine, theirs)
+    )(scalars, own, other, mine, theirs)
+
+
+def add_norm_kernel(base_ref, kept_ref, came_ref, stream_ref, normed_ref):
+    total = base_ref[...].astype(jnp.float32) + (
+        kept_ref[...] + came_ref[...].astype(jnp.float32)
+    )
+    stream_ref[...] = total
+    normed_ref[...] = rms_normalize(total).astype(jnp.bfloat16)
+
+
+def add_norm(base, kept, came):
+    return pl.pallas_call(
+        add_norm_kernel,
+        in_specs=[IN_VMEM] * 3,
+        out_specs=[IN_VMEM] * 2,
+        out_shape=[
+            jax.ShapeDtypeStruct(kept.shape, jnp.float32),
+            jax.ShapeDtypeStruct(kept.shape, jnp.bfloat16),
+        ],
+        compiler_params=pltpu.CompilerParams(vmem_limit_bytes=4 * MIB),
+        name="add_norm",
+    )(base, kept, came)
 
 
 def context_heads_kernel(
-    scale, scalars_ref, context_hbm, mine_hbm, theirs_hbm, pair_ref, query_ref, latent_ref,
-    context_ref, mine_ref, theirs_ref, loaded,
+    scale, scalars_ref, context_ref, rows_ref, mine_ref, theirs_ref, pair_ref, query_ref,
+    latent_ref, weights_ref,
 ):
     core, duo, place = scalars_ref[0], scalars_ref[1], scalars_ref[2]
-    inner = mine_ref.shape[0]
-    size = mine_ref.shape[1] // 3
+    _, part, columns = mine_ref.shape
+    owners, tiles, rows, size = query_ref.shape
+    inner = owners * part
     keys = pair_ref.shape[0]
-    owners, _, rows, _ = query_ref.shape
     tile = owners * rows
-    count = context_ref.shape[0] // tile
-    own = pl.ds(pl.multiple_of(core * inner, inner), inner)
-    other = pl.ds(pl.multiple_of((1 - core) * inner, inner), inner)
-    loads = [
-        pltpu.make_async_copy(mine_hbm, mine_ref, loaded.at[count]),
-        pltpu.make_async_copy(theirs_hbm, theirs_ref, loaded.at[count + 1]),
-    ] + [
-        pltpu.make_async_copy(
-            context_hbm.at[pl.ds(i * tile, tile)], context_ref.at[pl.ds(i * tile, tile)], loaded.at[i]
+    for side, ref in ((core, mine_ref), (1 - core, theirs_ref)):
+        span = pl.ds(pl.multiple_of(side * inner, inner), inner)
+        weights_ref[span, :] = ref[...].reshape(inner, columns)
+
+    def product(left, columns):
+        return jnp.dot(left, weights_ref[:, columns], preferred_element_type=jnp.float32)
+
+    for start in range(0, keys, tile):
+        span = slice(start, start + tile)
+        pair_ref[span, :] = product(context_ref[span, :], slice(size, 3 * size)).astype(
+            jnp.bfloat16
         )
-        for i in range(count)
-    ]
-    for load in loads:
-        load.start()
-    loads[0].wait()
-    loads[1].wait()
-
-    def product(span, columns):
-        return jnp.dot(
-            context_ref[span, own], mine_ref[:, columns], preferred_element_type=jnp.float32
-        ) + jnp.dot(
-            context_ref[span, other], theirs_ref[:, columns], preferred_element_type=jnp.float32
-        )
-
-    for index in range(count):
-        loads[2 + index].wait()
-        span = slice(index * tile, (index + 1) * tile)
-        if index * tile < keys:
-            pair_ref[span, :] = product(span, slice(size, 3 * size)).astype(jnp.bfloat16)
-        else:
-            query = (product(span, slice(0, size)) * scale).astype(jnp.bfloat16)
-            query_ref[:, index - keys // tile] = query.reshape(owners, rows, size)
-    start = pl.multiple_of(keys + duo * tile + place * rows, rows)
-    latent = context_ref[pl.ds(start, rows), :]
-    part = inner // owners
+    for index in range(tiles):
+        left = rows_ref[index * tile : (index + 1) * tile, :]
+        query = (product(left, slice(0, size)) * scale).astype(jnp.bfloat16)
+        query_ref[:, index] = query.reshape(owners, rows, size)
+    start = pl.multiple_of(duo * tile + place * rows, rows)
+    latent = rows_ref[pl.ds(start, rows), :]
     for half in range(2):
         for owner in range(owners):
             source = half * inner + owner * part
@@ -464,34 +487,74 @@
             latent_ref[:, target : target + part] = latent[:, source : source + part]
 
 
-def context_heads(scalars, context, mine, theirs, shape):
+def context_heads(scalars, context, latent, mine, theirs, shape):
     owners, tiles, rows = shape
-    count, width = context.shape
-    tile = owners * rows
-    keys = count - tiles * tile
-    inner, columns = mine.shape
-    size = columns // 3
+    keys, width = context.shape
+    size = mine.shape[2] // 3
     return pl.pallas_call(
         lambda *refs: context_heads_kernel(size**-0.5, *refs),
-        in_specs=[IN_SMEM] + [ANYWHERE] * 3,
+        in_specs=[IN_SMEM] + [IN_VMEM] * 4,
         out_specs=[IN_VMEM] * 3,
         out_shape=[
             jax.ShapeDtypeStruct((keys, 2 * size), jnp.bfloat16),
             jax.ShapeDtypeStruct((owners, tiles, rows, size), jnp.bfloat16),
             jax.ShapeDtypeStruct((rows, width), jnp.bfloat16),
         ],
-        scratch_shapes=[
-            pltpu.VMEM(context.shape, jnp.bfloat16),
-            pltpu.VMEM(mine.shape, jnp.bfloat16),
-            pltpu.VMEM(mine.shape, jnp.bfloat16),
-            pltpu.SemaphoreType.DMA((count // tile + 2,)),
-        ],
+        scratch_shapes=[pltpu.VMEM((width, 3 * size), jnp.bfloat16)],
         cost_estimate=pl.CostEstimate(
-            flops=4 * count * inner * columns, bytes_accessed=context.size * 2, transcendentals=0
+            flops=4 * (keys + owners * tiles * rows) * width * size,
+            bytes_accessed=keys * width * 2,
+            transcendentals=0,
         ),
-        compiler_params=pltpu.CompilerParams(vmem_limit_bytes=BIG),
+        compiler_params=pltpu.CompilerParams(vmem_limit_bytes=12 * MIB),
         name="context_heads",
-    )(scalars, context, mine, theirs)
+    )(scalars, context, latent, mine, theirs)
+
+
+def order_kernel(scalars_ref, mine_ref, theirs_ref, *block_refs):
+    core, place = scalars_ref[0], scalars_ref[2]
+    heads = mine_ref.shape[0]
+    for distance, block_ref in enumerate(block_refs):
+        head = place ^ distance
+        local = lax.rem(head, heads)
+        own = lax.div(head, heads) == core
+
+        @pl.when(own)
+        def _():
+            block_ref[...] = mine_ref[local]
+
+        @pl.when(jnp.logical_not(own))
+        def _():
+            block_ref[...] = theirs_ref[local]
+
+
+def order_blocks(scalars, mine, theirs):
+    heads, rows, columns = mine.shape
+    return pl.pallas_call(
+        order_kernel,
+        in_specs=[IN_SMEM, IN_VMEM, IN_VMEM],
+        out_specs=[IN_VMEM] * (2 * heads),
+        out_shape=[jax.ShapeDtypeStruct((rows, columns), jnp.bfloat16)] * (2 * heads),
+        compiler_params=pltpu.CompilerParams(vmem_limit_bytes=4 * MIB),
+        name="order_blocks",
+    )(scalars, mine, theirs)
+
+
+def gather_kernel(scalars_ref, *refs):
+    *block_refs, out_ref = refs
+    for distance, block_ref in enumerate(block_refs):
+        out_ref[scalars_ref[2] ^ distance] = block_ref[...]
+
+
+def gather_blocks(scalars, blocks):
+    return pl.pallas_call(
+        gather_kernel,
+        in_specs=[IN_SMEM] + [IN_VMEM] * len(blocks),
+        out_specs=IN_VMEM,
+        out_shape=jax.ShapeDtypeStruct((len(blocks), *blocks[0].shape), blocks[0].dtype),
+        compiler_params=pltpu.CompilerParams(vmem_limit_bytes=4 * MIB),
+        name="gather_blocks",
+    )(scalars, *blocks)
 
 
 def mlp_kernel(scalars_ref, *refs):
@@ -564,15 +627,14 @@
     core = group % 2
     duo = group // 2
     duos = groups // 2
-    first = core == 0
     offset = latent_offset[0]
     block = token_ids.shape[0]
+    width = embed_table.shape[1]
     share = cross_q.shape[0]
     group_rows = LATENTS // groups
     rows = group_rows // owners
     duo_rows = duos * rows
-    half = share // 2
-    scalars = jnp.stack([core, duo, place, group]).astype(jnp.int32)
+    scalars = jnp.stack([core, duo, place, group, offset]).astype(jnp.int32)
 
     def swap(value):
         return lax.ppermute(value, "lat", [(i, i ^ 1) for i in range(groups)])
@@ -590,16 +652,14 @@
         size = matrix.shape[0] // groups
         return lax.dynamic_slice_in_dim(matrix, group * size, size, 0)
 
-    def ordered(mine, theirs):
-        return jnp.where(
-            first, jnp.concatenate([mine, theirs]), jnp.concatenate([theirs, mine])
-        )
-
     mine, theirs = prepare_weights(scalars, cross_q, cross_kv)
-    sent = ordered(mine, swap(theirs))
-
-    every_token = exchange(jnp.broadcast_to(token_ids[None], (owners, block)))
-    arrived = exchange(sent).reshape(owners * half, 3 * HD)
+    blocks = order_blocks(scalars, mine, swap(theirs))
+
+    lanes = token_ids.reshape(1, block // HD, HD)
+    every_token = exchange(jnp.broadcast_to(lanes, (owners, block // HD, HD)))
+    arrived = [blocks[0]]
+    for distance in range(1, owners):
+        arrived.append(across(blocks[distance], distance))
 
     step = FINE * FINE
     latent_starts = (2 * jnp.arange(duos, dtype=jnp.int32) + core) * group_rows
@@ -633,60 +693,38 @@
             (offset + latent_starts[:, None] + latent_inner[None, :]).reshape(-1),
         ]
     )
-    ids = jnp.concatenate([own_ids.reshape(-1, step), latent_ids.reshape(-1, step)])
-    context = context_rows(ids, starts, embed_table, owners)
+    coarse, fine = sinusoid_tables(starts, width)
+    tiles = half_blocks * pieces
+    context = context_rows(own_ids.reshape(-1, step), coarse[:tiles], fine, embed_table, owners)
+    latent = context_rows(latent_ids.reshape(-1, step), coarse[tiles:], fine, embed_table, owners)
+    arrived = gather_blocks(scalars, arrived)
+    arrived_other = swap(arrived)
     pairs, queries, own_latent = context_heads(
-        scalars, context, arrived, swap(arrived), (owners, duos, rows)
+        scalars, context, latent, arrived, arrived_other, (owners, duos, rows)
     )
     other_pairs = swap(pairs)
     by_block = (1, half_blocks, block, 2 * HD)
-    places = jnp.stack(
-        [
-            offset + core * group_rows,
-            2 * group_rows,
-            core * block,
-            2 * block,
-            (1 - core) * block,
-            2 * block,
-        ]
-    ).astype(jnp.int32)
     attended = head_attention(
-        queries, pairs.reshape(by_block), other_pairs.reshape(by_block), places, block
-    )
-
-    def project(attended, mine, theirs):
+        scalars, queries, pairs.reshape(by_block), other_pairs.reshape(by_block), True, block
+    )
+
+    def project(base, attended, mine, theirs):
         heads = exchange(attended.reshape(owners, duo_rows, HD))
         kept, given = project_rows(scalars, heads, mine, theirs)
-        return kept + cross(given).astype(jnp.float32)
-
-    projected = project(attended, cross_out, swap(cross_out))
-    first_stream = own_latent.astype(jnp.float32) + projected
-
-    normed = rms_normalize(first_stream).astype(jnp.bfloat16)
+        return add_norm(base, kept, cross(given))
+
+    first_stream, normed = project(own_latent, attended, cross_out, swap(cross_out))
     normed_other = cross(normed)
-    normed = jnp.where(
-        duo == 0,
-        jnp.concatenate([normed, normed_other]),
-        jnp.concatenate([normed_other, normed]),
-    )
     self_qkv_other = swap(self_qkv)
-    triples = exchange(triple_heads(scalars, normed, self_qkv, self_qkv_other))
+    triples = exchange(triple_heads(scalars, normed, normed_other, self_qkv, self_qkv_other))
     triples = triples.reshape(owners, duos, rows, 3 * HD)
-    self_places = jnp.stack(
-        [
-            core * group_rows,
-            2 * group_rows,
-            core * group_rows,
-            2 * group_rows,
-            (1 - core) * group_rows,
-            2 * group_rows,
-        ]
-    ).astype(jnp.int32)
-    self_attended = head_attention(triples, triples, swap(triples), self_places, group_rows)
-    projected = project(self_attended, self_out, swap(self_out))
-    second_stream = first_stream + projected
-
-    mlp_normed = rms_normalize(second_stream).astype(jnp.bfloat16)
+    self_attended = head_attention(
+        scalars, triples, triples, swap(triples), False, group_rows
+    )
+    second_stream, mlp_normed = project(
+        first_stream, self_attended, self_out, swap(self_out)
+    )
+
     distances = [2 * i for i in range(1, owners // 2)]
     blocks = [mlp_normed] + [across(mlp_normed, distance) for distance in distances]
     kept, *given = mlp_shares(scalars, blocks, mlp_in, mlp_out, *fetched)

time: 199 us -> 219 us (1.10)
  waiting for transfers between devices: 82.7 us -> 101 us
  starting transfers between devices: 43.3 us -> 58.3 us
  local copies, waits for them, and re-layouts: 19.5 us -> 11.1 us
  other arithmetic: 9.13 us -> 4.62 us
    ppermute x5, waiting for transfers between devices: 8.38 us -> 30.4 us  [cross(): return lax.ppermute(value, 'lat', [(i, i ^ 2) for i in range(groups)])]
    all_to_all x5 -> x4, waiting for transfers between devices: 33.2 us -> 48.4 us  [exchange(): return lax.all_to_all(value, 'ctx', 0, 0, tiled=True)]
    ppermute x8 -> x15, starting transfers between devices: 10.7 us -> 25 us  [across(): lax.ppermute(value, 'ctx', [(i, i ^ distance) for i in range(owners)])]
    ppermute x8 -> x15, waiting for transfers between devices: 35.6 us -> 22.4 us  [across(): lax.ppermute(value, 'ctx', [(i, i ^ distance) for i in range(owners)])]
    unnamed x36 -> x24, local copies, waits for them, and re-layouts: 13.9 us -> 4.86 us
    pallas_call x1, Pallas kernels: 9.56 us -> 3.56 us  [context_heads(): pl.pallas_call(lambda *refs: context_heads_kernel(size ** (-0.5), *refs),...]
    ppermute x11, waiting for transfers between devices: 5.52 us -> 0.03 us  [swap(): return lax.ppermute(value, 'lat', [(i, i ^ 1) for i in range(groups)])]
    pallas_call x2 -> x6, Pallas kernels: 7.67 us -> 9.97 us  [the longest x2 8.37 us: head_attention(): pl.pallas_call(lambda *refs: attention_kernel(key_tile, shifted, *refs),...]
  transfers between devices with their start and end apart: 29 -> 35, of which waited for: 16 -> 12; matrix products, arithmetic and copies ran while one was open for 7% -> 5% of each run, Pallas kernels for 19% -> 17%
where the time goes in v3:
time: 219 us
  waiting for transfers between devices  101 us (46%)
  starting transfers between devices  58.3 us (27%)
  Pallas kernels  42.4 us (19%)
  local copies, waits for them, and re-layouts  11.1 us (5%)
  other arithmetic  4.62 us (2%)
    all_to_all x4, waiting for transfers between devices, exchange(): return lax.all_to_all(value, 'ctx', 0, 0, tiled=True)  48.4 us
    ppermute x5, waiting for transfers between devices, cross(): return lax.ppermute(value, 'lat', [(i, i ^ 2) for i in range(groups)])  30.4 us
    ppermute x15, starting transfers between devices, across(): lax.ppermute(value, 'ctx', [(i, i ^ distance) for i in range(owners)])  25 us
    all_to_all x4, starting transfers between devices, exchange(): return lax.all_to_all(value, 'ctx', 0, 0, tiled=True)  24.1 us
    ppermute x15, waiting for transfers between devices, across(): lax.ppermute(value, 'ctx', [(i, i ^ distance) for i in range(owners)])  22.4 us
    pallas_call x2, Pallas kernels, context_rows(): pl.pallas_call(lambda *refs: context_kernel(owners, *refs), grid=(count,)...  9.83 us
    pallas_call x2, Pallas kernels, head_attention(): pl.pallas_call(lambda *refs: attention_kernel(key_tile, shifted, *refs),...  8.37 us
    pallas_call x1, Pallas kernels, triple_heads(): pl.pallas_call(lambda *refs: triple_kernel(HD ** (-0.5), *refs), in_specs...  7.14 us
  transfers between devices with their start and end apart: 35, of which 12 were waited for; matrix products, arithmetic and copies ran while one was open for 5% of the time, Pallas kernels for 17%

profile of v3, /device:TPU:0, one launch (start us, length us, event | category | flops | bytes accessed | tf_op | source)
XLA Modules:
  0.0 218.5 jit_solution(13162678844963899180)
XLA Ops:
  0.0 0.5 collective-permute-start.13
  1.2 1.0 copy-done.4
  2.3 0.9 copy-done.7
  3.2 0.7 prepare_weights.1
  3.9 0.2 collective-permute-start
  4.1 1.3 broadcast_in_dim.37
  5.4 7.2 %all-to-all-start = ((s32[8,4,128]{2,1,0:T(4,128)}), s32[8,4,128]{2,1,0:T(4,128)S(1)}, u32[]{:S(2)}, u32[]{:S(2)}) async-start(s32[8,4,128]{2,1,0:T(4,128)} %broadcast_in_dim.37), calls=%async_computation | async-start | bytes 32768 | tf_op jit(solution)/shard_map/all_to_all | solution.py:646
  12.7 0.1 add.115
  12.9 0.9 multiply_cosine_fusion
  13.8 2.5 %broadcast_select_fusion = (f32[10,1,2048]{2,1,0:T(1,128)S(1)}, f32[10,1,2048]{2,1,0:T(1,128)S(1)}) fusion(pred[2048]{0:T(1024)(128)(4,1)S(1)} %fusion.4, f32[2048]{0:T(1024)S(1)} %fusion.8, f32[10]{0:T(128)S(1)} %add_convert_fusion.1), kind=kLoop, calls=%fused_computation.6 | loop fusion | flops 81920 | bytes 174120 | tf_op jit(solution)/shard_map/jit(_where)/select_n | solution.py:219
  16.4 0.7 order_blocks.1
  17.1 2.1 collective-permute-start.1
  19.2 1.5 collective-permute-start.2
  20.8 2.9 %collective-permute-start.4 = (bf16[128,384]{1,0:T(8,128)(2,1)S(1)}, bf16[128,384]{1,0:T(8,128)(2,1)S(1)}, u32[]{:S(2)}, u32[]{:S(2)}) collective-permute-start(bf16[128,384]{1,0:T(8,128)(2,1)S(1)} %get-tuple-element.36), channel_id=1, source_target_pairs={{0,16},{4,20},{8,24},{12,28},{16,0},{20,4},{24,8},{28,12},{1,17},{... | collective-permute-start | bytes 294920 | tf_op jit(solution)/shard_map/ppermute | solution.py:649
  23.7 2.6 %collective-permute-start.5 = (bf16[128,384]{1,0:T(8,128)(2,1)S(1)}, bf16[128,384]{1,0:T(8,128)(2,1)S(1)}, u32[]{:S(2)}, u32[]{:S(2)}) collective-permute-start(bf16[128,384]{1,0:T(8,128)(2,1)S(1)} %get-tuple-element.37), channel_id=1, source_target_pairs={{0,20},{4,16},{8,28},{12,24},{16,4},{20,0},{24,12},{28,8},{1,21},{... | collective-permute-start | bytes 294920 | tf_op jit(solution)/shard_map/ppermute | solution.py:649
  26.2 2.2 collective-permute-start.6
  28.4 2.8 %collective-permute-start.7 = (bf16[128,384]{1,0:T(8,128)(2,1)S(1)}, bf16[128,384]{1,0:T(8,128)(2,1)S(1)}, u32[]{:S(2)}, u32[]{:S(2)}) collective-permute-start(bf16[128,384]{1,0:T(8,128)(2,1)S(1)} %get-tuple-element.39), channel_id=1, source_target_pairs={{0,28},{4,24},{8,20},{12,16},{16,12},{20,8},{24,4},{28,0},{1,29},{... | collective-permute-start | bytes 294920 | tf_op jit(solution)/shard_map/ppermute | solution.py:649
  31.2 0.1 fusion.refs_1_
  31.4 7.8 %collective-permute-done.5.refs_5_ = bf16[128,384]{1,0:T(8,128)(2,1)S(1)} collective-permute-done((bf16[128,384]{1,0:T(8,128)(2,1)S(1)}, bf16[128,384]{1,0:T(8,128)(2,1)S(1)}, u32[]{:S(2)}, u32[]{:S(2)}) %collective-permute-start.5) | collective-permute-done | bytes 98336 | tf_op jit(solution)/shard_map/ppermute | solution.py:649
  39.3 0.6 gather_blocks.1.refs_3_
  40.2 2.3 %context_rows.3.refs_2_ = bf16[512,2048]{1,0:T(8,128)(2,1)S(1)} custom-call(s32[2,1,256]{2,1,0:T(1,128)S(1)} %broadcast_in_dim.39.refs_0_, f32[2,2,2048]{2,1,0:T(2,128)S(1)} %pad_maximum_fusion.1.refs_1_, f32[4,16,2048]{2,1,0:T(8,128)S(1)} %pad_maximum_fusion.refs_2_, bf16[256,2048]{1,0:T(8,128)(2,1)S(1)} %copy-done.2), custom_call_target="tpu_custom_call" | custom-call | flops 536870912 | bytes 2097152 | tf_op jit(solution)/shard_map/context_rows/pallas_call | solution.py:231
  42.6 7.5 %context_rows.2.refs_1_ = bf16[2048,2048]{1,0:T(8,128)(2,1)S(1)} custom-call(s32[8,1,256]{2,1,0:T(1,128)S(1)} %bitcast.23, f32[8,2,2048]{2,1,0:T(2,128)S(1)} %fusion.refs_1_, f32[4,16,2048]{2,1,0:T(8,128)S(1)} %pad_maximum_fusion.refs_2_, bf16[256,2048]{1,0:T(8,128)(2,1)S(1)} %copy-done.2), custom_call_target="tpu_custom_call" | custom-call | flops 2147483648 | bytes 8388608 | tf_op jit(solution)/shard_map/context_rows/pallas_call | solution.py:231
  50.1 3.6 %context_heads.1 = (bf16[2048,256]{1,0:T(8,128)(2,1)S(1)}, bf16[8,2,32,128]{3,2,1,0:T(8,128)(2,1)S(1)}, bf16[32,2048]{1,0:T(8,128)(2,1)S(1)}) custom-call(s32[5]{0:T(128)S(1)} %stack.40.core_ref.scalars_ref.refs_0_, bf16[2048,2048]{1,0:T(8,128)(2,1)S(1)} %context_rows.2.refs_1_, bf16[512,2048]{1,0:T(8,128)(2,1)S(1)} %context_rows.3.refs_2_, ...), custom_call_target="tpu_custom_call" | custom-call | flops 2684354560 | bytes 8388608 | tf_op jit(solution)/shard_map/context_heads/pallas_call | solution.py:494
  53.6 0.6 collective-permute-start.9
  54.2 2.3 %constant_dynamic-slice_fusion.1 = bf16[512,1024]{1,0:T(8,128)(2,1)} fusion(bf16[2048,1024]{1,0:T(8,128)(2,1)} %refs_4_.1, s32[]{:T(128)S(6)} %select_n.86), kind=kLoop, calls=%fused_computation.33 | loop fusion | bytes 2097156 | tf_op jit(solution)/shard_map/dynamic_slice | solution.py:653
  56.5 2.3 %constant_dynamic-slice_fusion = bf16[256,2048]{1,0:T(8,128)(2,1)} fusion(bf16[1024,2048]{1,0:T(8,128)(2,1)} %refs_5_.1, s32[]{:T(128)S(6)} %select_n.87), kind=kLoop, calls=%fused_computation.32 | loop fusion | bytes 2097156 | tf_op jit(solution)/shard_map/dynamic_slice | solution.py:653
  58.9 2.0 collective-permute-start.24
  60.9 5.8 %head_attention.2 = bf16[8,2,32,128]{3,2,1,0:T(8,128)(2,1)} custom-call(s32[5]{0:T(128)S(1)} %stack.40.core_ref.scalars_ref.refs_0_, bf16[8,2,32,128]{3,2,1,0:T(8,128)(2,1)S(1)} %get-tuple-element.41.refs_1_, bf16[1,4,512,256]{3,2,1,0:T(8,128)(2,1)S(1)} %bitcast.24, bf16[1,4,512,256]{3,2,1,0:T(8,128)(2,1)} %bitcast.11.refs_3_), custom_call_target="tpu_custom_call" | custom-call | flops 2147483648 | bytes 2097152 | tf_op jit(solution)/shard_map/head_attention/pallas_call | solution.py:296
  66.7 5.6 %all-to-all-start.1 = ((bf16[8,64,128]{2,1,0:T(8,128)(2,1)}), bf16[8,64,128]{2,1,0:T(8,128)(2,1)S(1)}, u32[]{:S(2)}, u32[]{:S(2)}) async-start(bf16[8,64,128]{2,1,0:T(8,128)(2,1)} %bitcast.12), calls=%async_computation.1 | async-start | bytes 262144 | tf_op jit(solution)/shard_map/all_to_all | solution.py:646
  72.3 33.4 %all-to-all-done.1.heads_ref = bf16[8,64,128]{2,1,0:T(8,128)(2,1)S(1)} async-done(((bf16[8,64,128]{2,1,0:T(8,128)(2,1)}), bf16[8,64,128]{2,1,0:T(8,128)(2,1)S(1)}, u32[]{:S(2)}, u32[]{:S(2)}) %all-to-all-start.1) | async-done | bytes 131104 | tf_op jit(solution)/shard_map/all_to_all | solution.py:646
  105.7 2.4 %project_rows.2 = (f32[32,2048]{1,0:T(8,128)S(1)}, bf16[32,2048]{1,0:T(8,128)(2,1)S(1)}) custom-call(s32[5]{0:T(128)S(1)} %stack.40.core_ref.scalars_ref.refs_0_, bf16[8,64,128]{2,1,0:T(8,128)(2,1)S(1)} %all-to-all-done.1.heads_ref, bf16[512,2048]{1,0:T(8,128)(2,1)S(1)} %copy-done.3, bf16[512,2048]{1,0:T(8,128)(2,1)} %collective-permute-done.10.theirs_ref), custom_call_target="tpu_custom_call" | custom-call | flops 268435456 | bytes 4194304 | tf_op jit(solution)/shard_map/project_rows/pallas_call | solution.py:366
  108.2 1.6 collective-permute-start.11
  109.8 3.4 %collective-permute-done.11.came_ref = bf16[32,2048]{1,0:T(8,128)(2,1)S(1)} collective-permute-done((bf16[32,2048]{1,0:T(8,128)(2,1)S(1)}, bf16[32,2048]{1,0:T(8,128)(2,1)S(1)}, u32[]{:S(2)}, u32[]{:S(2)}) %collective-permute-start.11) | collective-permute-done | bytes 131104 | tf_op jit(solution)/shard_map/ppermute | solution.py:643
  113.2 0.1 add_norm.2
  113.4 1.6 collective-permute-start.12
  115.0 0.5 collective-permute-start.21
  115.5 4.3 %collective-permute-done.12.refs_2_ = bf16[32,2048]{1,0:T(8,128)(2,1)S(1)} collective-permute-done((bf16[32,2048]{1,0:T(8,128)(2,1)S(1)}, bf16[32,2048]{1,0:T(8,128)(2,1)S(1)}, u32[]{:S(2)}, u32[]{:S(2)}) %collective-permute-start.12) | collective-permute-done | bytes 131104 | tf_op jit(solution)/shard_map/ppermute | solution.py:643
  119.8 0.6 copy-done.11
  120.5 7.1 %triple_heads.1 = bf16[8,64,384]{2,1,0:T(8,128)(2,1)} custom-call(s32[5]{0:T(128)} %copy-done.9, bf16[32,2048]{1,0:T(8,128)(2,1)} %copy-done.8, bf16[32,2048]{1,0:T(8,128)(2,1)} %copy-done.11, bf16[3,2048,512]{2,1,0:T(8,128)(2,1)} %refs_3_.5, bf16[3,2048,512]{2,1,0:T(8,128)(2,1)} %collective-permute-done.13.refs_4_), custom_call_target="tpu_custom_call" | custom-call | flops 805306368 | bytes 12582912 | tf_op jit(solution)/shard_map/triple_heads/pallas_call | solution.py:414
  127.6 5.6 %all-to-all-start.2 = ((bf16[8,64,384]{2,1,0:T(8,128)(2,1)}), bf16[8,64,384]{2,1,0:T(8,128)(2,1)S(1)}, u32[]{:S(2)}, u32[]{:S(2)}) async-start(bf16[8,64,384]{2,1,0:T(8,128)(2,1)} %triple_heads.1), calls=%async_computation.2 | async-start | bytes 786432 | tf_op jit(solution)/shard_map/all_to_all | solution.py:646
  133.2 1.6 collective-permute-start.25
  134.8 7.6 %all-to-all-done.2 = bf16[8,64,384]{2,1,0:T(8,128)(2,1)S(1)} async-done(((bf16[8,64,384]{2,1,0:T(8,128)(2,1)}), bf16[8,64,384]{2,1,0:T(8,128)(2,1)S(1)}, u32[]{:S(2)}, u32[]{:S(2)}) %all-to-all-start.2) | async-done | bytes 393248 | tf_op jit(solution)/shard_map/all_to_all | solution.py:646
  142.4 0.5 collective-permute-start.22
  143.0 19.1 %collective-permute-done.25.refs_11_ = bf16[256,2048]{1,0:T(8,128)(2,1)} collective-permute-done((bf16[256,2048]{1,0:T(8,128)(2,1)}, bf16[256,2048]{1,0:T(8,128)(2,1)}, u32[]{:S(2)}, u32[]{:S(2)}) %collective-permute-start.25) | collective-permute-done | bytes 1048608 | tf_op jit(solution)/shard_map/ppermute | solution.py:643
  162.1 0.5 collective-permute-start.27
  162.6 2.5 %head_attention.3 = bf16[8,2,32,128]{3,2,1,0:T(8,128)(2,1)} custom-call(s32[5]{0:T(128)S(1)} %copy-done.10, bf16[8,2,32,384]{3,2,1,0:T(8,128)(2,1)S(1)} %bitcast.21, bf16[8,2,32,384]{3,2,1,0:T(8,128)(2,1)S(1)} %bitcast.22, bf16[8,2,32,384]{3,2,1,0:T(8,128)(2,1)S(1)} %collective-permute-done.14.refs_3_), custom_call_target="tpu_custom_call" | custom-call | flops 536870912 | bytes 524288 | tf_op jit(solution)/shard_map/head_attention/pallas_call | solution.py:296
  165.1 5.7 %all-to-all-start.3 = ((bf16[8,64,128]{2,1,0:T(8,128)(2,1)}), bf16[8,64,128]{2,1,0:T(8,128)(2,1)S(1)}, u32[]{:S(2)}, u32[]{:S(2)}) async-start(bf16[8,64,128]{2,1,0:T(8,128)(2,1)} %bitcast.14), calls=%async_computation.3 | async-start | bytes 262144 | tf_op jit(solution)/shard_map/all_to_all | solution.py:646
  170.8 7.3 %all-to-all-done.3.heads_ref = bf16[8,64,128]{2,1,0:T(8,128)(2,1)S(1)} async-done(((bf16[8,64,128]{2,1,0:T(8,128)(2,1)}), bf16[8,64,128]{2,1,0:T(8,128)(2,1)S(1)}, u32[]{:S(2)}, u32[]{:S(2)}) %all-to-all-start.3) | async-done | bytes 131104 | tf_op jit(solution)/shard_map/all_to_all | solution.py:646
  178.2 2.6 %project_rows.3 = (f32[32,2048]{1,0:T(8,128)S(1)}, bf16[32,2048]{1,0:T(8,128)(2,1)S(1)}) custom-call(s32[5]{0:T(128)S(1)} %copy-done.10, bf16[8,64,128]{2,1,0:T(8,128)(2,1)S(1)} %all-to-all-done.3.heads_ref, bf16[512,2048]{1,0:T(8,128)(2,1)} %mine_ref.3, bf16[512,2048]{1,0:T(8,128)(2,1)S(1)} %collective-permute-done.15.theirs_ref), custom_call_target="tpu_custom_call" | custom-call | flops 268435456 | bytes 4194304 | tf_op jit(solution)/shard_map/project_rows/pallas_call | solution.py:366
  180.8 1.5 collective-permute-start.16
  182.3 3.5 %collective-permute-done.16.came_ref = bf16[32,2048]{1,0:T(8,128)(2,1)S(1)} collective-permute-done((bf16[32,2048]{1,0:T(8,128)(2,1)S(1)}, bf16[32,2048]{1,0:T(8,128)(2,1)S(1)}, u32[]{:S(2)}, u32[]{:S(2)}) %collective-permute-start.16) | collective-permute-done | bytes 131104 | tf_op jit(solution)/shard_map/ppermute | solution.py:643
  185.8 0.1 add_norm.3
  186.1 1.3 collective-permute-start.18
  187.3 3.1 %collective-permute-start.19 = (bf16[32,2048]{1,0:T(8,128)(2,1)S(1)}, bf16[32,2048]{1,0:T(8,128)(2,1)S(1)}, u32[]{:S(2)}, u32[]{:S(2)}) collective-permute-start(bf16[32,2048]{1,0:T(8,128)(2,1)S(1)} %get-tuple-element.50.refs_0_), channel_id=1, source_target_pairs={{0,24},{4,28},{8,16},{12,20},{16,8},{20,12},{24,0},{28,4},{1,25},{... | collective-permute-start | bytes 393224 | tf_op jit(solution)/shard_map/ppermute | solution.py:649
  190.4 2.6 %collective-permute-done.17.refs_1_ = bf16[32,2048]{1,0:T(8,128)(2,1)S(1)} collective-permute-done((bf16[32,2048]{1,0:T(8,128)(2,1)S(1)}, bf16[32,2048]{1,0:T(8,128)(2,1)S(1)}, u32[]{:S(2)}, u32[]{:S(2)}) %collective-permute-start.17) | collective-permute-done | bytes 131104 | tf_op jit(solution)/shard_map/ppermute | solution.py:649
  193.0 3.9 %collective-permute-done.18.refs_2_ = bf16[32,2048]{1,0:T(8,128)(2,1)S(1)} collective-permute-done((bf16[32,2048]{1,0:T(8,128)(2,1)S(1)}, bf16[32,2048]{1,0:T(8,128)(2,1)S(1)}, u32[]{:S(2)}, u32[]{:S(2)}) %collective-permute-start.18) | collective-permute-done | bytes 131104 | tf_op jit(solution)/shard_map/ppermute | solution.py:649
  196.9 2.2 copy-done.1
  199.1 6.2 %mlp_shares.1 = (f32[32,2048]{1,0:T(8,128)S(1)}, bf16[32,2048]{1,0:T(8,128)(2,1)S(1)}, bf16[32,2048]{1,0:T(8,128)(2,1)S(1)}, bf16[32,2048]{1,0:T(8,128)(2,1)S(1)}) custom-call(s32[5]{0:T(128)S(1)} %copy-done.10, bf16[32,2048]{1,0:T(8,128)(2,1)S(1)} %get-tuple-element.50.refs_0_, bf16[32,2048]{1,0:T(8,128)(2,1)S(1)} %collective-permute-done.17.refs_1_, ...), custom_call_target="tpu_custom_call" | custom-call | flops 2147483648 | bytes 16777216 | tf_op jit(solution)/shard_map/mlp_shares/pallas_call | solution.py:593
  205.3 2.0 collective-permute-start.28
  207.3 0.2 collective-permute-start.29
  207.5 2.3 %collective-permute-start.30 = (bf16[32,2048]{1,0:T(8,128)(2,1)S(1)}, bf16[32,2048]{1,0:T(8,128)(2,1)S(1)}, u32[]{:S(2)}, u32[]{:S(2)}) collective-permute-start(bf16[32,2048]{1,0:T(8,128)(2,1)S(1)} %get-tuple-element.54), channel_id=1, source_target_pairs={{0,24},{4,28},{8,16},{12,20},{16,8},{20,12},{24,0},{28,4},{1,25},{... | collective-permute-start | bytes 393224 | tf_op jit(solution)/shard_map/ppermute | solution.py:649
  209.8 3.3 %collective-permute-done.28 = bf16[32,2048]{1,0:T(8,128)(2,1)S(1)} collective-permute-done((bf16[32,2048]{1,0:T(8,128)(2,1)S(1)}, bf16[32,2048]{1,0:T(8,128)(2,1)S(1)}, u32[]{:S(2)}, u32[]{:S(2)}) %collective-permute-start.28) | collective-permute-done | bytes 131104 | tf_op jit(solution)/shard_map/ppermute | solution.py:649
  213.1 4.7 %collective-permute-done.29 = bf16[32,2048]{1,0:T(8,128)(2,1)S(1)} collective-permute-done((bf16[32,2048]{1,0:T(8,128)(2,1)S(1)}, bf16[32,2048]{1,0:T(8,128)(2,1)S(1)}, u32[]{:S(2)}, u32[]{:S(2)}) %collective-permute-start.29) | collective-permute-done | bytes 131104 | tf_op jit(solution)/shard_map/ppermute | solution.py:649
  217.8 0.7 fusion.1
  (68 shorter events, 0.9 us)
Async XLA Ops:
  0.0 40.2 %copy-start.2 = (bf16[256,2048]{1,0:T(8,128)(2,1)S(1)}, bf16[256,2048]{1,0:T(8,128)(2,1)}, u32[]{:S(2)}) copy-start(bf16[256,2048]{1,0:T(8,128)(2,1)} %refs_3_.4) | copy-start | bytes 3145732
  0.0 119.8 %collective-permute-start.13 = (bf16[3,2048,512]{2,1,0:T(8,128)(2,1)}, bf16[3,2048,512]{2,1,0:T(8,128)(2,1)}, u32[]{:S(2)}, u32[]{:S(2)}) collective-permute-start(bf16[3,2048,512]{2,1,0:T(8,128)(2,1)} %refs_3_.5), channel_id=1, source_target_pairs={{0,1},{1,0},{2,3},{3,2},{4,5},{5,4},{6,7},{7,6},{8,9},{9,8},{10,11... | collective-permute-start | bytes 18874376 | tf_op jit(solution)/shard_map/ppermute | solution.py:640
  1.2 1.0 copy-start.4
  2.3 0.9 copy-start.7
  3.2 102.5 %copy-start.9 = (s32[5]{0:T(128)}, s32[5]{0:T(128)S(1)}, u32[]{:S(2)}) copy-start(s32[5]{0:T(128)S(1)} %stack.40.core_ref.scalars_ref.refs_0_) | copy-start | bytes 64
  3.9 12.4 %collective-permute-start = (bf16[4,128,384]{2,1,0:T(8,128)(2,1)S(1)}, bf16[4,128,384]{2,1,0:T(8,128)(2,1)S(1)}, u32[]{:S(2)}, u32[]{:S(2)}) collective-permute-start(bf16[4,128,384]{2,1,0:T(8,128)(2,1)S(1)} %get-tuple-element.31), channel_id=1, source_target_pairs={{0,1},{1,0},{2,3},{3,2},{4,5},{5,4},{6,7},{7,6},{8,9},{9,8},{10,11... | collective-permute-start | bytes 1179656 | tf_op jit(solution)/shard_map/ppermute | solution.py:640
  5.4 34.7 %all-to-all-start = ((s32[8,4,128]{2,1,0:T(4,128)}), s32[8,4,128]{2,1,0:T(4,128)S(1)}, u32[]{:S(2)}, u32[]{:S(2)}) async-start(s32[8,4,128]{2,1,0:T(4,128)} %broadcast_in_dim.37), calls=%async_computation | async-start | bytes 32768 | tf_op jit(solution)/shard_map/all_to_all | solution.py:646
  17.1 6.6 %collective-permute-start.1 = (bf16[128,384]{1,0:T(8,128)(2,1)S(1)}, bf16[128,384]{1,0:T(8,128)(2,1)S(1)}, u32[]{:S(2)}, u32[]{:S(2)}) collective-permute-start(bf16[128,384]{1,0:T(8,128)(2,1)S(1)} %get-tuple-element.33), channel_id=1, source_target_pairs={{0,4},{4,0},{8,12},{12,8},{16,20},{20,16},{24,28},{28,24},{1,5},{5... | collective-permute-start | bytes 294920 | tf_op jit(solution)/shard_map/ppermute | solution.py:649
  19.2 7.1 %collective-permute-start.2 = (bf16[128,384]{1,0:T(8,128)(2,1)S(1)}, bf16[128,384]{1,0:T(8,128)(2,1)S(1)}, u32[]{:S(2)}, u32[]{:S(2)}) collective-permute-start(bf16[128,384]{1,0:T(8,128)(2,1)S(1)} %get-tuple-element.34), channel_id=1, source_target_pairs={{0,8},{4,12},{8,0},{12,4},{16,24},{20,28},{24,16},{28,20},{1,9},{5... | collective-permute-start | bytes 294920 | tf_op jit(solution)/shard_map/ppermute | solution.py:649
  20.6 7.8 %collective-permute-start.3 = (bf16[128,384]{1,0:T(8,128)(2,1)S(1)}, bf16[128,384]{1,0:T(8,128)(2,1)S(1)}, u32[]{:S(2)}, u32[]{:S(2)}) collective-permute-start(bf16[128,384]{1,0:T(8,128)(2,1)S(1)} %get-tuple-element.35), channel_id=1, source_target_pairs={{0,12},{4,8},{8,4},{12,0},{16,28},{20,24},{24,20},{28,16},{1,13},{... | collective-permute-start | bytes 294920 | tf_op jit(solution)/shard_map/ppermute | solution.py:649
  20.8 10.6 %collective-permute-start.4 = (bf16[128,384]{1,0:T(8,128)(2,1)S(1)}, bf16[128,384]{1,0:T(8,128)(2,1)S(1)}, u32[]{:S(2)}, u32[]{:S(2)}) collective-permute-start(bf16[128,384]{1,0:T(8,128)(2,1)S(1)} %get-tuple-element.36), channel_id=1, source_target_pairs={{0,16},{4,20},{8,24},{12,28},{16,0},{20,4},{24,8},{28,12},{1,17},{... | collective-permute-start | bytes 294920 | tf_op jit(solution)/shard_map/ppermute | solution.py:649
  23.7 15.6 %collective-permute-start.5 = (bf16[128,384]{1,0:T(8,128)(2,1)S(1)}, bf16[128,384]{1,0:T(8,128)(2,1)S(1)}, u32[]{:S(2)}, u32[]{:S(2)}) collective-permute-start(bf16[128,384]{1,0:T(8,128)(2,1)S(1)} %get-tuple-element.37), channel_id=1, source_target_pairs={{0,20},{4,16},{8,28},{12,24},{16,4},{20,0},{24,12},{28,8},{1,21},{... | collective-permute-start | bytes 294920 | tf_op jit(solution)/shard_map/ppermute | solution.py:649
  26.2 13.1 %collective-permute-start.6 = (bf16[128,384]{1,0:T(8,128)(2,1)S(1)}, bf16[128,384]{1,0:T(8,128)(2,1)S(1)}, u32[]{:S(2)}, u32[]{:S(2)}) collective-permute-start(bf16[128,384]{1,0:T(8,128)(2,1)S(1)} %get-tuple-element.38), channel_id=1, source_target_pairs={{0,24},{4,28},{8,16},{12,20},{16,8},{20,12},{24,0},{28,4},{1,25},{... | collective-permute-start | bytes 294920 | tf_op jit(solution)/shard_map/ppermute | solution.py:649
  28.4 10.9 %collective-permute-start.7 = (bf16[128,384]{1,0:T(8,128)(2,1)S(1)}, bf16[128,384]{1,0:T(8,128)(2,1)S(1)}, u32[]{:S(2)}, u32[]{:S(2)}) collective-permute-start(bf16[128,384]{1,0:T(8,128)(2,1)S(1)} %get-tuple-element.39), channel_id=1, source_target_pairs={{0,28},{4,24},{8,20},{12,16},{16,12},{20,8},{24,4},{28,0},{1,29},{... | collective-permute-start | bytes 294920 | tf_op jit(solution)/shard_map/ppermute | solution.py:649
  31.4 40.9 %collective-permute-start.10 = (bf16[512,2048]{1,0:T(8,128)(2,1)}, bf16[512,2048]{1,0:T(8,128)(2,1)}, u32[]{:S(2)}, u32[]{:S(2)}) collective-permute-start(bf16[512,2048]{1,0:T(8,128)(2,1)} %mine_ref.2), channel_id=1, source_target_pairs={{0,1},{1,0},{2,3},{3,2},{4,5},{5,4},{6,7},{7,6},{8,9},{9,8},{10,11... | collective-permute-start | bytes 6291464 | tf_op jit(solution)/shard_map/ppermute | solution.py:640
  39.9 10.2 %collective-permute-start.8 = (bf16[8,128,384]{2,1,0:T(8,128)(2,1)S(1)}, bf16[8,128,384]{2,1,0:T(8,128)(2,1)S(1)}, u32[]{:S(2)}, u32[]{:S(2)}) collective-permute-start(bf16[8,128,384]{2,1,0:T(8,128)(2,1)S(1)} %gather_blocks.1.refs_3_), channel_id=1, source_target_pairs={{0,1},{1,0},{2,3},{3,2},{4,5},{5,4},{6,7},{7,6},{8,9},{9,8},{10,11... | collective-permute-start | bytes 2359304 | tf_op jit(solution)/shard_map/ppermute | solution.py:640
  53.6 7.2 %collective-permute-start.9 = (bf16[2048,256]{1,0:T(8,128)(2,1)S(1)}, bf16[2048,256]{1,0:T(8,128)(2,1)}, u32[]{:S(2)}, u32[]{:S(2)}) collective-permute-start(bf16[2048,256]{1,0:T(8,128)(2,1)S(1)} %get-tuple-element.42), channel_id=1, source_target_pairs={{0,1},{1,0},{2,3},{3,2},{4,5},{5,4},{6,7},{7,6},{8,9},{9,8},{10,11... | collective-permute-start | bytes 3145736 | tf_op jit(solution)/shard_map/ppermute | solution.py:640
  56.5 58.4 %collective-permute-start.20 = (bf16[512,1024]{1,0:T(8,128)(2,1)}, bf16[512,1024]{1,0:T(8,128)(2,1)}, u32[]{:S(2)}, u32[]{:S(2)}) collective-permute-start(bf16[512,1024]{1,0:T(8,128)(2,1)} %constant_dynamic-slice_fusion.1), channel_id=1, source_target_pairs={{0,4},{4,0},{8,12},{12,8},{16,20},{20,16},{24,28},{28,24},{1,5},{5... | collective-permute-start | bytes 3145736 | tf_op jit(solution)/shard_map/ppermute | solution.py:649
  58.9 46.9 %copy-start.3 = (bf16[512,2048]{1,0:T(8,128)(2,1)S(1)}, bf16[512,2048]{1,0:T(8,128)(2,1)}, u32[]{:S(2)}) copy-start(bf16[512,2048]{1,0:T(8,128)(2,1)} %mine_ref.2) | copy-start | bytes 6291460
  58.9 74.4 %collective-permute-start.24 = (bf16[256,2048]{1,0:T(8,128)(2,1)}, bf16[256,2048]{1,0:T(8,128)(2,1)}, u32[]{:S(2)}, u32[]{:S(2)}) collective-permute-start(bf16[256,2048]{1,0:T(8,128)(2,1)} %constant_dynamic-slice_fusion), channel_id=1, source_target_pairs={{0,4},{4,0},{8,12},{12,8},{16,20},{20,16},{24,28},{28,24},{1,5},{5... | collective-permute-start | bytes 3145736 | tf_op jit(solution)/shard_map/ppermute | solution.py:649
  66.7 39.0 %all-to-all-start.1 = ((bf16[8,64,128]{2,1,0:T(8,128)(2,1)}), bf16[8,64,128]{2,1,0:T(8,128)(2,1)S(1)}, u32[]{:S(2)}, u32[]{:S(2)}) async-start(bf16[8,64,128]{2,1,0:T(8,128)(2,1)} %bitcast.12), calls=%async_computation.1 | async-start | bytes 262144 | tf_op jit(solution)/shard_map/all_to_all | solution.py:646
  108.2 5.0 %collective-permute-start.11 = (bf16[32,2048]{1,0:T(8,128)(2,1)S(1)}, bf16[32,2048]{1,0:T(8,128)(2,1)S(1)}, u32[]{:S(2)}, u32[]{:S(2)}) collective-permute-start(bf16[32,2048]{1,0:T(8,128)(2,1)S(1)} %get-tuple-element.44), channel_id=1, source_target_pairs={{0,2},{1,3},{2,0},{3,1},{4,6},{5,7},{6,4},{7,5},{8,10},{9,11},{10,... | collective-permute-start | bytes 393224 | tf_op jit(solution)/shard_map/ppermute | solution.py:643
  109.8 61.1 %collective-permute-start.15 = (bf16[512,2048]{1,0:T(8,128)(2,1)}, bf16[512,2048]{1,0:T(8,128)(2,1)S(1)}, u32[]{:S(2)}, u32[]{:S(2)}) collective-permute-start(bf16[512,2048]{1,0:T(8,128)(2,1)} %mine_ref.3), channel_id=1, source_target_pairs={{0,1},{1,0},{2,3},{3,2},{4,5},{5,4},{6,7},{7,6},{8,9},{9,8},{10,11... | collective-permute-start | bytes 6291464 | tf_op jit(solution)/shard_map/ppermute | solution.py:640
  113.4 6.5 %copy-start.8 = (bf16[32,2048]{1,0:T(8,128)(2,1)}, bf16[32,2048]{1,0:T(8,128)(2,1)S(1)}, u32[]{:S(2)}) copy-start(bf16[32,2048]{1,0:T(8,128)(2,1)S(1)} %get-tuple-element.46.refs_1_) | copy-start | bytes 393220
  113.4 14.3 %copy-start.5 = (f32[32,2048]{1,0:T(8,128)}, f32[32,2048]{1,0:T(8,128)S(1)}, u32[]{:S(2)}) copy-start(f32[32,2048]{1,0:T(8,128)S(1)} %get-tuple-element.45.base_ref) | copy-start | bytes 786436
  113.4 49.2 %copy-start.10 = (s32[5]{0:T(128)S(1)}, s32[5]{0:T(128)}, u32[]{:S(2)}) copy-start(s32[5]{0:T(128)} %copy-done.9) | copy-start | bytes 64
  113.4 6.4 %collective-permute-start.12 = (bf16[32,2048]{1,0:T(8,128)(2,1)S(1)}, bf16[32,2048]{1,0:T(8,128)(2,1)S(1)}, u32[]{:S(2)}, u32[]{:S(2)}) collective-permute-start(bf16[32,2048]{1,0:T(8,128)(2,1)S(1)} %get-tuple-element.46.refs_1_), channel_id=1, source_target_pairs={{0,2},{1,3},{2,0},{3,1},{4,6},{5,7},{6,4},{7,5},{8,10},{9,11},{10,... | collective-permute-start | bytes 393224 | tf_op jit(solution)/shard_map/ppermute | solution.py:643
  115.0 28.0 %collective-permute-start.21 = (bf16[512,1024]{1,0:T(8,128)(2,1)}, bf16[512,1024]{1,0:T(8,128)(2,1)}, u32[]{:S(2)}, u32[]{:S(2)}) collective-permute-start(bf16[512,1024]{1,0:T(8,128)(2,1)} %collective-permute-done.20.refs_6_), channel_id=1, source_target_pairs={{0,2},{1,3},{2,0},{3,1},{4,6},{5,7},{6,4},{7,5},{8,10},{9,11},{10,... | collective-permute-start | bytes 3145736 | tf_op jit(solution)/shard_map/ppermute | solution.py:643
  119.8 0.7 copy-start.11
  127.6 14.8 %all-to-all-start.2 = ((bf16[8,64,384]{2,1,0:T(8,128)(2,1)}), bf16[8,64,384]{2,1,0:T(8,128)(2,1)S(1)}, u32[]{:S(2)}, u32[]{:S(2)}) async-start(bf16[8,64,384]{2,1,0:T(8,128)(2,1)} %triple_heads.1), calls=%async_computation.2 | async-start | bytes 786432 | tf_op jit(solution)/shard_map/all_to_all | solution.py:646
  133.2 28.8 %collective-permute-start.25 = (bf16[256,2048]{1,0:T(8,128)(2,1)}, bf16[256,2048]{1,0:T(8,128)(2,1)}, u32[]{:S(2)}, u32[]{:S(2)}) collective-permute-start(bf16[256,2048]{1,0:T(8,128)(2,1)} %collective-permute-done.24.refs_10_), channel_id=1, source_target_pairs={{0,2},{1,3},{2,0},{3,1},{4,6},{5,7},{6,4},{7,5},{8,10},{9,11},{10,... | collective-permute-start | bytes 3145736 | tf_op jit(solution)/shard_map/ppermute | solution.py:643
  142.4 19.6 %collective-permute-start.14 = (bf16[8,2,32,384]{3,2,1,0:T(8,128)(2,1)S(1)}, bf16[8,2,32,384]{3,2,1,0:T(8,128)(2,1)S(1)}, u32[]{:S(2)}, u32[]{:S(2)}) collective-permute-start(bf16[8,2,32,384]{3,2,1,0:T(8,128)(2,1)S(1)} %bitcast.20), channel_id=1, source_target_pairs={{0,1},{1,0},{2,3},{3,2},{4,5},{5,4},{6,7},{7,6},{8,9},{9,8},{10,11... | collective-permute-start | bytes 1179656 | tf_op jit(solution)/shard_map/ppermute | solution.py:640
  142.4 43.6 %collective-permute-start.22 = (bf16[512,1024]{1,0:T(8,128)(2,1)}, bf16[512,1024]{1,0:T(8,128)(2,1)}, u32[]{:S(2)}, u32[]{:S(2)}) collective-permute-start(bf16[512,1024]{1,0:T(8,128)(2,1)} %collective-permute-done.20.refs_6_), channel_id=1, source_target_pairs={{0,1},{1,0},{2,3},{3,2},{4,5},{5,4},{6,7},{7,6},{8,9},{9,8},{10,11... | collective-permute-start | bytes 3145736 | tf_op jit(solution)/shard_map/ppermute | solution.py:640
  143.0 44.4 %collective-permute-start.26 = (bf16[256,2048]{1,0:T(8,128)(2,1)}, bf16[256,2048]{1,0:T(8,128)(2,1)}, u32[]{:S(2)}, u32[]{:S(2)}) collective-permute-start(bf16[256,2048]{1,0:T(8,128)(2,1)} %collective-permute-done.24.refs_10_), channel_id=1, source_target_pairs={{0,1},{1,0},{2,3},{3,2},{4,5},{5,4},{6,7},{7,6},{8,9},{9,8},{10,11... | collective-permute-start | bytes 3145736 | tf_op jit(solution)/shard_map/ppermute | solution.py:640
  162.1 28.4 %collective-permute-start.23 = (bf16[512,1024]{1,0:T(8,128)(2,1)}, bf16[512,1024]{1,0:T(8,128)(2,1)}, u32[]{:S(2)}, u32[]{:S(2)}) collective-permute-start(bf16[512,1024]{1,0:T(8,128)(2,1)} %collective-permute-done.21.refs_7_), channel_id=1, source_target_pairs={{0,1},{1,0},{2,3},{3,2},{4,5},{5,4},{6,7},{7,6},{8,9},{9,8},{10,11... | collective-permute-start | bytes 3145736 | tf_op jit(solution)/shard_map/ppermute | solution.py:640
  162.1 28.4 %collective-permute-start.27 = (bf16[256,2048]{1,0:T(8,128)(2,1)}, bf16[256,2048]{1,0:T(8,128)(2,1)}, u32[]{:S(2)}, u32[]{:S(2)}) collective-permute-start(bf16[256,2048]{1,0:T(8,128)(2,1)} %collective-permute-done.25.refs_11_), channel_id=1, source_target_pairs={{0,1},{1,0},{2,3},{3,2},{4,5},{5,4},{6,7},{7,6},{8,9},{9,8},{10,11... | collective-permute-start | bytes 3145736 | tf_op jit(solution)/shard_map/ppermute | solution.py:640
  165.1 20.7 %copy-start.6 = (f32[32,2048]{1,0:T(8,128)S(1)}, f32[32,2048]{1,0:T(8,128)}, u32[]{:S(2)}) copy-start(f32[32,2048]{1,0:T(8,128)} %copy-done.5) | copy-start | bytes 786436
  165.1 13.1 %all-to-all-start.3 = ((bf16[8,64,128]{2,1,0:T(8,128)(2,1)}), bf16[8,64,128]{2,1,0:T(8,128)(2,1)S(1)}, u32[]{:S(2)}, u32[]{:S(2)}) async-start(bf16[8,64,128]{2,1,0:T(8,128)(2,1)} %bitcast.14), calls=%async_computation.3 | async-start | bytes 262144 | tf_op jit(solution)/shard_map/all_to_all | solution.py:646
  178.2 18.7 %copy-start = (bf16[2048,1024]{1,0:T(8,128)(2,1)S(1)}, bf16[2048,1024]{1,0:T(8,128)(2,1)}, u32[]{:S(2)}) copy-start(bf16[2048,1024]{1,0:T(8,128)(2,1)} %refs_4_.1) | copy-start | bytes 12582916
  180.8 5.0 %collective-permute-start.16 = (bf16[32,2048]{1,0:T(8,128)(2,1)S(1)}, bf16[32,2048]{1,0:T(8,128)(2,1)S(1)}, u32[]{:S(2)}, u32[]{:S(2)}) collective-permute-start(bf16[32,2048]{1,0:T(8,128)(2,1)S(1)} %get-tuple-element.48), channel_id=1, source_target_pairs={{0,2},{1,3},{2,0},{3,1},{4,6},{5,7},{6,4},{7,5},{8,10},{9,11},{10,... | collective-permute-start | bytes 393224 | tf_op jit(solution)/shard_map/ppermute | solution.py:643
  186.0 7.1 %collective-permute-start.17 = (bf16[32,2048]{1,0:T(8,128)(2,1)S(1)}, bf16[32,2048]{1,0:T(8,128)(2,1)S(1)}, u32[]{:S(2)}, u32[]{:S(2)}) collective-permute-start(bf16[32,2048]{1,0:T(8,128)(2,1)S(1)} %get-tuple-element.50.refs_0_), channel_id=1, source_target_pairs={{0,8},{4,12},{8,0},{12,4},{16,24},{20,28},{24,16},{28,20},{1,9},{5... | collective-permute-start | bytes 393224 | tf_op jit(solution)/shard_map/ppermute | solution.py:649
  186.1 10.9 %collective-permute-start.18 = (bf16[32,2048]{1,0:T(8,128)(2,1)S(1)}, bf16[32,2048]{1,0:T(8,128)(2,1)S(1)}, u32[]{:S(2)}, u32[]{:S(2)}) collective-permute-start(bf16[32,2048]{1,0:T(8,128)(2,1)S(1)} %get-tuple-element.50.refs_0_), channel_id=1, source_target_pairs={{0,16},{4,20},{8,24},{12,28},{16,0},{20,4},{24,8},{28,12},{1,17},{... | collective-permute-start | bytes 393224 | tf_op jit(solution)/shard_map/ppermute | solution.py:649
  187.3 9.6 %collective-permute-start.19 = (bf16[32,2048]{1,0:T(8,128)(2,1)S(1)}, bf16[32,2048]{1,0:T(8,128)(2,1)S(1)}, u32[]{:S(2)}, u32[]{:S(2)}) collective-permute-start(bf16[32,2048]{1,0:T(8,128)(2,1)S(1)} %get-tuple-element.50.refs_0_), channel_id=1, source_target_pairs={{0,24},{4,28},{8,16},{12,20},{16,8},{20,12},{24,0},{28,4},{1,25},{... | collective-permute-start | bytes 393224 | tf_op jit(solution)/shard_map/ppermute | solution.py:649
  196.9 2.2 %copy-start.1 = (bf16[1024,2048]{1,0:T(8,128)(2,1)S(1)}, bf16[1024,2048]{1,0:T(8,128)(2,1)}, u32[]{:S(2)}) copy-start(bf16[1024,2048]{1,0:T(8,128)(2,1)} %refs_5_.1) | copy-start | bytes 12582916
  205.3 7.8 %collective-permute-start.28 = (bf16[32,2048]{1,0:T(8,128)(2,1)S(1)}, bf16[32,2048]{1,0:T(8,128)(2,1)S(1)}, u32[]{:S(2)}, u32[]{:S(2)}) collective-permute-start(bf16[32,2048]{1,0:T(8,128)(2,1)S(1)} %get-tuple-element.52), channel_id=1, source_target_pairs={{0,8},{4,12},{8,0},{12,4},{16,24},{20,28},{24,16},{28,20},{1,9},{5... | collective-permute-start | bytes 393224 | tf_op jit(solution)/shard_map/ppermute | solution.py:649
  207.3 10.5 %collective-permute-start.29 = (bf16[32,2048]{1,0:T(8,128)(2,1)S(1)}, bf16[32,2048]{1,0:T(8,128)(2,1)S(1)}, u32[]{:S(2)}, u32[]{:S(2)}) collective-permute-start(bf16[32,2048]{1,0:T(8,128)(2,1)S(1)} %get-tuple-element.53), channel_id=1, source_target_pairs={{0,16},{4,20},{8,24},{12,28},{16,0},{20,4},{24,8},{28,12},{1,17},{... | collective-permute-start | bytes 393224 | tf_op jit(solution)/shard_map/ppermute | solution.py:649
  207.5 10.3 %collective-permute-start.30 = (bf16[32,2048]{1,0:T(8,128)(2,1)S(1)}, bf16[32,2048]{1,0:T(8,128)(2,1)S(1)}, u32[]{:S(2)}, u32[]{:S(2)}) collective-permute-start(bf16[32,2048]{1,0:T(8,128)(2,1)S(1)} %get-tuple-element.54), channel_id=1, source_target_pairs={{0,24},{4,28},{8,16},{12,20},{16,8},{20,12},{24,0},{28,4},{1,25},{... | collective-permute-start | bytes 393224 | tf_op jit(solution)/shard_map/ppermute | solution.py:649

commit v4 on v3

--- a/solution.py
+++ b/solution.py
@@ -173,7 +173,6 @@
 
 FINE = 16
 MIB = 1 << 20
-BIG = 58 * MIB
 
 
 def rate_row(width):
@@ -181,12 +180,17 @@
     return jnp.exp(index * (-2.0 * math.log(10000.0) / width))
 
 
-def context_kernel(halves, ids_ref, coarse_ref, fine_ref, table_ref, out_ref, cos_ref, sin_ref):
-    @pl.when(pl.program_id(0) == 0)
+def context_kernel(
+    halves, first, ids_ref, sine_ref, cosine_ref, high_cos_ref, high_sin_ref, low_cos_ref,
+    low_sin_ref, table_ref, out_ref, cos_ref, sin_ref,
+):
+    tile = pl.program_id(0)
+
+    @pl.when(tile == 0)
     def _():
-        low_cos, low_sin = fine_ref[2], fine_ref[3]
+        low_cos, low_sin = low_cos_ref[...], low_sin_ref[...]
         for step in range(FINE):
-            high_cos, high_sin = fine_ref[0, step : step + 1, :], fine_ref[1, step : step + 1, :]
+            high_cos, high_sin = high_cos_ref[step : step + 1], high_sin_ref[step : step + 1]
             rows = pl.ds(step * FINE, FINE)
             cos_ref[rows, :] = high_cos * low_cos - high_sin * low_sin
             sin_ref[rows, :] = high_sin * low_cos + high_cos * low_sin
@@ -199,7 +203,8 @@
     looked = lax.dot_general(
         one_hot, table_ref[...], (((0,), (0,)), ((), ())), preferred_element_type=jnp.float32
     )
-    total = looked + coarse_ref[0, 0:1, :] * cos_ref[...] + coarse_ref[0, 1:2, :] * sin_ref[...]
+    start = pl.ds(first + tile, 1)
+    total = looked + sine_ref[start, :] * cos_ref[...] + cosine_ref[start, :] * sin_ref[...]
     power = jnp.mean(total * total, axis=1, keepdims=True)
     normed = (total * lax.rsqrt(power + EPSILON)).astype(jnp.bfloat16)
     part = width // (2 * halves)
@@ -213,30 +218,30 @@
 def sinusoid_tables(starts, width):
     rates = rate_row(width)
     odd = (jnp.arange(width, dtype=jnp.int32) % 2)[None, :] == 1
-    angles = starts.astype(jnp.float32)[:, None] * rates[None, :]
+    places = jnp.pad(starts, (0, -starts.shape[0] % FINE)).astype(jnp.float32)
+    angles = places[:, None] * rates[None, :]
     sines, cosines = jnp.sin(angles), jnp.cos(angles)
-    coarse = jnp.stack(
-        [jnp.where(odd, cosines, sines), jnp.where(odd, -sines, cosines)], axis=1
-    )
     steps = jnp.arange(FINE, dtype=jnp.float32)
     high = (steps * FINE)[:, None] * rates[None, :]
     low = steps[:, None] * rates[None, :]
-    fine = jnp.stack([jnp.cos(high), jnp.sin(high), jnp.cos(low), jnp.sin(low)])
-    return coarse, fine
-
-
-def context_rows(ids, coarse, fine, table, owners):
+    return (
+        jnp.where(odd, cosines, sines),
+        jnp.where(odd, -sines, cosines),
+        jnp.cos(high),
+        jnp.sin(high),
+        jnp.cos(low),
+        jnp.sin(low),
+    )
+
+
+def context_rows(ids, first, tables, table, owners):
     count, rows = ids.shape[0], FINE * FINE
     width = table.shape[1]
     return pl.pallas_call(
-        lambda *refs: context_kernel(owners, *refs),
+        lambda *refs: context_kernel(owners, first, *refs),
         grid=(count,),
-        in_specs=[
-            pl.BlockSpec((1, 1, rows), lambda i: (i, 0, 0)),
-            pl.BlockSpec((1, 2, width), lambda i: (i, 0, 0)),
-            pl.BlockSpec((4, FINE, width), lambda i: (0, 0, 0)),
-            pl.BlockSpec(table.shape, lambda i: (0, 0)),
-        ],
+        in_specs=[pl.BlockSpec((1, 1, rows), lambda i: (i, 0, 0))]
+        + [pl.BlockSpec(array.shape, lambda i: (0, 0)) for array in (*tables, table)],
         out_specs=pl.BlockSpec((rows, width), lambda i: (i, 0)),
         out_shape=jax.ShapeDtypeStruct((count * rows, width), jnp.bfloat16),
         scratch_shapes=[pltpu.VMEM((rows, width), jnp.float32)] * 2,
@@ -247,7 +252,7 @@
         ),
         compiler_params=pltpu.CompilerParams(vmem_limit_bytes=20 * MIB),
         name="context_rows",
-    )(ids[:, None, :], coarse, fine, table)
+    )(ids[:, None, :], *tables, table)
 
 
 def attention_kernel(key_tile, shifted, scalars_ref, query_ref, own_ref, other_ref, out_ref):
@@ -316,30 +321,55 @@
     )(scalars, triples, own, other)
 
 
-def prepare_kernel(core_ref, query_ref, pair_ref, mine_ref, theirs_ref):
+def in_hbm(array):
+    return pltpu.with_memory_space_constraint(array, pltpu.HBM)
+
+
+def prepare_kernel(
+    scalars_ref, query_hbm, pair_hbm, matrix_hbm, mine_ref, theirs_ref, part_ref, query_ref,
+    pair_ref, loaded,
+):
+    core, group = scalars_ref[0], scalars_ref[3]
     heads, half, columns = mine_ref.shape
     size = columns // 3
-    for target, core in ((mine_ref, core_ref[0]), (theirs_ref, 1 - core_ref[0])):
-        rows = pl.ds(pl.multiple_of(core * half, half), half)
+    depth = part_ref.shape[0]
+    quarter = matrix_hbm.at[pl.ds(pl.multiple_of(group * depth, depth), depth), :]
+    loads = [
+        pltpu.make_async_copy(query_hbm, query_ref, loaded.at[0]),
+        pltpu.make_async_copy(pair_hbm, pair_ref, loaded.at[1]),
+        pltpu.make_async_copy(quarter, part_ref, loaded.at[2]),
+    ]
+    for load in loads:
+        load.start()
+    loads[0].wait()
+    loads[1].wait()
+    for target, side in ((theirs_ref, 1 - core), (mine_ref, core)):
+        rows = pl.ds(pl.multiple_of(side * half, half), half)
         for head in range(heads):
             span = slice(head * size, (head + 1) * size)
             target[head, :, 0:size] = query_ref[rows, span]
             target[head, :, size : 2 * size] = pair_ref[0, rows, span]
             target[head, :, 2 * size :] = pair_ref[1, rows, span]
-
-
-def prepare_weights(core, cross_q, cross_kv):
+    loads[2].wait()
+
+
+def prepare_weights(scalars, cross_q, cross_kv, matrix, groups):
     share, columns = cross_q.shape
     shape = jax.ShapeDtypeStruct((columns // HD, share // 2, 3 * HD), jnp.bfloat16)
+    part = jax.ShapeDtypeStruct((matrix.shape[0] // groups, matrix.shape[1]), jnp.bfloat16)
     return pl.pallas_call(
         prepare_kernel,
-        in_specs=[pl.BlockSpec(memory_space=pltpu.SMEM)]
-        + [pl.BlockSpec(memory_space=pltpu.VMEM)] * 2,
-        out_specs=[pl.BlockSpec(memory_space=pltpu.VMEM)] * 2,
-        out_shape=[shape, shape],
-        compiler_params=pltpu.CompilerParams(vmem_limit_bytes=4 * MIB),
+        in_specs=[IN_SMEM] + [ANYWHERE] * 3,
+        out_specs=[IN_VMEM] * 3,
+        out_shape=[shape, shape, part],
+        scratch_shapes=[
+            pltpu.VMEM(cross_q.shape, jnp.bfloat16),
+            pltpu.VMEM(cross_kv.shape, jnp.bfloat16),
+            pltpu.SemaphoreType.DMA((3,)),
+        ],
+        compiler_params=pltpu.CompilerParams(vmem_limit_bytes=8 * MIB),
         name="prepare_weights",
-    )(core, cross_q, cross_kv)
+    )(scalars, in_hbm(cross_q), in_hbm(cross_kv), in_hbm(matrix))
 
 
 def project_kernel(scalars_ref, heads_ref, mine_ref, theirs_ref, kept_ref, given_ref):
@@ -425,9 +455,9 @@
             bytes_accessed=4 * kinds * inner * columns,
             transcendentals=0,
         ),
-        compiler_params=pltpu.CompilerParams(vmem_limit_bytes=BIG),
+        compiler_params=pltpu.CompilerParams(vmem_limit_bytes=20 * MIB),
         name="triple_heads",
-    )(scalars, own, other, mine, theirs)
+    )(scalars, own, other, in_hbm(mine), in_hbm(theirs))
 
 
 def add_norm_kernel(base_ref, kept_ref, came_ref, stream_ref, normed_ref):
@@ -540,15 +570,15 @@
     )(scalars, mine, theirs)
 
 
-def gather_kernel(scalars_ref, *refs):
+def gather_kernel(step, scalars_ref, *refs):
     *block_refs, out_ref = refs
     for distance, block_ref in enumerate(block_refs):
-        out_ref[scalars_ref[2] ^ distance] = block_ref[...]
-
-
-def gather_blocks(scalars, blocks):
-    return pl.pallas_call(
-        gather_kernel,
+        out_ref[lax.div(scalars_ref[2], step) ^ distance] = block_ref[...]
+
+
+def gather_blocks(scalars, blocks, step):
+    return pl.pallas_call(
+        lambda *refs: gather_kernel(step, *refs),
         in_specs=[IN_SMEM] + [IN_VMEM] * len(blocks),
         out_specs=IN_VMEM,
         out_shape=jax.ShapeDtypeStruct((len(blocks), *blocks[0].shape), blocks[0].dtype),
@@ -559,9 +589,11 @@
 
 def mlp_kernel(scalars_ref, *refs):
     group = scalars_ref[3]
-    *refs, hidden_ref = refs
+    *refs, hidden_ref, out_ref, loaded = refs
     count = (len(refs) - 10) // 2
-    blocks, (in_ref, out_ref), rest = refs[:count], refs[count : count + 2], refs[count + 2 :]
+    blocks, (in_ref, out_hbm), rest = refs[:count], refs[count : count + 2], refs[count + 2 :]
+    load = pltpu.make_async_copy(out_hbm, out_ref, loaded)
+    load.start()
     in_parts, out_parts, shares = rest[:4], rest[4:8], rest[8:]
     rows = jnp.concatenate([block[...] for block in blocks])
     depth, units = in_parts[0].shape[0], out_parts[0].shape[0]
@@ -569,8 +601,7 @@
     def hidden_of(total):
         return jax.nn.gelu(total, approximate=True).astype(jnp.bfloat16)
 
-    total = jnp.dot(rows, in_ref[...], preferred_element_type=jnp.float32)
-    share = jnp.dot(hidden_of(total), out_ref[...], preferred_element_type=jnp.float32)
+    hidden = hidden_of(jnp.dot(rows, in_ref[...], preferred_element_type=jnp.float32))
     quarters = [group, group ^ 2, group ^ 1, group ^ 3]
     total = 0.0
     for quarter, part in zip(quarters, in_parts):
@@ -578,6 +609,8 @@
         piece = jnp.concatenate([block[:, span] for block in blocks])
         total += jnp.dot(piece, part[...], preferred_element_type=jnp.float32)
     hidden_ref[...] = hidden_of(total)
+    load.wait()
+    share = jnp.dot(hidden, out_ref[...], preferred_element_type=jnp.float32)
     for quarter, part in zip(quarters, out_parts):
         span = pl.ds(pl.multiple_of(quarter * units, units), units)
         share += jnp.dot(hidden_ref[:, span], part[...], preferred_element_type=jnp.float32)
@@ -589,21 +622,26 @@
 def mlp_shares(scalars, blocks, mlp_in, mlp_out, in_parts, out_parts):
     first = jax.ShapeDtypeStruct(blocks[0].shape, jnp.float32)
     other = jax.ShapeDtypeStruct(blocks[0].shape, jnp.bfloat16)
-    operands = [*blocks, mlp_in, mlp_out, *in_parts, *out_parts]
+    operands = [*blocks, mlp_in, in_hbm(mlp_out), *in_parts, *out_parts]
     return pl.pallas_call(
         mlp_kernel,
-        in_specs=[IN_SMEM] + [IN_VMEM] * len(operands),
+        in_specs=[IN_SMEM]
+        + [IN_VMEM] * (len(blocks) + 1)
+        + [ANYWHERE]
+        + [IN_VMEM] * (len(operands) - len(blocks) - 2),
         out_specs=[IN_VMEM] * len(blocks),
         out_shape=[first] + [other] * (len(blocks) - 1),
         scratch_shapes=[
-            pltpu.VMEM((len(blocks) * blocks[0].shape[0], mlp_in.shape[1]), jnp.bfloat16)
+            pltpu.VMEM((len(blocks) * blocks[0].shape[0], mlp_in.shape[1]), jnp.bfloat16),
+            pltpu.VMEM(mlp_out.shape, jnp.bfloat16),
+            pltpu.SemaphoreType.DMA(()),
         ],
         cost_estimate=pl.CostEstimate(
             flops=8 * len(blocks) * blocks[0].size * mlp_in.shape[1],
             bytes_accessed=8 * mlp_in.size,
             transcendentals=0,
         ),
-        compiler_params=pltpu.CompilerParams(vmem_limit_bytes=12 * MIB),
+        compiler_params=pltpu.CompilerParams(vmem_limit_bytes=16 * MIB),
         name="mlp_shares",
     )(scalars, *operands)
 
@@ -645,6 +683,8 @@
     def exchange(value):
         return lax.all_to_all(value, "ctx", 0, 0, tiled=True)
 
+    distances = [2 * i for i in range(1, owners // 2)]
+
     def across(value, distance):
         return lax.ppermute(value, "ctx", [(i, i ^ distance) for i in range(owners)])
 
@@ -652,11 +692,19 @@
         size = matrix.shape[0] // groups
         return lax.dynamic_slice_in_dim(matrix, group * size, size, 0)
 
-    mine, theirs = prepare_weights(scalars, cross_q, cross_kv)
+    mine, theirs, in_part = prepare_weights(scalars, cross_q, cross_kv, mlp_in, groups)
     blocks = order_blocks(scalars, mine, swap(theirs))
 
     lanes = token_ids.reshape(1, block // HD, HD)
-    every_token = exchange(jnp.broadcast_to(lanes, (owners, block // HD, HD)))
+    lanes_other = across(lanes, 1)
+    even = place % 2 == 0
+    lanes = jnp.concatenate(
+        [jnp.where(even, lanes, lanes_other), jnp.where(even, lanes_other, lanes)]
+    )
+    pair_lanes = [lanes]
+    for distance in distances:
+        pair_lanes.append(across(lanes, distance))
+    every_token = gather_blocks(scalars, pair_lanes, 2).reshape(owners, block)
     arrived = [blocks[0]]
     for distance in range(1, owners):
         arrived.append(across(blocks[distance], distance))
@@ -677,8 +725,8 @@
         ]
     )
     fetched = []
-    for matrix in (mlp_in, mlp_out):
-        one = across(quarter(matrix), 1)
+    for part in (in_part, None):
+        one = across(quarter(mlp_out) if part is None else part, 1)
         two = cross(one)
         three = swap(one)
         four = swap(two)
@@ -693,11 +741,11 @@
             (offset + latent_starts[:, None] + latent_inner[None, :]).reshape(-1),
         ]
     )
-    coarse, fine = sinusoid_tables(starts, width)
+    tables = sinusoid_tables(starts, width)
     tiles = half_blocks * pieces
-    context = context_rows(own_ids.reshape(-1, step), coarse[:tiles], fine, embed_table, owners)
-    latent = context_rows(latent_ids.reshape(-1, step), coarse[tiles:], fine, embed_table, owners)
-    arrived = gather_blocks(scalars, arrived)
+    context = context_rows(own_ids.reshape(-1, step), 0, tables, embed_table, owners)
+    latent = context_rows(latent_ids.reshape(-1, step), tiles, tables, embed_table, owners)
+    arrived = gather_blocks(scalars, arrived, 1)
     arrived_other = swap(arrived)
     pairs, queries, own_latent = context_heads(
         scalars, context, latent, arrived, arrived_other, (owners, duos, rows)
@@ -711,7 +759,8 @@
     def project(base, attended, mine, theirs):
         heads = exchange(attended.reshape(owners, duo_rows, HD))
         kept, given = project_rows(scalars, heads, mine, theirs)
-        return add_norm(base, kept, cross(given))
+        came = cross(given)
+        return add_norm(base, kept, came)
 
     first_stream, normed = project(own_latent, attended, cross_out, swap(cross_out))
     normed_other = cross(normed)
@@ -725,12 +774,14 @@
         first_stream, self_attended, self_out, swap(self_out)
     )
 
-    distances = [2 * i for i in range(1, owners // 2)]
-    blocks = [mlp_normed] + [across(mlp_normed, distance) for distance in distances]
+    blocks = [mlp_normed]
+    for distance in distances:
+        blocks.append(across(mlp_normed, distance))
     kept, *given = mlp_shares(scalars, blocks, mlp_in, mlp_out, *fetched)
     result = second_stream + kept
     for share, distance in zip(given, distances):
-        result = result + across(share, distance).astype(jnp.float32)
+        came = across(share, distance)
+        result = result + came.astype(jnp.float32)
     return result.astype(jnp.bfloat16)[None]
 
 

time: 219 us -> 218 us (level)
  waiting for transfers between devices: 101 us -> 109 us
  local copies, waits for them, and re-layouts: 11.1 us -> 3.96 us
  starting transfers between devices: 58.3 us -> 54 us
  Pallas kernels: 42.4 us -> 46.6 us
  other arithmetic: 4.62 us -> 2.37 us
    all_to_all x4 -> x3, starting transfers between devices: 24.1 us -> 10.8 us  [exchange(): return lax.all_to_all(value, 'ctx', 0, 0, tiled=True)]
    ppermute x15 -> x19, starting transfers between devices: 25 us -> 34.2 us  [across(): lax.ppermute(value, 'ctx', [(i, i ^ distance) for i in range(owners)])]
    pallas_call x5 -> x6, Pallas kernels: 17.3 us -> 21.8 us  [the longest x2 9.94 us: context_rows(): pl.pallas_call(lambda *refs: context_kernel(owners, first, *refs), grid=(...]
    ppermute x5, waiting for transfers between devices: 30.4 us -> 34.4 us  [cross(): return lax.ppermute(value, 'lat', [(i, i ^ 2) for i in range(groups)])]
    unnamed x24 -> x14, local copies, waits for them, and re-layouts: 4.86 us -> 1.37 us
    ppermute x11, waiting for transfers between devices: 0.03 us -> 3.37 us  [swap(): return lax.ppermute(value, 'lat', [(i, i ^ 1) for i in range(groups)])]
    select_n x1, other arithmetic: 2.54 us -> 0.01 us  [paired_device(): jnp.where(even, lanes, lanes_other)]
    dynamic_slice x2 -> x1, local copies, waits for them, and re-layouts: 4.65 us -> 2.29 us  [quarter(): return lax.dynamic_slice_in_dim(matrix, group * size, size, 0)]
  transfers between devices with their start and end apart: 35 -> 38, of which waited for: 12 -> 16; matrix products, arithmetic and copies ran while one was open for 5% -> 2% of each run, Pallas kernels for 17% -> 18%
where the time goes in v4:
time: 218 us; the launch traced here: 217 us
  waiting for transfers between devices  109 us (50%)
  starting transfers between devices  54 us (25%)
  Pallas kernels  46.6 us (21%)
  local copies, waits for them, and re-layouts  3.96 us (2%)
  other arithmetic  2.37 us (1%)
    all_to_all x3, waiting for transfers between devices, exchange(): return lax.all_to_all(value, 'ctx', 0, 0, tiled=True)  50.6 us
    ppermute x5, waiting for transfers between devices, cross(): return lax.ppermute(value, 'lat', [(i, i ^ 2) for i in range(groups)])  34.4 us
    ppermute x19, starting transfers between devices, across(): lax.ppermute(value, 'ctx', [(i, i ^ distance) for i in range(owners)])  34.2 us
    ppermute x19, waiting for transfers between devices, across(): lax.ppermute(value, 'ctx', [(i, i ^ distance) for i in range(owners)])  20.8 us
    all_to_all x3, starting transfers between devices, exchange(): return lax.all_to_all(value, 'ctx', 0, 0, tiled=True)  10.8 us
    pallas_call x2, Pallas kernels, context_rows(): pl.pallas_call(lambda *refs: context_kernel(owners, first, *refs), grid=(...  9.94 us
    pallas_call x2, Pallas kernels, head_attention(): pl.pallas_call(lambda *refs: attention_kernel(key_tile, shifted, *refs),...  8.07 us
    pallas_call x1, Pallas kernels, mlp_shares(): pl.pallas_call(mlp_kernel, in_specs=[IN_SMEM] + [IN_VMEM] * (len(blocks)...  7.66 us
  transfers between devices with their start and end apart: 38, of which 16 were waited for; matrix products, arithmetic and copies ran while one was open for 2% of the time, Pallas kernels for 18%

profile of v4, /device:TPU:0, one launch (start us, length us, event | category | flops | bytes accessed | tf_op | source)
XLA Modules:
  0.0 217.1 jit_solution(7540759196342048659)
XLA Ops:
  0.0 0.5 collective-permute-start.17
  1.3 3.0 %prepare_weights.1 = (bf16[4,128,384]{2,1,0:T(8,128)(2,1)S(1)}, bf16[4,128,384]{2,1,0:T(8,128)(2,1)S(1)}, bf16[512,1024]{1,0:T(8,128)(2,1)}) custom-call(s32[5]{0:T(128)S(1)} %stack.28.refs_0_.scalars_ref, bf16[256,512]{1,0:T(8,128)(2,1)} %query_hbm.1, bf16[2,256,512]{2,1,0:T(8,128)(2,1)} %pair_hbm.1, bf16[2048,1024]{1,0:T(8,128)(2,1)} %refs_4_.1), custom_call_target="tpu_custom_call" | custom-call | tf_op jit(solution)/shard_map/prepare_weights/pallas_call | solution.py:360
  4.4 3.0 %collective-permute-start = (s32[1,4,128]{2,1,0:T(4,128)S(1)}, s32[1,4,128]{2,1,0:T(4,128)S(1)}, u32[]{:S(2)}, u32[]{:S(2)}) collective-permute-start(s32[1,4,128]{2,1,0:T(4,128)S(1)} %bitcast.30), channel_id=1, source_target_pairs={{0,4},{4,0},{8,12},{12,8},{16,20},{20,16},{24,28},{28,24},{1,5},{5... | collective-permute-start | bytes 6152 | tf_op jit(solution)/shard_map/ppermute | solution.py:689
  7.7 3.3 %collective-permute-done.4.theirs_ref = bf16[4,128,384]{2,1,0:T(8,128)(2,1)S(1)} collective-permute-done((bf16[4,128,384]{2,1,0:T(8,128)(2,1)S(1)}, bf16[4,128,384]{2,1,0:T(8,128)(2,1)S(1)}, u32[]{:S(2)}, u32[]{:S(2)}) %collective-permute-start.4) | collective-permute-done | bytes 393248 | tf_op jit(solution)/shard_map/ppermute | solution.py:678
  11.1 0.7 order_blocks.1
  11.8 5.0 %collective-permute-start.10 = (bf16[128,384]{1,0:T(8,128)(2,1)S(1)}, bf16[128,384]{1,0:T(8,128)(2,1)S(1)}, u32[]{:S(2)}, u32[]{:S(2)}) collective-permute-start(bf16[128,384]{1,0:T(8,128)(2,1)S(1)} %get-tuple-element.39), channel_id=1, source_target_pairs={{0,24},{4,28},{8,16},{12,20},{16,8},{20,12},{24,0},{28,4},{1,25},{... | collective-permute-start | bytes 294920 | tf_op jit(solution)/shard_map/ppermute | solution.py:689
  16.8 1.1 collective-permute-start.11
  17.9 0.4 collective-permute-start.5
  18.3 1.7 collective-permute-done.10.refs_7_
  20.0 5.5 %collective-permute-start.7 = (bf16[128,384]{1,0:T(8,128)(2,1)S(1)}, bf16[128,384]{1,0:T(8,128)(2,1)S(1)}, u32[]{:S(2)}, u32[]{:S(2)}) collective-permute-start(bf16[128,384]{1,0:T(8,128)(2,1)S(1)} %get-tuple-element.36), channel_id=1, source_target_pairs={{0,12},{4,8},{8,4},{12,0},{16,28},{20,24},{24,20},{28,16},{1,13},{... | collective-permute-start | bytes 294920 | tf_op jit(solution)/shard_map/ppermute | solution.py:689
  25.5 3.0 %collective-permute-start.8 = (bf16[128,384]{1,0:T(8,128)(2,1)S(1)}, bf16[128,384]{1,0:T(8,128)(2,1)S(1)}, u32[]{:S(2)}, u32[]{:S(2)}) collective-permute-start(bf16[128,384]{1,0:T(8,128)(2,1)S(1)} %get-tuple-element.37), channel_id=1, source_target_pairs={{0,16},{4,20},{8,24},{12,28},{16,0},{20,4},{24,8},{28,12},{1,17},{... | collective-permute-start | bytes 294920 | tf_op jit(solution)/shard_map/ppermute | solution.py:689
  28.5 0.5 collective-permute-start.9
  29.0 0.8 collective-permute-start.1
  29.8 2.0 collective-permute-start.2
  31.9 3.8 %collective-permute-done.8.refs_5_ = bf16[128,384]{1,0:T(8,128)(2,1)S(1)} collective-permute-done((bf16[128,384]{1,0:T(8,128)(2,1)S(1)}, bf16[128,384]{1,0:T(8,128)(2,1)S(1)}, u32[]{:S(2)}, u32[]{:S(2)}) %collective-permute-start.8) | collective-permute-done | bytes 98336 | tf_op jit(solution)/shard_map/ppermute | solution.py:689
  35.6 1.9 collective-permute-start.3
  37.6 0.6 gather_blocks.3.refs_3_
  38.3 1.4 fusion.4
  39.7 0.6 collective-permute-start.14
  40.3 0.8 collective-permute-done.3.refs_4_
  41.0 0.5 gather_blocks.2
  41.7 2.4 %context_rows.3.refs_2_ = bf16[512,2048]{1,0:T(8,128)(2,1)S(1)} custom-call(s32[2,1,256]{2,1,0:T(1,128)S(1)} %broadcast_in_dim.30.refs_0_, f32[16,2048]{1,0:T(8,128)S(1)} %get-tuple-element.67.refs_1_, f32[16,2048]{1,0:T(8,128)S(1)} %get-tuple-element.68.refs_2_, f32[16,2048]{1,0:T(8,128)S(1)} %get-tuple-element.65.refs_3_, ...), custom_call_target="tpu_custom_call" | custom-call | flops 536870912 | bytes 2097152 | tf_op jit(solution)/shard_map/context_rows/pallas_call | solution.py:240
  44.1 7.6 %context_rows.2.refs_1_ = bf16[2048,2048]{1,0:T(8,128)(2,1)S(1)} custom-call(s32[8,1,256]{2,1,0:T(1,128)S(1)} %bitcast.27, f32[16,2048]{1,0:T(8,128)S(1)} %get-tuple-element.67.refs_1_, f32[16,2048]{1,0:T(8,128)S(1)} %get-tuple-element.68.refs_2_, f32[16,2048]{1,0:T(8,128)S(1)} %get-tuple-element.65.refs_3_, f32[16,2048]{1,0:T(8,128)S(1)} %get-tuple-element.66.refs_4_, ...), custom_call_target="tpu_custom_call" | custom-call | flops 2147483648 | bytes 8388608 | tf_op jit(solution)/shard_map/context_rows/pallas_call | solution.py:240
  51.7 4.1 %context_heads.1 = (bf16[2048,256]{1,0:T(8,128)(2,1)}, bf16[8,2,32,128]{3,2,1,0:T(8,128)(2,1)S(1)}, bf16[32,2048]{1,0:T(8,128)(2,1)S(1)}) custom-call(s32[5]{0:T(128)S(1)} %stack.28.refs_0_.scalars_ref, bf16[2048,2048]{1,0:T(8,128)(2,1)S(1)} %context_rows.2.refs_1_, bf16[512,2048]{1,0:T(8,128)(2,1)S(1)} %context_rows.3.refs_2_, ...), custom_call_target="tpu_custom_call" | custom-call | flops 2684354560 | bytes 8388608 | tf_op jit(solution)/shard_map/context_heads/pallas_call | solution.py:524
  55.8 0.2 collective-permute-start.24
  56.0 2.3 %constant_dynamic-slice_fusion = bf16[256,2048]{1,0:T(8,128)(2,1)} fusion(bf16[1024,2048]{1,0:T(8,128)(2,1)} %refs_5_.1, s32[]{:T(128)S(6)} %select_n.97), kind=kLoop, calls=%fused_computation.37 | loop fusion | bytes 2097156 | tf_op jit(solution)/shard_map/dynamic_slice | solution.py:693
  58.3 1.8 collective-permute-start.28
  60.1 6.2 %head_attention.2 = bf16[8,2,32,128]{3,2,1,0:T(8,128)(2,1)} custom-call(s32[5]{0:T(128)S(1)} %stack.28.refs_0_.scalars_ref, bf16[8,2,32,128]{3,2,1,0:T(8,128)(2,1)S(1)} %get-tuple-element.42.refs_1_, bf16[1,4,512,256]{3,2,1,0:T(8,128)(2,1)} %bitcast.9.refs_2_, bf16[1,4,512,256]{3,2,1,0:T(8,128)(2,1)} %bitcast.10.refs_3_), custom_call_target="tpu_custom_call" | custom-call | flops 2147483648 | bytes 2097152 | tf_op jit(solution)/shard_map/head_attention/pallas_call | solution.py:301
  66.2 3.6 %all-to-all-start = ((bf16[8,64,128]{2,1,0:T(8,128)(2,1)}), bf16[8,64,128]{2,1,0:T(8,128)(2,1)S(1)}, u32[]{:S(2)}, u32[]{:S(2)}) async-start(bf16[8,64,128]{2,1,0:T(8,128)(2,1)} %bitcast.11), calls=%async_computation | async-start | bytes 262144 | tf_op jit(solution)/shard_map/all_to_all | solution.py:684
  69.8 35.6 %all-to-all-done.heads_ref = bf16[8,64,128]{2,1,0:T(8,128)(2,1)S(1)} async-done(((bf16[8,64,128]{2,1,0:T(8,128)(2,1)}), bf16[8,64,128]{2,1,0:T(8,128)(2,1)S(1)}, u32[]{:S(2)}, u32[]{:S(2)}) %all-to-all-start) | async-done | bytes 131104 | tf_op jit(solution)/shard_map/all_to_all | solution.py:684
  105.4 2.4 %project_rows.2 = (f32[32,2048]{1,0:T(8,128)S(1)}, bf16[32,2048]{1,0:T(8,128)(2,1)S(1)}) custom-call(s32[5]{0:T(128)S(1)} %stack.28.refs_0_.scalars_ref, bf16[8,64,128]{2,1,0:T(8,128)(2,1)S(1)} %all-to-all-done.heads_ref, bf16[512,2048]{1,0:T(8,128)(2,1)S(1)} %copy-done.2, bf16[512,2048]{1,0:T(8,128)(2,1)} %collective-permute-done.14.theirs_ref), custom_call_target="tpu_custom_call" | custom-call | flops 268435456 | bytes 4194304 | tf_op jit(solution)/shard_map/project_rows/pallas_call | solution.py:396
  107.9 1.6 collective-permute-start.15
  109.5 3.6 %collective-permute-done.15.came_ref = bf16[32,2048]{1,0:T(8,128)(2,1)S(1)} collective-permute-done((bf16[32,2048]{1,0:T(8,128)(2,1)S(1)}, bf16[32,2048]{1,0:T(8,128)(2,1)S(1)}, u32[]{:S(2)}, u32[]{:S(2)}) %collective-permute-start.15) | collective-permute-done | bytes 131104 | tf_op jit(solution)/shard_map/ppermute | solution.py:681
  113.1 0.1 add_norm.2
  113.3 0.7 copy-done.3
  114.0 1.5 collective-permute-start.16
  115.5 0.5 collective-permute-start.25
  116.0 4.3 %collective-permute-done.16.refs_2_ = bf16[32,2048]{1,0:T(8,128)(2,1)S(1)} collective-permute-done((bf16[32,2048]{1,0:T(8,128)(2,1)S(1)}, bf16[32,2048]{1,0:T(8,128)(2,1)S(1)}, u32[]{:S(2)}, u32[]{:S(2)}) %collective-permute-start.16) | collective-permute-done | bytes 131104 | tf_op jit(solution)/shard_map/ppermute | solution.py:681
  120.3 6.7 %triple_heads.1 = bf16[8,64,384]{2,1,0:T(8,128)(2,1)} custom-call(s32[5]{0:T(128)S(1)} %stack.28.refs_0_.scalars_ref, bf16[32,2048]{1,0:T(8,128)(2,1)S(1)} %get-tuple-element.47.refs_1_, bf16[32,2048]{1,0:T(8,128)(2,1)S(1)} %collective-permute-done.16.refs_2_, bf16[3,2048,512]{2,1,0:T(8,128)(2,1)} %refs_3_.1, ...), custom_call_target="tpu_custom_call" | custom-call | flops 805306368 | bytes 12582912 | tf_op jit(solution)/shard_map/triple_heads/pallas_call | solution.py:444
  127.1 3.6 %all-to-all-start.1 = ((bf16[8,64,384]{2,1,0:T(8,128)(2,1)}), bf16[8,64,384]{2,1,0:T(8,128)(2,1)S(1)}, u32[]{:S(2)}, u32[]{:S(2)}) async-start(bf16[8,64,384]{2,1,0:T(8,128)(2,1)} %triple_heads.1), calls=%async_computation.1 | async-start | bytes 786432 | tf_op jit(solution)/shard_map/all_to_all | solution.py:684
  130.6 1.6 collective-permute-start.29
  132.2 7.6 %all-to-all-done.1 = bf16[8,64,384]{2,1,0:T(8,128)(2,1)S(1)} async-done(((bf16[8,64,384]{2,1,0:T(8,128)(2,1)}), bf16[8,64,384]{2,1,0:T(8,128)(2,1)S(1)}, u32[]{:S(2)}, u32[]{:S(2)}) %all-to-all-start.1) | async-done | bytes 393248 | tf_op jit(solution)/shard_map/all_to_all | solution.py:684
  139.8 0.5 collective-permute-start.26
  140.3 2.6 %collective-permute-done.25.refs_7_ = bf16[512,1024]{1,0:T(8,128)(2,1)} collective-permute-done((bf16[512,1024]{1,0:T(8,128)(2,1)S(1)}, bf16[512,1024]{1,0:T(8,128)(2,1)}, u32[]{:S(2)}, u32[]{:S(2)}) %collective-permute-start.25) | collective-permute-done | bytes 1048608 | tf_op jit(solution)/shard_map/ppermute | solution.py:681
  142.9 20.4 %collective-permute-done.29.refs_11_ = bf16[256,2048]{1,0:T(8,128)(2,1)} collective-permute-done((bf16[256,2048]{1,0:T(8,128)(2,1)}, bf16[256,2048]{1,0:T(8,128)(2,1)}, u32[]{:S(2)}, u32[]{:S(2)}) %collective-permute-start.29) | collective-permute-done | bytes 1048608 | tf_op jit(solution)/shard_map/ppermute | solution.py:681
  163.3 0.5 collective-permute-start.31
  163.8 1.9 head_attention.3
  165.8 0.6 copy-done.5
  166.4 3.7 %all-to-all-start.2 = ((bf16[8,64,128]{2,1,0:T(8,128)(2,1)}), bf16[8,64,128]{2,1,0:T(8,128)(2,1)S(1)}, u32[]{:S(2)}, u32[]{:S(2)}) async-start(bf16[8,64,128]{2,1,0:T(8,128)(2,1)} %bitcast.25), calls=%async_computation.2 | async-start | bytes 262144 | tf_op jit(solution)/shard_map/all_to_all | solution.py:684
  170.1 7.3 %all-to-all-done.2.heads_ref = bf16[8,64,128]{2,1,0:T(8,128)(2,1)S(1)} async-done(((bf16[8,64,128]{2,1,0:T(8,128)(2,1)}), bf16[8,64,128]{2,1,0:T(8,128)(2,1)S(1)}, u32[]{:S(2)}, u32[]{:S(2)}) %all-to-all-start.2) | async-done | bytes 131104 | tf_op jit(solution)/shard_map/all_to_all | solution.py:684
  177.4 2.6 %project_rows.3 = (f32[32,2048]{1,0:T(8,128)S(1)}, bf16[32,2048]{1,0:T(8,128)(2,1)S(1)}) custom-call(s32[5]{0:T(128)S(1)} %stack.28.refs_0_.scalars_ref, bf16[8,64,128]{2,1,0:T(8,128)(2,1)S(1)} %all-to-all-done.2.heads_ref, bf16[512,2048]{1,0:T(8,128)(2,1)} %mine_ref.3, bf16[512,2048]{1,0:T(8,128)(2,1)S(1)} %collective-permute-done.19.theirs_ref), custom_call_target="tpu_custom_call" | custom-call | flops 268435456 | bytes 4194304 | tf_op jit(solution)/shard_map/project_rows/pallas_call | solution.py:396
  180.0 1.6 collective-permute-start.20
  181.6 3.4 %collective-permute-done.20.came_ref = bf16[32,2048]{1,0:T(8,128)(2,1)S(1)} collective-permute-done((bf16[32,2048]{1,0:T(8,128)(2,1)S(1)}, bf16[32,2048]{1,0:T(8,128)(2,1)S(1)}, u32[]{:S(2)}, u32[]{:S(2)}) %collective-permute-start.20) | collective-permute-done | bytes 131104 | tf_op jit(solution)/shard_map/ppermute | solution.py:681
  185.1 0.1 add_norm.3
  185.3 1.3 collective-permute-start.22
  186.6 3.1 %collective-permute-start.23 = (bf16[32,2048]{1,0:T(8,128)(2,1)S(1)}, bf16[32,2048]{1,0:T(8,128)(2,1)S(1)}, u32[]{:S(2)}, u32[]{:S(2)}) collective-permute-start(bf16[32,2048]{1,0:T(8,128)(2,1)S(1)} %get-tuple-element.51.refs_0_), channel_id=1, source_target_pairs={{0,24},{4,28},{8,16},{12,20},{16,8},{20,12},{24,0},{28,4},{1,25},{... | collective-permute-start | bytes 393224 | tf_op jit(solution)/shard_map/ppermute | solution.py:689
  189.7 2.6 %collective-permute-done.21.refs_1_ = bf16[32,2048]{1,0:T(8,128)(2,1)S(1)} collective-permute-done((bf16[32,2048]{1,0:T(8,128)(2,1)S(1)}, bf16[32,2048]{1,0:T(8,128)(2,1)S(1)}, u32[]{:S(2)}, u32[]{:S(2)}) %collective-permute-start.21) | collective-permute-done | bytes 131104 | tf_op jit(solution)/shard_map/ppermute | solution.py:689
  192.3 3.9 %collective-permute-done.22.refs_2_ = bf16[32,2048]{1,0:T(8,128)(2,1)S(1)} collective-permute-done((bf16[32,2048]{1,0:T(8,128)(2,1)S(1)}, bf16[32,2048]{1,0:T(8,128)(2,1)S(1)}, u32[]{:S(2)}, u32[]{:S(2)}) %collective-permute-start.22) | collective-permute-done | bytes 131104 | tf_op jit(solution)/shard_map/ppermute | solution.py:689
  196.2 7.7 %mlp_shares.1 = (f32[32,2048]{1,0:T(8,128)S(1)}, bf16[32,2048]{1,0:T(8,128)(2,1)S(1)}, bf16[32,2048]{1,0:T(8,128)(2,1)S(1)}, bf16[32,2048]{1,0:T(8,128)(2,1)S(1)}) custom-call(s32[5]{0:T(128)S(1)} %stack.28.refs_0_.scalars_ref, bf16[32,2048]{1,0:T(8,128)(2,1)S(1)} %get-tuple-element.51.refs_0_, bf16[32,2048]{1,0:T(8,128)(2,1)S(1)} %collective-permute-done.21.refs_1_, ...), custom_call_target="tpu_custom_call" | custom-call | flops 2147483648 | bytes 16777216 | tf_op jit(solution)/shard_map/mlp_shares/pallas_call | solution.py:626
  203.9 2.0 collective-permute-start.32
  206.0 2.3 %collective-permute-start.34 = (bf16[32,2048]{1,0:T(8,128)(2,1)S(1)}, bf16[32,2048]{1,0:T(8,128)(2,1)S(1)}, u32[]{:S(2)}, u32[]{:S(2)}) collective-permute-start(bf16[32,2048]{1,0:T(8,128)(2,1)S(1)} %get-tuple-element.56), channel_id=1, source_target_pairs={{0,24},{4,28},{8,16},{12,20},{16,8},{20,12},{24,0},{28,4},{1,25},{... | collective-permute-start | bytes 393224 | tf_op jit(solution)/shard_map/ppermute | solution.py:689
  208.4 3.3 %collective-permute-done.32 = bf16[32,2048]{1,0:T(8,128)(2,1)S(1)} collective-permute-done((bf16[32,2048]{1,0:T(8,128)(2,1)S(1)}, bf16[32,2048]{1,0:T(8,128)(2,1)S(1)}, u32[]{:S(2)}, u32[]{:S(2)}) %collective-permute-start.32) | collective-permute-done | bytes 131104 | tf_op jit(solution)/shard_map/ppermute | solution.py:689
  211.7 4.7 %collective-permute-done.33 = bf16[32,2048]{1,0:T(8,128)(2,1)S(1)} collective-permute-done((bf16[32,2048]{1,0:T(8,128)(2,1)S(1)}, bf16[32,2048]{1,0:T(8,128)(2,1)S(1)}, u32[]{:S(2)}, u32[]{:S(2)}) %collective-permute-start.33) | collective-permute-done | bytes 131104 | tf_op jit(solution)/shard_map/ppermute | solution.py:689
  216.4 0.7 fusion.3
  (62 shorter events, 1.0 us)
Async XLA Ops:
  0.0 4.4 %copy-start.6 = (s32[512]{0:T(512)S(1)}, s32[512]{0:T(512)}, u32[]{:S(2)}) copy-start(s32[512]{0:T(512)} %param.10) | copy-start | bytes 6148
  0.0 120.3 %collective-permute-start.17 = (bf16[3,2048,512]{2,1,0:T(8,128)(2,1)}, bf16[3,2048,512]{2,1,0:T(8,128)(2,1)}, u32[]{:S(2)}, u32[]{:S(2)}) collective-permute-start(bf16[3,2048,512]{2,1,0:T(8,128)(2,1)} %refs_3_.1), channel_id=1, source_target_pairs={{0,1},{1,0},{2,3},{3,2},{4,5},{5,4},{6,7},{7,6},{8,9},{9,8},{10,11... | collective-permute-start | bytes 18874376 | tf_op jit(solution)/shard_map/ppermute | solution.py:678
  0.5 41.2 %copy-start.1 = (bf16[256,2048]{1,0:T(8,128)(2,1)S(1)}, bf16[256,2048]{1,0:T(8,128)(2,1)}, u32[]{:S(2)}) copy-start(bf16[256,2048]{1,0:T(8,128)(2,1)} %refs_7_.3) | copy-start | bytes 3145732
  4.4 6.7 %collective-permute-start.4 = (bf16[4,128,384]{2,1,0:T(8,128)(2,1)S(1)}, bf16[4,128,384]{2,1,0:T(8,128)(2,1)S(1)}, u32[]{:S(2)}, u32[]{:S(2)}) collective-permute-start(bf16[4,128,384]{2,1,0:T(8,128)(2,1)S(1)} %get-tuple-element.32), channel_id=1, source_target_pairs={{0,1},{1,0},{2,3},{3,2},{4,5},{5,4},{6,7},{7,6},{8,9},{9,8},{10,11... | collective-permute-start | bytes 1179656 | tf_op jit(solution)/shard_map/ppermute | solution.py:678
  4.4 13.9 %collective-permute-start = (s32[1,4,128]{2,1,0:T(4,128)S(1)}, s32[1,4,128]{2,1,0:T(4,128)S(1)}, u32[]{:S(2)}, u32[]{:S(2)}) collective-permute-start(s32[1,4,128]{2,1,0:T(4,128)S(1)} %bitcast.30), channel_id=1, source_target_pairs={{0,4},{4,0},{8,12},{12,8},{16,20},{20,16},{24,28},{28,24},{1,5},{5... | collective-permute-start | bytes 6152 | tf_op jit(solution)/shard_map/ppermute | solution.py:689
  11.8 8.3 %collective-permute-start.10 = (bf16[128,384]{1,0:T(8,128)(2,1)S(1)}, bf16[128,384]{1,0:T(8,128)(2,1)S(1)}, u32[]{:S(2)}, u32[]{:S(2)}) collective-permute-start(bf16[128,384]{1,0:T(8,128)(2,1)S(1)} %get-tuple-element.39), channel_id=1, source_target_pairs={{0,24},{4,28},{8,16},{12,20},{16,8},{20,12},{24,0},{28,4},{1,25},{... | collective-permute-start | bytes 294920 | tf_op jit(solution)/shard_map/ppermute | solution.py:689
  16.8 8.7 %collective-permute-start.11 = (bf16[128,384]{1,0:T(8,128)(2,1)S(1)}, bf16[128,384]{1,0:T(8,128)(2,1)S(1)}, u32[]{:S(2)}, u32[]{:S(2)}) collective-permute-start(bf16[128,384]{1,0:T(8,128)(2,1)S(1)} %get-tuple-element.40), channel_id=1, source_target_pairs={{0,28},{4,24},{8,20},{12,16},{16,12},{20,8},{24,4},{28,0},{1,29},{... | collective-permute-start | bytes 294920 | tf_op jit(solution)/shard_map/ppermute | solution.py:689
  17.9 10.6 %collective-permute-start.5 = (bf16[128,384]{1,0:T(8,128)(2,1)S(1)}, bf16[128,384]{1,0:T(8,128)(2,1)S(1)}, u32[]{:S(2)}, u32[]{:S(2)}) collective-permute-start(bf16[128,384]{1,0:T(8,128)(2,1)S(1)} %get-tuple-element.34), channel_id=1, source_target_pairs={{0,4},{4,0},{8,12},{12,8},{16,20},{20,16},{24,28},{28,24},{1,5},{5... | collective-permute-start | bytes 294920 | tf_op jit(solution)/shard_map/ppermute | solution.py:689
  18.3 10.7 %collective-permute-start.6 = (bf16[128,384]{1,0:T(8,128)(2,1)S(1)}, bf16[128,384]{1,0:T(8,128)(2,1)S(1)}, u32[]{:S(2)}, u32[]{:S(2)}) collective-permute-start(bf16[128,384]{1,0:T(8,128)(2,1)S(1)} %get-tuple-element.35), channel_id=1, source_target_pairs={{0,8},{4,12},{8,0},{12,4},{16,24},{20,28},{24,16},{28,20},{1,9},{5... | collective-permute-start | bytes 294920 | tf_op jit(solution)/shard_map/ppermute | solution.py:689
  20.0 9.8 %collective-permute-start.7 = (bf16[128,384]{1,0:T(8,128)(2,1)S(1)}, bf16[128,384]{1,0:T(8,128)(2,1)S(1)}, u32[]{:S(2)}, u32[]{:S(2)}) collective-permute-start(bf16[128,384]{1,0:T(8,128)(2,1)S(1)} %get-tuple-element.36), channel_id=1, source_target_pairs={{0,12},{4,8},{8,4},{12,0},{16,28},{20,24},{24,20},{28,16},{1,13},{... | collective-permute-start | bytes 294920 | tf_op jit(solution)/shard_map/ppermute | solution.py:689
  25.5 10.1 %collective-permute-start.8 = (bf16[128,384]{1,0:T(8,128)(2,1)S(1)}, bf16[128,384]{1,0:T(8,128)(2,1)S(1)}, u32[]{:S(2)}, u32[]{:S(2)}) collective-permute-start(bf16[128,384]{1,0:T(8,128)(2,1)S(1)} %get-tuple-element.37), channel_id=1, source_target_pairs={{0,16},{4,20},{8,24},{12,28},{16,0},{20,4},{24,8},{28,12},{1,17},{... | collective-permute-start | bytes 294920 | tf_op jit(solution)/shard_map/ppermute | solution.py:689
  28.5 9.0 %collective-permute-start.9 = (bf16[128,384]{1,0:T(8,128)(2,1)S(1)}, bf16[128,384]{1,0:T(8,128)(2,1)S(1)}, u32[]{:S(2)}, u32[]{:S(2)}) collective-permute-start(bf16[128,384]{1,0:T(8,128)(2,1)S(1)} %get-tuple-element.38), channel_id=1, source_target_pairs={{0,20},{4,16},{8,28},{12,24},{16,4},{20,0},{24,12},{28,8},{1,21},{... | collective-permute-start | bytes 294920 | tf_op jit(solution)/shard_map/ppermute | solution.py:689
  29.0 10.7 %collective-permute-start.1 = (s32[2,4,128]{2,1,0:T(4,128)S(1)}, s32[2,4,128]{2,1,0:T(4,128)S(1)}, u32[]{:S(2)}, u32[]{:S(2)}) collective-permute-start(s32[2,4,128]{2,1,0:T(4,128)S(1)} %pad_add_fusion.refs_1_), channel_id=1, source_target_pairs={{0,8},{4,12},{8,0},{12,4},{16,24},{20,28},{24,16},{28,20},{1,9},{5... | collective-permute-start | bytes 12296 | tf_op jit(solution)/shard_map/ppermute | solution.py:689
  29.8 10.4 %collective-permute-start.2 = (s32[2,4,128]{2,1,0:T(4,128)S(1)}, s32[2,4,128]{2,1,0:T(4,128)S(1)}, u32[]{:S(2)}, u32[]{:S(2)}) collective-permute-start(s32[2,4,128]{2,1,0:T(4,128)S(1)} %pad_add_fusion.refs_1_), channel_id=1, source_target_pairs={{0,16},{4,20},{8,24},{12,28},{16,0},{20,4},{24,8},{28,12},{1,17},{... | collective-permute-start | bytes 12296 | tf_op jit(solution)/shard_map/ppermute | solution.py:689
  35.6 5.4 %collective-permute-start.3 = (s32[2,4,128]{2,1,0:T(4,128)S(1)}, s32[2,4,128]{2,1,0:T(4,128)S(1)}, u32[]{:S(2)}, u32[]{:S(2)}) collective-permute-start(s32[2,4,128]{2,1,0:T(4,128)S(1)} %pad_add_fusion.refs_1_), channel_id=1, source_target_pairs={{0,24},{4,28},{8,16},{12,20},{16,8},{20,12},{24,0},{28,4},{1,25},{... | collective-permute-start | bytes 12296 | tf_op jit(solution)/shard_map/ppermute | solution.py:689
  38.2 13.5 %collective-permute-start.12 = (bf16[8,128,384]{2,1,0:T(8,128)(2,1)S(1)}, bf16[8,128,384]{2,1,0:T(8,128)(2,1)S(1)}, u32[]{:S(2)}, u32[]{:S(2)}) collective-permute-start(bf16[8,128,384]{2,1,0:T(8,128)(2,1)S(1)} %gather_blocks.3.refs_3_), channel_id=1, source_target_pairs={{0,1},{1,0},{2,3},{3,2},{4,5},{5,4},{6,7},{7,6},{8,9},{9,8},{10,11... | collective-permute-start | bytes 2359304 | tf_op jit(solution)/shard_map/ppermute | solution.py:678
  39.7 30.1 %collective-permute-start.14 = (bf16[512,2048]{1,0:T(8,128)(2,1)}, bf16[512,2048]{1,0:T(8,128)(2,1)}, u32[]{:S(2)}, u32[]{:S(2)}) collective-permute-start(bf16[512,2048]{1,0:T(8,128)(2,1)} %mine_ref.2), channel_id=1, source_target_pairs={{0,1},{1,0},{2,3},{3,2},{4,5},{5,4},{6,7},{7,6},{8,9},{9,8},{10,11... | collective-permute-start | bytes 6291464 | tf_op jit(solution)/shard_map/ppermute | solution.py:678
  55.8 4.3 %collective-permute-start.13 = (bf16[2048,256]{1,0:T(8,128)(2,1)}, bf16[2048,256]{1,0:T(8,128)(2,1)}, u32[]{:S(2)}, u32[]{:S(2)}) collective-permute-start(bf16[2048,256]{1,0:T(8,128)(2,1)} %get-tuple-element.43), channel_id=1, source_target_pairs={{0,1},{1,0},{2,3},{3,2},{4,5},{5,4},{6,7},{7,6},{8,9},{9,8},{10,11... | collective-permute-start | bytes 3145736 | tf_op jit(solution)/shard_map/ppermute | solution.py:678
  55.8 59.7 %collective-permute-start.24 = (bf16[512,1024]{1,0:T(8,128)(2,1)}, bf16[512,1024]{1,0:T(8,128)(2,1)S(1)}, u32[]{:S(2)}, u32[]{:S(2)}) collective-permute-start(bf16[512,1024]{1,0:T(8,128)(2,1)} %get-tuple-element.52), channel_id=1, source_target_pairs={{0,4},{4,0},{8,12},{12,8},{16,20},{20,16},{24,28},{28,24},{1,5},{5... | collective-permute-start | bytes 3145736 | tf_op jit(solution)/shard_map/ppermute | solution.py:689
  58.3 47.2 %copy-start.2 = (bf16[512,2048]{1,0:T(8,128)(2,1)S(1)}, bf16[512,2048]{1,0:T(8,128)(2,1)}, u32[]{:S(2)}) copy-start(bf16[512,2048]{1,0:T(8,128)(2,1)} %mine_ref.2) | copy-start | bytes 6291460
  58.3 72.4 %collective-permute-start.28 = (bf16[256,2048]{1,0:T(8,128)(2,1)}, bf16[256,2048]{1,0:T(8,128)(2,1)}, u32[]{:S(2)}, u32[]{:S(2)}) collective-permute-start(bf16[256,2048]{1,0:T(8,128)(2,1)} %constant_dynamic-slice_fusion), channel_id=1, source_target_pairs={{0,4},{4,0},{8,12},{12,8},{16,20},{20,16},{24,28},{28,24},{1,5},{5... | collective-permute-start | bytes 3145736 | tf_op jit(solution)/shard_map/ppermute | solution.py:689
  66.2 39.2 %all-to-all-start = ((bf16[8,64,128]{2,1,0:T(8,128)(2,1)}), bf16[8,64,128]{2,1,0:T(8,128)(2,1)S(1)}, u32[]{:S(2)}, u32[]{:S(2)}) async-start(bf16[8,64,128]{2,1,0:T(8,128)(2,1)} %bitcast.11), calls=%async_computation | async-start | bytes 262144 | tf_op jit(solution)/shard_map/all_to_all | solution.py:684
  107.9 5.2 %collective-permute-start.15 = (bf16[32,2048]{1,0:T(8,128)(2,1)S(1)}, bf16[32,2048]{1,0:T(8,128)(2,1)S(1)}, u32[]{:S(2)}, u32[]{:S(2)}) collective-permute-start(bf16[32,2048]{1,0:T(8,128)(2,1)S(1)} %get-tuple-element.45), channel_id=1, source_target_pairs={{0,2},{1,3},{2,0},{3,1},{4,6},{5,7},{6,4},{7,5},{8,10},{9,11},{10,... | collective-permute-start | bytes 393224 | tf_op jit(solution)/shard_map/ppermute | solution.py:681
  109.5 60.6 %collective-permute-start.19 = (bf16[512,2048]{1,0:T(8,128)(2,1)}, bf16[512,2048]{1,0:T(8,128)(2,1)S(1)}, u32[]{:S(2)}, u32[]{:S(2)}) collective-permute-start(bf16[512,2048]{1,0:T(8,128)(2,1)} %mine_ref.3), channel_id=1, source_target_pairs={{0,1},{1,0},{2,3},{3,2},{4,5},{5,4},{6,7},{7,6},{8,9},{9,8},{10,11... | collective-permute-start | bytes 6291464 | tf_op jit(solution)/shard_map/ppermute | solution.py:678
  113.3 0.7 copy-start.3
  114.0 6.4 %collective-permute-start.16 = (bf16[32,2048]{1,0:T(8,128)(2,1)S(1)}, bf16[32,2048]{1,0:T(8,128)(2,1)S(1)}, u32[]{:S(2)}, u32[]{:S(2)}) collective-permute-start(bf16[32,2048]{1,0:T(8,128)(2,1)S(1)} %get-tuple-element.47.refs_1_), channel_id=1, source_target_pairs={{0,2},{1,3},{2,0},{3,1},{4,6},{5,7},{6,4},{7,5},{8,10},{9,11},{10,... | collective-permute-start | bytes 393224 | tf_op jit(solution)/shard_map/ppermute | solution.py:681
  115.5 27.4 %collective-permute-start.25 = (bf16[512,1024]{1,0:T(8,128)(2,1)S(1)}, bf16[512,1024]{1,0:T(8,128)(2,1)}, u32[]{:S(2)}, u32[]{:S(2)}) collective-permute-start(bf16[512,1024]{1,0:T(8,128)(2,1)S(1)} %collective-permute-done.24.refs_6_), channel_id=1, source_target_pairs={{0,2},{1,3},{2,0},{3,1},{4,6},{5,7},{6,4},{7,5},{8,10},{9,11},{10,... | collective-permute-start | bytes 3145736 | tf_op jit(solution)/shard_map/ppermute | solution.py:681
  127.1 12.8 %all-to-all-start.1 = ((bf16[8,64,384]{2,1,0:T(8,128)(2,1)}), bf16[8,64,384]{2,1,0:T(8,128)(2,1)S(1)}, u32[]{:S(2)}, u32[]{:S(2)}) async-start(bf16[8,64,384]{2,1,0:T(8,128)(2,1)} %triple_heads.1), calls=%async_computation.1 | async-start | bytes 786432 | tf_op jit(solution)/shard_map/all_to_all | solution.py:684
  130.6 32.7 %collective-permute-start.29 = (bf16[256,2048]{1,0:T(8,128)(2,1)}, bf16[256,2048]{1,0:T(8,128)(2,1)}, u32[]{:S(2)}, u32[]{:S(2)}) collective-permute-start(bf16[256,2048]{1,0:T(8,128)(2,1)} %collective-permute-done.28.refs_10_), channel_id=1, source_target_pairs={{0,2},{1,3},{2,0},{3,1},{4,6},{5,7},{6,4},{7,5},{8,10},{9,11},{10,... | collective-permute-start | bytes 3145736 | tf_op jit(solution)/shard_map/ppermute | solution.py:681
  139.8 23.5 %collective-permute-start.18 = (bf16[8,2,32,384]{3,2,1,0:T(8,128)(2,1)S(1)}, bf16[8,2,32,384]{3,2,1,0:T(8,128)(2,1)S(1)}, u32[]{:S(2)}, u32[]{:S(2)}) collective-permute-start(bf16[8,2,32,384]{3,2,1,0:T(8,128)(2,1)S(1)} %bitcast.22), channel_id=1, source_target_pairs={{0,1},{1,0},{2,3},{3,2},{4,5},{5,4},{6,7},{7,6},{8,9},{9,8},{10,11... | collective-permute-start | bytes 1179656 | tf_op jit(solution)/shard_map/ppermute | solution.py:678
  139.8 45.5 %collective-permute-start.26 = (bf16[512,1024]{1,0:T(8,128)(2,1)S(1)}, bf16[512,1024]{1,0:T(8,128)(2,1)}, u32[]{:S(2)}, u32[]{:S(2)}) collective-permute-start(bf16[512,1024]{1,0:T(8,128)(2,1)S(1)} %collective-permute-done.24.refs_6_), channel_id=1, source_target_pairs={{0,1},{1,0},{2,3},{3,2},{4,5},{5,4},{6,7},{7,6},{8,9},{9,8},{10,11... | collective-permute-start | bytes 3145736 | tf_op jit(solution)/shard_map/ppermute | solution.py:678
  142.9 43.7 %collective-permute-start.30 = (bf16[256,2048]{1,0:T(8,128)(2,1)}, bf16[256,2048]{1,0:T(8,128)(2,1)}, u32[]{:S(2)}, u32[]{:S(2)}) collective-permute-start(bf16[256,2048]{1,0:T(8,128)(2,1)} %collective-permute-done.28.refs_10_), channel_id=1, source_target_pairs={{0,1},{1,0},{2,3},{3,2},{4,5},{5,4},{6,7},{7,6},{8,9},{9,8},{10,11... | collective-permute-start | bytes 3145736 | tf_op jit(solution)/shard_map/ppermute | solution.py:678
  163.3 26.4 %collective-permute-start.27 = (bf16[512,1024]{1,0:T(8,128)(2,1)}, bf16[512,1024]{1,0:T(8,128)(2,1)}, u32[]{:S(2)}, u32[]{:S(2)}) collective-permute-start(bf16[512,1024]{1,0:T(8,128)(2,1)} %collective-permute-done.25.refs_7_), channel_id=1, source_target_pairs={{0,1},{1,0},{2,3},{3,2},{4,5},{5,4},{6,7},{7,6},{8,9},{9,8},{10,11... | collective-permute-start | bytes 3145736 | tf_op jit(solution)/shard_map/ppermute | solution.py:678
  163.3 26.4 %collective-permute-start.31 = (bf16[256,2048]{1,0:T(8,128)(2,1)}, bf16[256,2048]{1,0:T(8,128)(2,1)}, u32[]{:S(2)}, u32[]{:S(2)}) collective-permute-start(bf16[256,2048]{1,0:T(8,128)(2,1)} %collective-permute-done.29.refs_11_), channel_id=1, source_target_pairs={{0,1},{1,0},{2,3},{3,2},{4,5},{5,4},{6,7},{7,6},{8,9},{9,8},{10,11... | collective-permute-start | bytes 3145736 | tf_op jit(solution)/shard_map/ppermute | solution.py:678
  165.8 0.7 copy-start.5
  166.4 18.7 %copy-start.4 = (f32[32,2048]{1,0:T(8,128)S(1)}, f32[32,2048]{1,0:T(8,128)}, u32[]{:S(2)}) copy-start(f32[32,2048]{1,0:T(8,128)} %copy-done.3) | copy-start | bytes 786436
  166.4 11.0 %all-to-all-start.2 = ((bf16[8,64,128]{2,1,0:T(8,128)(2,1)}), bf16[8,64,128]{2,1,0:T(8,128)(2,1)S(1)}, u32[]{:S(2)}, u32[]{:S(2)}) async-start(bf16[8,64,128]{2,1,0:T(8,128)(2,1)} %bitcast.25), calls=%async_computation.2 | async-start | bytes 262144 | tf_op jit(solution)/shard_map/all_to_all | solution.py:684
  177.4 18.8 %copy-start = (bf16[2048,1024]{1,0:T(8,128)(2,1)S(1)}, bf16[2048,1024]{1,0:T(8,128)(2,1)}, u32[]{:S(2)}) copy-start(bf16[2048,1024]{1,0:T(8,128)(2,1)} %refs_4_.1) | copy-start | bytes 12582916
  180.0 5.0 %collective-permute-start.20 = (bf16[32,2048]{1,0:T(8,128)(2,1)S(1)}, bf16[32,2048]{1,0:T(8,128)(2,1)S(1)}, u32[]{:S(2)}, u32[]{:S(2)}) collective-permute-start(bf16[32,2048]{1,0:T(8,128)(2,1)S(1)} %get-tuple-element.49), channel_id=1, source_target_pairs={{0,2},{1,3},{2,0},{3,1},{4,6},{5,7},{6,4},{7,5},{8,10},{9,11},{10,... | collective-permute-start | bytes 393224 | tf_op jit(solution)/shard_map/ppermute | solution.py:681
  185.2 7.1 %collective-permute-start.21 = (bf16[32,2048]{1,0:T(8,128)(2,1)S(1)}, bf16[32,2048]{1,0:T(8,128)(2,1)S(1)}, u32[]{:S(2)}, u32[]{:S(2)}) collective-permute-start(bf16[32,2048]{1,0:T(8,128)(2,1)S(1)} %get-tuple-element.51.refs_0_), channel_id=1, source_target_pairs={{0,8},{4,12},{8,0},{12,4},{16,24},{20,28},{24,16},{28,20},{1,9},{5... | collective-permute-start | bytes 393224 | tf_op jit(solution)/shard_map/ppermute | solution.py:689
  185.3 10.9 %collective-permute-start.22 = (bf16[32,2048]{1,0:T(8,128)(2,1)S(1)}, bf16[32,2048]{1,0:T(8,128)(2,1)S(1)}, u32[]{:S(2)}, u32[]{:S(2)}) collective-permute-start(bf16[32,2048]{1,0:T(8,128)(2,1)S(1)} %get-tuple-element.51.refs_0_), channel_id=1, source_target_pairs={{0,16},{4,20},{8,24},{12,28},{16,0},{20,4},{24,8},{28,12},{1,17},{... | collective-permute-start | bytes 393224 | tf_op jit(solution)/shard_map/ppermute | solution.py:689
  186.6 9.6 %collective-permute-start.23 = (bf16[32,2048]{1,0:T(8,128)(2,1)S(1)}, bf16[32,2048]{1,0:T(8,128)(2,1)S(1)}, u32[]{:S(2)}, u32[]{:S(2)}) collective-permute-start(bf16[32,2048]{1,0:T(8,128)(2,1)S(1)} %get-tuple-element.51.refs_0_), channel_id=1, source_target_pairs={{0,24},{4,28},{8,16},{12,20},{16,8},{20,12},{24,0},{28,4},{1,25},{... | collective-permute-start | bytes 393224 | tf_op jit(solution)/shard_map/ppermute | solution.py:689
  203.9 7.8 %collective-permute-start.32 = (bf16[32,2048]{1,0:T(8,128)(2,1)S(1)}, bf16[32,2048]{1,0:T(8,128)(2,1)S(1)}, u32[]{:S(2)}, u32[]{:S(2)}) collective-permute-start(bf16[32,2048]{1,0:T(8,128)(2,1)S(1)} %get-tuple-element.54), channel_id=1, source_target_pairs={{0,8},{4,12},{8,0},{12,4},{16,24},{20,28},{24,16},{28,20},{1,9},{5... | collective-permute-start | bytes 393224 | tf_op jit(solution)/shard_map/ppermute | solution.py:689
  205.9 10.4 %collective-permute-start.33 = (bf16[32,2048]{1,0:T(8,128)(2,1)S(1)}, bf16[32,2048]{1,0:T(8,128)(2,1)S(1)}, u32[]{:S(2)}, u32[]{:S(2)}) collective-permute-start(bf16[32,2048]{1,0:T(8,128)(2,1)S(1)} %get-tuple-element.55), channel_id=1, source_target_pairs={{0,16},{4,20},{8,24},{12,28},{16,0},{20,4},{24,8},{28,12},{1,17},{... | collective-permute-start | bytes 393224 | tf_op jit(solution)/shard_map/ppermute | solution.py:689
  206.0 10.3 %collective-permute-start.34 = (bf16[32,2048]{1,0:T(8,128)(2,1)S(1)}, bf16[32,2048]{1,0:T(8,128)(2,1)S(1)}, u32[]{:S(2)}, u32[]{:S(2)}) collective-permute-start(bf16[32,2048]{1,0:T(8,128)(2,1)S(1)} %get-tuple-element.56), channel_id=1, source_target_pairs={{0,24},{4,28},{8,16},{12,20},{16,8},{20,12},{24,0},{28,4},{1,25},{... | collective-permute-start | bytes 393224 | tf_op jit(solution)/shard_map/ppermute | solution.py:689

commit v5 on v4

--- a/solution.py
+++ b/solution.py
@@ -321,6 +321,52 @@
     )(scalars, triples, own, other)
 
 
+def stream_kernel(
+    scalars_ref, heads_ref, came_ref, base_ref, *refs,
+):
+    *matrix_refs, stream_ref, normed_ref, matrices, loaded = refs
+    core, duo = scalars_ref[0], scalars_ref[1]
+    half = heads_ref.shape[0] // 2
+    loads = [
+        pltpu.make_async_copy(source, matrices.at[index], loaded.at[index])
+        for index, source in enumerate(matrix_refs)
+    ]
+    for load in loads:
+        load.start()
+    total = base_ref[...].astype(jnp.float32)
+    sides = [(heads_ref, core), (heads_ref, 1 - core), (came_ref, core), (came_ref, 1 - core)]
+    for index, (ref, side) in enumerate(sides):
+        left = jnp.concatenate([ref[side * half + head] for head in range(half)], axis=1)
+        loads[index].wait()
+        total += jnp.dot(left, matrices[index], preferred_element_type=jnp.float32)
+    rows = stream_ref.shape[0]
+    stream_ref[...] = jnp.where(duo == 0, total[:rows], total[rows:])
+    normed_ref[...] = rms_normalize(total).astype(jnp.bfloat16)
+
+
+def stream_rows(scalars, heads, came, base, matrices):
+    rows, width = base.shape
+    inner = matrices[0].shape[0]
+    return pl.pallas_call(
+        stream_kernel,
+        in_specs=[IN_SMEM] + [IN_VMEM] * 3 + [ANYWHERE] * len(matrices),
+        out_specs=[IN_VMEM] * 2,
+        out_shape=[
+            jax.ShapeDtypeStruct((rows // 2, width), jnp.float32),
+            jax.ShapeDtypeStruct((rows, width), jnp.bfloat16),
+        ],
+        scratch_shapes=[
+            pltpu.VMEM((len(matrices), inner, width), jnp.bfloat16),
+            pltpu.SemaphoreType.DMA((len(matrices),)),
+        ],
+        cost_estimate=pl.CostEstimate(
+            flops=8 * rows * inner * width, bytes_accessed=8 * inner * width, transcendentals=0
+        ),
+        compiler_params=pltpu.CompilerParams(vmem_limit_bytes=20 * MIB),
+        name="stream_rows",
+    )(scalars, heads, came, base, *[in_hbm(matrix) for matrix in matrices])
+
+
 def in_hbm(array):
     return pltpu.with_memory_space_constraint(array, pltpu.HBM)
 
@@ -409,8 +455,8 @@
     )(scalars, heads, mine, theirs)
 
 
-def triple_kernel(scale, scalars_ref, own_ref, other_ref, mine_hbm, theirs_hbm, out_ref, matrices, loaded):
-    core, duo = scalars_ref[0], scalars_ref[1]
+def triple_kernel(scale, scalars_ref, rows_ref, mine_hbm, theirs_hbm, out_ref, matrices, loaded):
+    core = scalars_ref[0]
     heads = out_ref.shape[0] // 2
     kinds = mine_hbm.shape[0]
     loads = [
@@ -421,8 +467,7 @@
     ahead = 3
     for load in loads[:ahead]:
         load.start()
-    own, other = own_ref[...], other_ref[...]
-    rows = jnp.concatenate([jnp.where(duo == 0, own, other), jnp.where(duo == 0, other, own)])
+    rows = rows_ref[...]
     for index, load in enumerate(loads):
         load.wait()
         for later in loads[index + ahead : index + ahead + 1]:
@@ -437,27 +482,27 @@
             ]
 
 
-def triple_heads(scalars, own, other, mine, theirs):
-    count, _ = own.shape
+def triple_heads(scalars, rows, mine, theirs):
+    count = rows.shape[0]
     kinds, inner, columns = mine.shape
     heads = columns // HD
     return pl.pallas_call(
         lambda *refs: triple_kernel(HD**-0.5, *refs),
-        in_specs=[IN_SMEM, IN_VMEM, IN_VMEM, ANYWHERE, ANYWHERE],
+        in_specs=[IN_SMEM, IN_VMEM, ANYWHERE, ANYWHERE],
         out_specs=IN_VMEM,
-        out_shape=jax.ShapeDtypeStruct((2 * heads, 2 * count, kinds * HD), jnp.bfloat16),
+        out_shape=jax.ShapeDtypeStruct((2 * heads, count, kinds * HD), jnp.bfloat16),
         scratch_shapes=[
             pltpu.VMEM((2 * kinds, inner, columns), jnp.bfloat16),
             pltpu.SemaphoreType.DMA((2 * kinds,)),
         ],
         cost_estimate=pl.CostEstimate(
-            flops=8 * kinds * count * inner * columns,
+            flops=4 * kinds * count * inner * columns,
             bytes_accessed=4 * kinds * inner * columns,
             transcendentals=0,
         ),
         compiler_params=pltpu.CompilerParams(vmem_limit_bytes=20 * MIB),
         name="triple_heads",
-    )(scalars, own, other, in_hbm(mine), in_hbm(theirs))
+    )(scalars, rows, in_hbm(mine), in_hbm(theirs))
 
 
 def add_norm_kernel(base_ref, kept_ref, came_ref, stream_ref, normed_ref):
@@ -486,7 +531,7 @@
     scale, scalars_ref, context_ref, rows_ref, mine_ref, theirs_ref, pair_ref, query_ref,
     latent_ref, weights_ref,
 ):
-    core, duo, place = scalars_ref[0], scalars_ref[1], scalars_ref[2]
+    core, place = scalars_ref[0], scalars_ref[2]
     _, part, columns = mine_ref.shape
     owners, tiles, rows, size = query_ref.shape
     inner = owners * part
@@ -508,13 +553,16 @@
         left = rows_ref[index * tile : (index + 1) * tile, :]
         query = (product(left, slice(0, size)) * scale).astype(jnp.bfloat16)
         query_ref[:, index] = query.reshape(owners, rows, size)
-    start = pl.multiple_of(duo * tile + place * rows, rows)
-    latent = rows_ref[pl.ds(start, rows), :]
-    for half in range(2):
-        for owner in range(owners):
-            source = half * inner + owner * part
-            target = (owner * 2 + half) * part
-            latent_ref[:, target : target + part] = latent[:, source : source + part]
+    for index in range(tiles):
+        start = pl.multiple_of(index * tile + place * rows, rows)
+        latent = rows_ref[pl.ds(start, rows), :]
+        for half in range(2):
+            for owner in range(owners):
+                source = half * inner + owner * part
+                target = (owner * 2 + half) * part
+                latent_ref[index * rows : (index + 1) * rows, target : target + part] = latent[
+                    :, source : source + part
+                ]
 
 
 def context_heads(scalars, context, latent, mine, theirs, shape):
@@ -528,7 +576,7 @@
         out_shape=[
             jax.ShapeDtypeStruct((keys, 2 * size), jnp.bfloat16),
             jax.ShapeDtypeStruct((owners, tiles, rows, size), jnp.bfloat16),
-            jax.ShapeDtypeStruct((rows, width), jnp.bfloat16),
+            jax.ShapeDtypeStruct((tiles * rows, width), jnp.bfloat16),
         ],
         scratch_shapes=[pltpu.VMEM((width, 3 * size), jnp.bfloat16)],
         cost_estimate=pl.CostEstimate(
@@ -747,7 +795,7 @@
     latent = context_rows(latent_ids.reshape(-1, step), tiles, tables, embed_table, owners)
     arrived = gather_blocks(scalars, arrived, 1)
     arrived_other = swap(arrived)
-    pairs, queries, own_latent = context_heads(
+    pairs, queries, kept_latent = context_heads(
         scalars, context, latent, arrived, arrived_other, (owners, duos, rows)
     )
     other_pairs = swap(pairs)
@@ -762,10 +810,20 @@
         came = cross(given)
         return add_norm(base, kept, came)
 
-    first_stream, normed = project(own_latent, attended, cross_out, swap(cross_out))
-    normed_other = cross(normed)
+    cross_out_duo = cross(cross_out)
+    cross_out_other = swap(cross_out)
+    cross_out_duo_other = swap(cross_out_duo)
+    cross_heads = exchange(attended.reshape(owners, duo_rows, HD))
+    cross_heads_duo = cross(cross_heads)
+    first_stream, normed = stream_rows(
+        scalars,
+        cross_heads,
+        cross_heads_duo,
+        kept_latent,
+        (cross_out, cross_out_other, cross_out_duo, cross_out_duo_other),
+    )
     self_qkv_other = swap(self_qkv)
-    triples = exchange(triple_heads(scalars, normed, normed_other, self_qkv, self_qkv_other))
+    triples = exchange(triple_heads(scalars, normed, self_qkv, self_qkv_other))
     triples = triples.reshape(owners, duos, rows, 3 * HD)
     self_attended = head_attention(
         scalars, triples, triples, swap(triples), False, group_rows

time: 218 us -> 216 us (level)
  waiting for transfers between devices: 109 us -> 98.9 us
  local copies, waits for them, and re-layouts: 3.96 us -> 7.58 us
  starting transfers between devices: 54 us -> 57.4 us
    ppermute x19, waiting for transfers between devices: 20.8 us -> 33.5 us  [across(): lax.ppermute(value, 'ctx', [(i, i ^ distance) for i in range(owners)])]
    all_to_all x3, waiting for transfers between devices: 50.6 us -> 38.3 us  [exchange(): return lax.all_to_all(value, 'ctx', 0, 0, tiled=True)]
    ppermute x5, waiting for transfers between devices: 34.4 us -> 25.2 us  [cross(): return lax.ppermute(value, 'lat', [(i, i ^ 2) for i in range(groups)])]
    pallas_call x0 -> x1, Pallas kernels: none -> 4.63 us  [stream_rows(): pl.pallas_call(stream_kernel, in_specs=[IN_SMEM] + [IN_VMEM] * 3 + [ANYWH...]
    unnamed x14 -> x24, local copies, waits for them, and re-layouts: 1.37 us -> 4.92 us
    pallas_call x2 -> x1, Pallas kernels: 5.03 us -> 2.59 us  [project_rows(): pl.pallas_call(project_kernel, in_specs=[IN_SMEM, IN_VMEM, IN_VMEM, IN_VM...]
    ppermute x19, starting transfers between devices: 34.2 us -> 36.6 us  [across(): lax.ppermute(value, 'ctx', [(i, i ^ distance) for i in range(owners)])]
  transfers between devices with their start and end apart: 38 -> 39, of which waited for: 16 -> 17; matrix products, arithmetic and copies ran while one was open for 2% -> 2% of each run, Pallas kernels for 18% -> 19%
where the time goes in v5:
time: 216 us; the launch traced here: 215 us
  waiting for transfers between devices  98.9 us (46%)
  starting transfers between devices  57.4 us (27%)
  Pallas kernels  48 us (22%)
  local copies, waits for them, and re-layouts  7.58 us (4%)
  other arithmetic  2.36 us (1%)
    all_to_all x3, waiting for transfers between devices, exchange(): return lax.all_to_all(value, 'ctx', 0, 0, tiled=True)  38.3 us
    ppermute x19, starting transfers between devices, across(): lax.ppermute(value, 'ctx', [(i, i ^ distance) for i in range(owners)])  36.6 us
    ppermute x19, waiting for transfers between devices, across(): lax.ppermute(value, 'ctx', [(i, i ^ distance) for i in range(owners)])  33.5 us
    ppermute x5, waiting for transfers between devices, cross(): return lax.ppermute(value, 'lat', [(i, i ^ 2) for i in range(groups)])  25.2 us
    all_to_all x3, starting transfers between devices, exchange(): return lax.all_to_all(value, 'ctx', 0, 0, tiled=True)  11.3 us
    pallas_call x2, Pallas kernels, context_rows(): pl.pallas_call(lambda *refs: context_kernel(owners, first, *refs), grid=(...  10.1 us
    pallas_call x1, Pallas kernels, mlp_shares(): pl.pallas_call(mlp_kernel, in_specs=[IN_SMEM] + [IN_VMEM] * (len(blocks)...  7.65 us
    pallas_call x2, Pallas kernels, head_attention(): pl.pallas_call(lambda *refs: attention_kernel(key_tile, shifted, *refs),...  7.3 us
  transfers between devices with their start and end apart: 39, of which 17 were waited for; matrix products, arithmetic and copies ran while one was open for 2% of the time, Pallas kernels for 19%

profile of v5, /device:TPU:0, one launch (start us, length us, event | category | flops | bytes accessed | tf_op | source)
XLA Modules:
  0.0 215.2 jit_solution(8407825902453164170)
XLA Ops:
  1.2 3.0 %prepare_weights.1 = (bf16[4,128,384]{2,1,0:T(8,128)(2,1)S(1)}, bf16[4,128,384]{2,1,0:T(8,128)(2,1)S(1)}, bf16[512,1024]{1,0:T(8,128)(2,1)}) custom-call(s32[5]{0:T(128)S(1)} %stack.28.refs_0_.scalars_ref, bf16[256,512]{1,0:T(8,128)(2,1)} %query_hbm.1, bf16[2,256,512]{2,1,0:T(8,128)(2,1)} %pair_hbm.1, bf16[2048,1024]{1,0:T(8,128)(2,1)} %refs_4_.1), custom_call_target="tpu_custom_call" | custom-call | tf_op jit(solution)/shard_map/prepare_weights/pallas_call | solution.py:406
  4.4 3.0 %collective-permute-start = (s32[1,4,128]{2,1,0:T(4,128)S(1)}, s32[1,4,128]{2,1,0:T(4,128)S(1)}, u32[]{:S(2)}, u32[]{:S(2)}) collective-permute-start(s32[1,4,128]{2,1,0:T(4,128)S(1)} %bitcast.32), channel_id=1, source_target_pairs={{0,4},{4,0},{8,12},{12,8},{16,20},{20,16},{24,28},{28,24},{1,5},{5... | collective-permute-start | bytes 6152 | tf_op jit(solution)/shard_map/ppermute | solution.py:737
  7.3 1.5 collective-permute-start.16
  9.2 1.9 collective-permute-done.4.theirs_ref
  11.1 0.7 order_blocks.1
  11.8 5.0 %collective-permute-start.10 = (bf16[128,384]{1,0:T(8,128)(2,1)S(1)}, bf16[128,384]{1,0:T(8,128)(2,1)S(1)}, u32[]{:S(2)}, u32[]{:S(2)}) collective-permute-start(bf16[128,384]{1,0:T(8,128)(2,1)S(1)} %get-tuple-element.37), channel_id=1, source_target_pairs={{0,24},{4,28},{8,16},{12,20},{16,8},{20,12},{24,0},{28,4},{1,25},{... | collective-permute-start | bytes 294920 | tf_op jit(solution)/shard_map/ppermute | solution.py:737
  16.8 1.1 collective-permute-start.11
  18.4 1.6 collective-permute-done.10.refs_7_
  20.0 3.7 %collective-permute-start.6 = (bf16[128,384]{1,0:T(8,128)(2,1)S(1)}, bf16[128,384]{1,0:T(8,128)(2,1)S(1)}, u32[]{:S(2)}, u32[]{:S(2)}) collective-permute-start(bf16[128,384]{1,0:T(8,128)(2,1)S(1)} %get-tuple-element.33), channel_id=1, source_target_pairs={{0,8},{4,12},{8,0},{12,4},{16,24},{20,28},{24,16},{28,20},{1,9},{5... | collective-permute-start | bytes 294920 | tf_op jit(solution)/shard_map/ppermute | solution.py:737
  23.7 0.5 collective-permute-done.11.refs_8_
  24.2 2.6 %collective-permute-start.7 = (bf16[128,384]{1,0:T(8,128)(2,1)S(1)}, bf16[128,384]{1,0:T(8,128)(2,1)S(1)}, u32[]{:S(2)}, u32[]{:S(2)}) collective-permute-start(bf16[128,384]{1,0:T(8,128)(2,1)S(1)} %get-tuple-element.34), channel_id=1, source_target_pairs={{0,12},{4,8},{8,4},{12,0},{16,28},{20,24},{24,20},{28,16},{1,13},{... | collective-permute-start | bytes 294920 | tf_op jit(solution)/shard_map/ppermute | solution.py:737
  26.8 0.8 collective-permute-start.1
  27.6 3.2 %collective-permute-start.8 = (bf16[128,384]{1,0:T(8,128)(2,1)S(1)}, bf16[128,384]{1,0:T(8,128)(2,1)S(1)}, u32[]{:S(2)}, u32[]{:S(2)}) collective-permute-start(bf16[128,384]{1,0:T(8,128)(2,1)S(1)} %get-tuple-element.35), channel_id=1, source_target_pairs={{0,16},{4,20},{8,24},{12,28},{16,0},{20,4},{24,8},{28,12},{1,17},{... | collective-permute-start | bytes 294920 | tf_op jit(solution)/shard_map/ppermute | solution.py:737
  30.8 3.5 %collective-permute-start.9 = (bf16[128,384]{1,0:T(8,128)(2,1)S(1)}, bf16[128,384]{1,0:T(8,128)(2,1)S(1)}, u32[]{:S(2)}, u32[]{:S(2)}) collective-permute-start(bf16[128,384]{1,0:T(8,128)(2,1)S(1)} %get-tuple-element.36), channel_id=1, source_target_pairs={{0,20},{4,16},{8,28},{12,24},{16,4},{20,0},{24,12},{28,8},{1,21},{... | collective-permute-start | bytes 294920 | tf_op jit(solution)/shard_map/ppermute | solution.py:737
  34.4 3.3 %collective-permute-done.8.refs_5_ = bf16[128,384]{1,0:T(8,128)(2,1)S(1)} collective-permute-done((bf16[128,384]{1,0:T(8,128)(2,1)S(1)}, bf16[128,384]{1,0:T(8,128)(2,1)S(1)}, u32[]{:S(2)}, u32[]{:S(2)}) %collective-permute-start.8) | collective-permute-done | bytes 98336 | tf_op jit(solution)/shard_map/ppermute | solution.py:737
  37.6 2.2 %collective-permute-done.9.refs_6_ = bf16[128,384]{1,0:T(8,128)(2,1)S(1)} collective-permute-done((bf16[128,384]{1,0:T(8,128)(2,1)S(1)}, bf16[128,384]{1,0:T(8,128)(2,1)S(1)}, u32[]{:S(2)}, u32[]{:S(2)}) %collective-permute-start.9) | collective-permute-done | bytes 98336 | tf_op jit(solution)/shard_map/ppermute | solution.py:737
  39.8 2.2 %collective-permute-start.3 = (s32[2,4,128]{2,1,0:T(4,128)S(1)}, s32[2,4,128]{2,1,0:T(4,128)S(1)}, u32[]{:S(2)}, u32[]{:S(2)}) collective-permute-start(s32[2,4,128]{2,1,0:T(4,128)S(1)} %pad_add_fusion.refs_1_), channel_id=1, source_target_pairs={{0,24},{4,28},{8,16},{12,20},{16,8},{20,12},{24,0},{28,4},{1,25},{... | collective-permute-start | bytes 12296 | tf_op jit(solution)/shard_map/ppermute | solution.py:737
  42.0 0.6 gather_blocks.3.refs_3_
  42.7 1.4 fusion.4
  44.2 0.6 collective-permute-start.15
  45.2 0.5 gather_blocks.2
  45.9 7.7 %context_rows.2.refs_1_ = bf16[2048,2048]{1,0:T(8,128)(2,1)S(1)} custom-call(s32[8,1,256]{2,1,0:T(1,128)S(1)} %bitcast.28, f32[16,2048]{1,0:T(8,128)S(1)} %get-tuple-element.63.refs_1_, f32[16,2048]{1,0:T(8,128)S(1)} %get-tuple-element.64.refs_2_, f32[16,2048]{1,0:T(8,128)S(1)} %get-tuple-element.61.refs_3_, f32[16,2048]{1,0:T(8,128)S(1)} %get-tuple-element.62.refs_4_, ...), custom_call_target="tpu_custom_call" | custom-call | flops 2147483648 | bytes 8388608 | tf_op jit(solution)/shard_map/context_rows/pallas_call | solution.py:240
  53.6 2.4 %context_rows.3.refs_2_ = bf16[512,2048]{1,0:T(8,128)(2,1)S(1)} custom-call(s32[2,1,256]{2,1,0:T(1,128)S(1)} %broadcast_in_dim.30.refs_0_, f32[16,2048]{1,0:T(8,128)S(1)} %get-tuple-element.63.refs_1_, f32[16,2048]{1,0:T(8,128)S(1)} %get-tuple-element.64.refs_2_, f32[16,2048]{1,0:T(8,128)S(1)} %get-tuple-element.61.refs_3_, ...), custom_call_target="tpu_custom_call" | custom-call | flops 536870912 | bytes 2097152 | tf_op jit(solution)/shard_map/context_rows/pallas_call | solution.py:240
  56.1 4.0 %context_heads.1 = (bf16[2048,256]{1,0:T(8,128)(2,1)}, bf16[8,2,32,128]{3,2,1,0:T(8,128)(2,1)S(1)}, bf16[64,2048]{1,0:T(8,128)(2,1)S(1)}) custom-call(s32[5]{0:T(128)S(1)} %stack.28.refs_0_.scalars_ref, bf16[2048,2048]{1,0:T(8,128)(2,1)S(1)} %context_rows.2.refs_1_, bf16[512,2048]{1,0:T(8,128)(2,1)S(1)} %context_rows.3.refs_2_, ...), custom_call_target="tpu_custom_call" | custom-call | flops 2684354560 | bytes 8388608 | tf_op jit(solution)/shard_map/context_heads/pallas_call | solution.py:572
  60.2 0.7 copy-done.3
  61.4 0.7 collective-permute-start.25
  62.1 2.4 %constant_dynamic-slice_fusion = bf16[256,2048]{1,0:T(8,128)(2,1)} fusion(bf16[1024,2048]{1,0:T(8,128)(2,1)} %refs_5_.1, s32[]{:T(128)S(6)} %select_n.97), kind=kLoop, calls=%fused_computation.37 | loop fusion | bytes 2097156 | tf_op jit(solution)/shard_map/dynamic_slice | solution.py:741
  64.4 1.0 copy-done.9
  65.4 1.3 collective-permute-start.29
  66.8 1.2 copy-done.10
  68.0 5.4 %head_attention.2 = bf16[8,2,32,128]{3,2,1,0:T(8,128)(2,1)S(1)} custom-call(s32[5]{0:T(128)S(1)} %stack.28.refs_0_.scalars_ref, bf16[8,2,32,128]{3,2,1,0:T(8,128)(2,1)S(1)} %get-tuple-element.39.refs_1_, bf16[1,4,512,256]{3,2,1,0:T(8,128)(2,1)} %bitcast.9.refs_2_, bf16[1,4,512,256]{3,2,1,0:T(8,128)(2,1)S(1)} %bitcast.29), custom_call_target="tpu_custom_call" | custom-call | flops 2147483648 | bytes 2097152 | tf_op jit(solution)/shard_map/head_attention/pallas_call | solution.py:301
  73.4 0.6 copy-done.7
  74.0 3.8 %all-to-all-start = ((bf16[8,64,128]{2,1,0:T(8,128)(2,1)}), bf16[8,64,128]{2,1,0:T(8,128)(2,1)S(1)}, u32[]{:S(2)}, u32[]{:S(2)}) async-start(bf16[8,64,128]{2,1,0:T(8,128)(2,1)} %bitcast.25), calls=%async_computation | async-start | bytes 262144 | tf_op jit(solution)/shard_map/all_to_all | solution.py:732
  77.8 10.9 %collective-permute-done.25.refs_6_ = bf16[512,1024]{1,0:T(8,128)(2,1)S(1)} collective-permute-done((bf16[512,1024]{1,0:T(8,128)(2,1)}, bf16[512,1024]{1,0:T(8,128)(2,1)S(1)}, u32[]{:S(2)}, u32[]{:S(2)}) %collective-permute-start.25) | collective-permute-done | bytes 1048608 | tf_op jit(solution)/shard_map/ppermute | solution.py:737
  88.7 21.9 %all-to-all-done.heads_ref = bf16[8,64,128]{2,1,0:T(8,128)(2,1)S(1)} async-done(((bf16[8,64,128]{2,1,0:T(8,128)(2,1)}), bf16[8,64,128]{2,1,0:T(8,128)(2,1)S(1)}, u32[]{:S(2)}, u32[]{:S(2)}) %all-to-all-start) | async-done | bytes 131104 | tf_op jit(solution)/shard_map/all_to_all | solution.py:732
  110.5 1.5 collective-permute-start.14
  112.1 3.4 %collective-permute-done.14.came_ref = bf16[8,64,128]{2,1,0:T(8,128)(2,1)S(1)} collective-permute-done((bf16[8,64,128]{2,1,0:T(8,128)(2,1)S(1)}, bf16[8,64,128]{2,1,0:T(8,128)(2,1)S(1)}, u32[]{:S(2)}, u32[]{:S(2)}) %collective-permute-start.14) | collective-permute-done | bytes 131104 | tf_op jit(solution)/shard_map/ppermute | solution.py:729
  115.5 1.5 collective-permute-start.26
  117.0 4.6 %stream_rows.1 = (f32[32,2048]{1,0:T(8,128)S(1)}, bf16[64,2048]{1,0:T(8,128)(2,1)S(1)}) custom-call(s32[5]{0:T(128)S(1)} %stack.28.refs_0_.scalars_ref, bf16[8,64,128]{2,1,0:T(8,128)(2,1)S(1)} %all-to-all-done.heads_ref, bf16[8,64,128]{2,1,0:T(8,128)(2,1)S(1)} %collective-permute-done.14.came_ref, bf16[64,2048]{1,0:T(8,128)(2,1)S(1)} %copy-done.4, ...), custom_call_target="tpu_custom_call" | custom-call | flops 536870912 | bytes 8388608 | tf_op jit(solution)/shard_map/stream_rows/pallas_call | solution.py:350
  121.7 0.7 copy-done.5
  122.4 6.7 %triple_heads.1 = bf16[8,64,384]{2,1,0:T(8,128)(2,1)} custom-call(s32[5]{0:T(128)S(1)} %stack.28.refs_0_.scalars_ref, bf16[64,2048]{1,0:T(8,128)(2,1)S(1)} %get-tuple-element.43.refs_1_, bf16[3,2048,512]{2,1,0:T(8,128)(2,1)} %refs_2_.1, bf16[3,2048,512]{2,1,0:T(8,128)(2,1)} %collective-permute-done.18.refs_3_), custom_call_target="tpu_custom_call" | custom-call | flops 805306368 | bytes 12582912 | tf_op jit(solution)/shard_map/triple_heads/pallas_call | solution.py:489
  129.1 3.8 %all-to-all-start.1 = ((bf16[8,64,384]{2,1,0:T(8,128)(2,1)}), bf16[8,64,384]{2,1,0:T(8,128)(2,1)S(1)}, u32[]{:S(2)}, u32[]{:S(2)}) async-start(bf16[8,64,384]{2,1,0:T(8,128)(2,1)} %triple_heads.1), calls=%async_computation.1 | async-start | bytes 786432 | tf_op jit(solution)/shard_map/all_to_all | solution.py:732
  132.8 0.6 collective-permute-start.30
  133.4 9.1 %all-to-all-done.1 = bf16[8,64,384]{2,1,0:T(8,128)(2,1)S(1)} async-done(((bf16[8,64,384]{2,1,0:T(8,128)(2,1)}), bf16[8,64,384]{2,1,0:T(8,128)(2,1)S(1)}, u32[]{:S(2)}, u32[]{:S(2)}) %all-to-all-start.1) | async-done | bytes 393248 | tf_op jit(solution)/shard_map/all_to_all | solution.py:732
  142.5 0.5 collective-permute-start.27
  143.0 18.3 %collective-permute-done.30.refs_11_ = bf16[256,2048]{1,0:T(8,128)(2,1)} collective-permute-done((bf16[256,2048]{1,0:T(8,128)(2,1)}, bf16[256,2048]{1,0:T(8,128)(2,1)}, u32[]{:S(2)}, u32[]{:S(2)}) %collective-permute-start.30) | collective-permute-done | bytes 1048608 | tf_op jit(solution)/shard_map/ppermute | solution.py:729
  161.3 0.5 collective-permute-start.32
  161.8 1.9 head_attention.3
  163.7 0.6 copy-done.8
  164.4 3.7 %all-to-all-start.2 = ((bf16[8,64,128]{2,1,0:T(8,128)(2,1)}), bf16[8,64,128]{2,1,0:T(8,128)(2,1)S(1)}, u32[]{:S(2)}, u32[]{:S(2)}) async-start(bf16[8,64,128]{2,1,0:T(8,128)(2,1)} %bitcast.26), calls=%async_computation.2 | async-start | bytes 262144 | tf_op jit(solution)/shard_map/all_to_all | solution.py:732
  168.1 7.3 %all-to-all-done.2.heads_ref = bf16[8,64,128]{2,1,0:T(8,128)(2,1)S(1)} async-done(((bf16[8,64,128]{2,1,0:T(8,128)(2,1)}), bf16[8,64,128]{2,1,0:T(8,128)(2,1)S(1)}, u32[]{:S(2)}, u32[]{:S(2)}) %all-to-all-start.2) | async-done | bytes 131104 | tf_op jit(solution)/shard_map/all_to_all | solution.py:732
  175.5 2.6 %project_rows.1 = (f32[32,2048]{1,0:T(8,128)S(1)}, bf16[32,2048]{1,0:T(8,128)(2,1)S(1)}) custom-call(s32[5]{0:T(128)S(1)} %stack.28.refs_0_.scalars_ref, bf16[8,64,128]{2,1,0:T(8,128)(2,1)S(1)} %all-to-all-done.2.heads_ref, bf16[512,2048]{1,0:T(8,128)(2,1)S(1)} %copy-done.2, bf16[512,2048]{1,0:T(8,128)(2,1)} %collective-permute-done.20.theirs_ref), custom_call_target="tpu_custom_call" | custom-call | flops 268435456 | bytes 4194304 | tf_op jit(solution)/shard_map/project_rows/pallas_call | solution.py:442
  178.1 1.6 collective-permute-start.21
  179.7 3.4 %collective-permute-done.21.came_ref = bf16[32,2048]{1,0:T(8,128)(2,1)S(1)} collective-permute-done((bf16[32,2048]{1,0:T(8,128)(2,1)S(1)}, bf16[32,2048]{1,0:T(8,128)(2,1)S(1)}, u32[]{:S(2)}, u32[]{:S(2)}) %collective-permute-start.21) | collective-permute-done | bytes 131104 | tf_op jit(solution)/shard_map/ppermute | solution.py:729
  183.3 1.3 collective-permute-start.23
  184.6 3.1 %collective-permute-start.24 = (bf16[32,2048]{1,0:T(8,128)(2,1)S(1)}, bf16[32,2048]{1,0:T(8,128)(2,1)S(1)}, u32[]{:S(2)}, u32[]{:S(2)}) collective-permute-start(bf16[32,2048]{1,0:T(8,128)(2,1)S(1)} %get-tuple-element.47.refs_0_), channel_id=1, source_target_pairs={{0,24},{4,28},{8,16},{12,20},{16,8},{20,12},{24,0},{28,4},{1,25},{... | collective-permute-start | bytes 393224 | tf_op jit(solution)/shard_map/ppermute | solution.py:737
  187.7 2.6 %collective-permute-done.22.refs_1_ = bf16[32,2048]{1,0:T(8,128)(2,1)S(1)} collective-permute-done((bf16[32,2048]{1,0:T(8,128)(2,1)S(1)}, bf16[32,2048]{1,0:T(8,128)(2,1)S(1)}, u32[]{:S(2)}, u32[]{:S(2)}) %collective-permute-start.22) | collective-permute-done | bytes 131104 | tf_op jit(solution)/shard_map/ppermute | solution.py:737
  190.3 3.9 %collective-permute-done.23.refs_2_ = bf16[32,2048]{1,0:T(8,128)(2,1)S(1)} collective-permute-done((bf16[32,2048]{1,0:T(8,128)(2,1)S(1)}, bf16[32,2048]{1,0:T(8,128)(2,1)S(1)}, u32[]{:S(2)}, u32[]{:S(2)}) %collective-permute-start.23) | collective-permute-done | bytes 131104 | tf_op jit(solution)/shard_map/ppermute | solution.py:737
  194.2 7.6 %mlp_shares.1 = (f32[32,2048]{1,0:T(8,128)S(1)}, bf16[32,2048]{1,0:T(8,128)(2,1)S(1)}, bf16[32,2048]{1,0:T(8,128)(2,1)S(1)}, bf16[32,2048]{1,0:T(8,128)(2,1)S(1)}) custom-call(s32[5]{0:T(128)S(1)} %stack.28.refs_0_.scalars_ref, bf16[32,2048]{1,0:T(8,128)(2,1)S(1)} %get-tuple-element.47.refs_0_, bf16[32,2048]{1,0:T(8,128)(2,1)S(1)} %collective-permute-done.22.refs_1_, ...), custom_call_target="tpu_custom_call" | custom-call | flops 2147483648 | bytes 16777216 | tf_op jit(solution)/shard_map/mlp_shares/pallas_call | solution.py:674
  201.9 2.0 collective-permute-start.33
  204.1 2.3 %collective-permute-start.35 = (bf16[32,2048]{1,0:T(8,128)(2,1)S(1)}, bf16[32,2048]{1,0:T(8,128)(2,1)S(1)}, u32[]{:S(2)}, u32[]{:S(2)}) collective-permute-start(bf16[32,2048]{1,0:T(8,128)(2,1)S(1)} %get-tuple-element.52), channel_id=1, source_target_pairs={{0,24},{4,28},{8,16},{12,20},{16,8},{20,12},{24,0},{28,4},{1,25},{... | collective-permute-start | bytes 393224 | tf_op jit(solution)/shard_map/ppermute | solution.py:737
  206.3 3.3 %collective-permute-done.33 = bf16[32,2048]{1,0:T(8,128)(2,1)S(1)} collective-permute-done((bf16[32,2048]{1,0:T(8,128)(2,1)S(1)}, bf16[32,2048]{1,0:T(8,128)(2,1)S(1)}, u32[]{:S(2)}, u32[]{:S(2)}) %collective-permute-start.33) | collective-permute-done | bytes 131104 | tf_op jit(solution)/shard_map/ppermute | solution.py:737
  209.6 4.8 %collective-permute-done.34 = bf16[32,2048]{1,0:T(8,128)(2,1)S(1)} collective-permute-done((bf16[32,2048]{1,0:T(8,128)(2,1)S(1)}, bf16[32,2048]{1,0:T(8,128)(2,1)S(1)}, u32[]{:S(2)}, u32[]{:S(2)}) %collective-permute-start.34) | collective-permute-done | bytes 131104 | tf_op jit(solution)/shard_map/ppermute | solution.py:737
  214.4 0.7 fusion.3
  (73 shorter events, 3.1 us)
Async XLA Ops:
  0.0 122.4 %collective-permute-start.18 = (bf16[3,2048,512]{2,1,0:T(8,128)(2,1)}, bf16[3,2048,512]{2,1,0:T(8,128)(2,1)}, u32[]{:S(2)}, u32[]{:S(2)}) collective-permute-start(bf16[3,2048,512]{2,1,0:T(8,128)(2,1)} %refs_2_.1), channel_id=1, source_target_pairs={{0,1},{1,0},{2,3},{3,2},{4,5},{5,4},{6,7},{7,6},{8,9},{9,8},{10,11... | collective-permute-start | bytes 18874376 | tf_op jit(solution)/shard_map/ppermute | solution.py:726
  1.2 3.1 %copy-start.11 = (s32[512]{0:T(512)S(1)}, s32[512]{0:T(512)}, u32[]{:S(2)}) copy-start(s32[512]{0:T(512)} %param.10) | copy-start | bytes 6148
  4.3 41.6 %copy-start.1 = (bf16[256,2048]{1,0:T(8,128)(2,1)S(1)}, bf16[256,2048]{1,0:T(8,128)(2,1)}, u32[]{:S(2)}) copy-start(bf16[256,2048]{1,0:T(8,128)(2,1)} %refs_7_.3) | copy-start | bytes 3145732
  4.3 6.8 %collective-permute-start.4 = (bf16[4,128,384]{2,1,0:T(8,128)(2,1)S(1)}, bf16[4,128,384]{2,1,0:T(8,128)(2,1)S(1)}, u32[]{:S(2)}, u32[]{:S(2)}) collective-permute-start(bf16[4,128,384]{2,1,0:T(8,128)(2,1)S(1)} %get-tuple-element.30), channel_id=1, source_target_pairs={{0,1},{1,0},{2,3},{3,2},{4,5},{5,4},{6,7},{7,6},{8,9},{9,8},{10,11... | collective-permute-start | bytes 1179656 | tf_op jit(solution)/shard_map/ppermute | solution.py:726
  4.4 13.6 %collective-permute-start = (s32[1,4,128]{2,1,0:T(4,128)S(1)}, s32[1,4,128]{2,1,0:T(4,128)S(1)}, u32[]{:S(2)}, u32[]{:S(2)}) collective-permute-start(s32[1,4,128]{2,1,0:T(4,128)S(1)} %bitcast.32), channel_id=1, source_target_pairs={{0,4},{4,0},{8,12},{12,8},{16,20},{20,16},{24,28},{28,24},{1,5},{5... | collective-permute-start | bytes 6152 | tf_op jit(solution)/shard_map/ppermute | solution.py:737
  7.3 48.7 %collective-permute-start.16 = (bf16[512,2048]{1,0:T(8,128)(2,1)}, bf16[512,2048]{1,0:T(8,128)(2,1)}, u32[]{:S(2)}, u32[]{:S(2)}) collective-permute-start(bf16[512,2048]{1,0:T(8,128)(2,1)} %refs_0_.1), channel_id=1, source_target_pairs={{0,2},{1,3},{2,0},{3,1},{4,6},{5,7},{6,4},{7,5},{8,10},{9,11},{10,... | collective-permute-start | bytes 6291464 | tf_op jit(solution)/shard_map/ppermute | solution.py:729
  11.8 8.3 %collective-permute-start.10 = (bf16[128,384]{1,0:T(8,128)(2,1)S(1)}, bf16[128,384]{1,0:T(8,128)(2,1)S(1)}, u32[]{:S(2)}, u32[]{:S(2)}) collective-permute-start(bf16[128,384]{1,0:T(8,128)(2,1)S(1)} %get-tuple-element.37), channel_id=1, source_target_pairs={{0,24},{4,28},{8,16},{12,20},{16,8},{20,12},{24,0},{28,4},{1,25},{... | collective-permute-start | bytes 294920 | tf_op jit(solution)/shard_map/ppermute | solution.py:737
  16.8 7.5 %collective-permute-start.11 = (bf16[128,384]{1,0:T(8,128)(2,1)S(1)}, bf16[128,384]{1,0:T(8,128)(2,1)S(1)}, u32[]{:S(2)}, u32[]{:S(2)}) collective-permute-start(bf16[128,384]{1,0:T(8,128)(2,1)S(1)} %get-tuple-element.38), channel_id=1, source_target_pairs={{0,28},{4,24},{8,20},{12,16},{16,12},{20,8},{24,4},{28,0},{1,29},{... | collective-permute-start | bytes 294920 | tf_op jit(solution)/shard_map/ppermute | solution.py:737
  17.9 8.9 %collective-permute-start.5 = (bf16[128,384]{1,0:T(8,128)(2,1)S(1)}, bf16[128,384]{1,0:T(8,128)(2,1)S(1)}, u32[]{:S(2)}, u32[]{:S(2)}) collective-permute-start(bf16[128,384]{1,0:T(8,128)(2,1)S(1)} %get-tuple-element.32), channel_id=1, source_target_pairs={{0,4},{4,0},{8,12},{12,8},{16,20},{20,16},{24,28},{28,24},{1,5},{5... | collective-permute-start | bytes 294920 | tf_op jit(solution)/shard_map/ppermute | solution.py:737
  20.0 7.6 %collective-permute-start.6 = (bf16[128,384]{1,0:T(8,128)(2,1)S(1)}, bf16[128,384]{1,0:T(8,128)(2,1)S(1)}, u32[]{:S(2)}, u32[]{:S(2)}) collective-permute-start(bf16[128,384]{1,0:T(8,128)(2,1)S(1)} %get-tuple-element.33), channel_id=1, source_target_pairs={{0,8},{4,12},{8,0},{12,4},{16,24},{20,28},{24,16},{28,20},{1,9},{5... | collective-permute-start | bytes 294920 | tf_op jit(solution)/shard_map/ppermute | solution.py:737
  24.2 6.6 %collective-permute-start.7 = (bf16[128,384]{1,0:T(8,128)(2,1)S(1)}, bf16[128,384]{1,0:T(8,128)(2,1)S(1)}, u32[]{:S(2)}, u32[]{:S(2)}) collective-permute-start(bf16[128,384]{1,0:T(8,128)(2,1)S(1)} %get-tuple-element.34), channel_id=1, source_target_pairs={{0,12},{4,8},{8,4},{12,0},{16,28},{20,24},{24,20},{28,16},{1,13},{... | collective-permute-start | bytes 294920 | tf_op jit(solution)/shard_map/ppermute | solution.py:737
  26.8 15.8 %collective-permute-start.1 = (s32[2,4,128]{2,1,0:T(4,128)S(1)}, s32[2,4,128]{2,1,0:T(4,128)S(1)}, u32[]{:S(2)}, u32[]{:S(2)}) collective-permute-start(s32[2,4,128]{2,1,0:T(4,128)S(1)} %pad_add_fusion.refs_1_), channel_id=1, source_target_pairs={{0,8},{4,12},{8,0},{12,4},{16,24},{20,28},{24,16},{28,20},{1,9},{5... | collective-permute-start | bytes 12296 | tf_op jit(solution)/shard_map/ppermute | solution.py:737
  27.6 10.0 %collective-permute-start.8 = (bf16[128,384]{1,0:T(8,128)(2,1)S(1)}, bf16[128,384]{1,0:T(8,128)(2,1)S(1)}, u32[]{:S(2)}, u32[]{:S(2)}) collective-permute-start(bf16[128,384]{1,0:T(8,128)(2,1)S(1)} %get-tuple-element.35), channel_id=1, source_target_pairs={{0,16},{4,20},{8,24},{12,28},{16,0},{20,4},{24,8},{28,12},{1,17},{... | collective-permute-start | bytes 294920 | tf_op jit(solution)/shard_map/ppermute | solution.py:737
  30.8 9.0 %collective-permute-start.9 = (bf16[128,384]{1,0:T(8,128)(2,1)S(1)}, bf16[128,384]{1,0:T(8,128)(2,1)S(1)}, u32[]{:S(2)}, u32[]{:S(2)}) collective-permute-start(bf16[128,384]{1,0:T(8,128)(2,1)S(1)} %get-tuple-element.36), channel_id=1, source_target_pairs={{0,20},{4,16},{8,28},{12,24},{16,4},{20,0},{24,12},{28,8},{1,21},{... | collective-permute-start | bytes 294920 | tf_op jit(solution)/shard_map/ppermute | solution.py:737
  37.6 6.6 %collective-permute-start.2 = (s32[2,4,128]{2,1,0:T(4,128)S(1)}, s32[2,4,128]{2,1,0:T(4,128)S(1)}, u32[]{:S(2)}, u32[]{:S(2)}) collective-permute-start(s32[2,4,128]{2,1,0:T(4,128)S(1)} %pad_add_fusion.refs_1_), channel_id=1, source_target_pairs={{0,16},{4,20},{8,24},{12,28},{16,0},{20,4},{24,8},{28,12},{1,17},{... | collective-permute-start | bytes 12296 | tf_op jit(solution)/shard_map/ppermute | solution.py:737
  39.8 5.4 %collective-permute-start.3 = (s32[2,4,128]{2,1,0:T(4,128)S(1)}, s32[2,4,128]{2,1,0:T(4,128)S(1)}, u32[]{:S(2)}, u32[]{:S(2)}) collective-permute-start(s32[2,4,128]{2,1,0:T(4,128)S(1)} %pad_add_fusion.refs_1_), channel_id=1, source_target_pairs={{0,24},{4,28},{8,16},{12,20},{16,8},{20,12},{24,0},{28,4},{1,25},{... | collective-permute-start | bytes 12296 | tf_op jit(solution)/shard_map/ppermute | solution.py:737
  42.7 13.5 %collective-permute-start.12 = (bf16[8,128,384]{2,1,0:T(8,128)(2,1)S(1)}, bf16[8,128,384]{2,1,0:T(8,128)(2,1)S(1)}, u32[]{:S(2)}, u32[]{:S(2)}) collective-permute-start(bf16[8,128,384]{2,1,0:T(8,128)(2,1)S(1)} %gather_blocks.3.refs_3_), channel_id=1, source_target_pairs={{0,1},{1,0},{2,3},{3,2},{4,5},{5,4},{6,7},{7,6},{8,9},{9,8},{10,11... | collective-permute-start | bytes 2359304 | tf_op jit(solution)/shard_map/ppermute | solution.py:726
  44.2 67.9 %collective-permute-start.15 = (bf16[512,2048]{1,0:T(8,128)(2,1)}, bf16[512,2048]{1,0:T(8,128)(2,1)}, u32[]{:S(2)}, u32[]{:S(2)}) collective-permute-start(bf16[512,2048]{1,0:T(8,128)(2,1)} %refs_0_.1), channel_id=1, source_target_pairs={{0,1},{1,0},{2,3},{3,2},{4,5},{5,4},{6,7},{7,6},{8,9},{9,8},{10,11... | collective-permute-start | bytes 6291464 | tf_op jit(solution)/shard_map/ppermute | solution.py:726
  56.0 61.0 %collective-permute-start.17 = (bf16[512,2048]{1,0:T(8,128)(2,1)}, bf16[512,2048]{1,0:T(8,128)(2,1)}, u32[]{:S(2)}, u32[]{:S(2)}) collective-permute-start(bf16[512,2048]{1,0:T(8,128)(2,1)} %collective-permute-done.16.refs_2_), channel_id=1, source_target_pairs={{0,1},{1,0},{2,3},{3,2},{4,5},{5,4},{6,7},{7,6},{8,9},{9,8},{10,11... | collective-permute-start | bytes 6291464 | tf_op jit(solution)/shard_map/ppermute | solution.py:726
  60.2 0.7 copy-start.3
  60.9 3.6 %collective-permute-start.13 = (bf16[2048,256]{1,0:T(8,128)(2,1)}, bf16[2048,256]{1,0:T(8,128)(2,1)S(1)}, u32[]{:S(2)}, u32[]{:S(2)}) collective-permute-start(bf16[2048,256]{1,0:T(8,128)(2,1)} %get-tuple-element.40), channel_id=1, source_target_pairs={{0,1},{1,0},{2,3},{3,2},{4,5},{5,4},{6,7},{7,6},{8,9},{9,8},{10,11... | collective-permute-start | bytes 3145736 | tf_op jit(solution)/shard_map/ppermute | solution.py:726
  61.4 27.3 %collective-permute-start.25 = (bf16[512,1024]{1,0:T(8,128)(2,1)}, bf16[512,1024]{1,0:T(8,128)(2,1)S(1)}, u32[]{:S(2)}, u32[]{:S(2)}) collective-permute-start(bf16[512,1024]{1,0:T(8,128)(2,1)} %get-tuple-element.48), channel_id=1, source_target_pairs={{0,4},{4,0},{8,12},{12,8},{16,20},{20,16},{24,28},{28,24},{1,5},{5... | collective-permute-start | bytes 3145736 | tf_op jit(solution)/shard_map/ppermute | solution.py:737
  64.4 1.0 copy-start.9
  65.4 67.4 %collective-permute-start.29 = (bf16[256,2048]{1,0:T(8,128)(2,1)}, bf16[256,2048]{1,0:T(8,128)(2,1)}, u32[]{:S(2)}, u32[]{:S(2)}) collective-permute-start(bf16[256,2048]{1,0:T(8,128)(2,1)} %constant_dynamic-slice_fusion), channel_id=1, source_target_pairs={{0,4},{4,0},{8,12},{12,8},{16,20},{20,16},{24,28},{28,24},{1,5},{5... | collective-permute-start | bytes 3145736 | tf_op jit(solution)/shard_map/ppermute | solution.py:737
  66.8 1.2 copy-start.10
  68.0 44.1 %copy-start.2 = (bf16[512,2048]{1,0:T(8,128)(2,1)S(1)}, bf16[512,2048]{1,0:T(8,128)(2,1)}, u32[]{:S(2)}) copy-start(bf16[512,2048]{1,0:T(8,128)(2,1)} %mine_ref.1) | copy-start | bytes 6291460
  68.0 49.1 %copy-start.4 = (bf16[64,2048]{1,0:T(8,128)(2,1)S(1)}, bf16[64,2048]{1,0:T(8,128)(2,1)}, u32[]{:S(2)}) copy-start(bf16[64,2048]{1,0:T(8,128)(2,1)} %copy-done.3) | copy-start | bytes 786436
  73.4 0.7 copy-start.7
  74.0 36.5 %all-to-all-start = ((bf16[8,64,128]{2,1,0:T(8,128)(2,1)}), bf16[8,64,128]{2,1,0:T(8,128)(2,1)S(1)}, u32[]{:S(2)}, u32[]{:S(2)}) async-start(bf16[8,64,128]{2,1,0:T(8,128)(2,1)} %bitcast.25), calls=%async_computation | async-start | bytes 262144 | tf_op jit(solution)/shard_map/all_to_all | solution.py:732
  110.5 5.0 %collective-permute-start.14 = (bf16[8,64,128]{2,1,0:T(8,128)(2,1)S(1)}, bf16[8,64,128]{2,1,0:T(8,128)(2,1)S(1)}, u32[]{:S(2)}, u32[]{:S(2)}) collective-permute-start(bf16[8,64,128]{2,1,0:T(8,128)(2,1)S(1)} %all-to-all-done.heads_ref), channel_id=1, source_target_pairs={{0,2},{1,3},{2,0},{3,1},{4,6},{5,7},{6,4},{7,5},{8,10},{9,11},{10,... | collective-permute-start | bytes 393224 | tf_op jit(solution)/shard_map/ppermute | solution.py:729
  112.1 56.1 %collective-permute-start.20 = (bf16[512,2048]{1,0:T(8,128)(2,1)S(1)}, bf16[512,2048]{1,0:T(8,128)(2,1)}, u32[]{:S(2)}, u32[]{:S(2)}) collective-permute-start(bf16[512,2048]{1,0:T(8,128)(2,1)S(1)} %copy-done.2), channel_id=1, source_target_pairs={{0,1},{1,0},{2,3},{3,2},{4,5},{5,4},{6,7},{7,6},{8,9},{9,8},{10,11... | collective-permute-start | bytes 6291464 | tf_op jit(solution)/shard_map/ppermute | solution.py:726
  115.5 27.5 %collective-permute-start.26 = (bf16[512,1024]{1,0:T(8,128)(2,1)S(1)}, bf16[512,1024]{1,0:T(8,128)(2,1)}, u32[]{:S(2)}, u32[]{:S(2)}) collective-permute-start(bf16[512,1024]{1,0:T(8,128)(2,1)S(1)} %collective-permute-done.25.refs_6_), channel_id=1, source_target_pairs={{0,2},{1,3},{2,0},{3,1},{4,6},{5,7},{6,4},{7,5},{8,10},{9,11},{10,... | collective-permute-start | bytes 3145736 | tf_op jit(solution)/shard_map/ppermute | solution.py:729
  121.7 0.7 copy-start.5
  129.1 13.4 %all-to-all-start.1 = ((bf16[8,64,384]{2,1,0:T(8,128)(2,1)}), bf16[8,64,384]{2,1,0:T(8,128)(2,1)S(1)}, u32[]{:S(2)}, u32[]{:S(2)}) async-start(bf16[8,64,384]{2,1,0:T(8,128)(2,1)} %triple_heads.1), calls=%async_computation.1 | async-start | bytes 786432 | tf_op jit(solution)/shard_map/all_to_all | solution.py:732
  132.8 28.4 %collective-permute-start.30 = (bf16[256,2048]{1,0:T(8,128)(2,1)}, bf16[256,2048]{1,0:T(8,128)(2,1)}, u32[]{:S(2)}, u32[]{:S(2)}) collective-permute-start(bf16[256,2048]{1,0:T(8,128)(2,1)} %collective-permute-done.29.refs_10_), channel_id=1, source_target_pairs={{0,2},{1,3},{2,0},{3,1},{4,6},{5,7},{6,4},{7,5},{8,10},{9,11},{10,... | collective-permute-start | bytes 3145736 | tf_op jit(solution)/shard_map/ppermute | solution.py:729
  142.5 18.8 %collective-permute-start.19 = (bf16[8,2,32,384]{3,2,1,0:T(8,128)(2,1)S(1)}, bf16[8,2,32,384]{3,2,1,0:T(8,128)(2,1)S(1)}, u32[]{:S(2)}, u32[]{:S(2)}) collective-permute-start(bf16[8,2,32,384]{3,2,1,0:T(8,128)(2,1)S(1)} %bitcast.22), channel_id=1, source_target_pairs={{0,1},{1,0},{2,3},{3,2},{4,5},{5,4},{6,7},{7,6},{8,9},{9,8},{10,11... | collective-permute-start | bytes 1179656 | tf_op jit(solution)/shard_map/ppermute | solution.py:726
  142.5 40.8 %collective-permute-start.27 = (bf16[512,1024]{1,0:T(8,128)(2,1)S(1)}, bf16[512,1024]{1,0:T(8,128)(2,1)}, u32[]{:S(2)}, u32[]{:S(2)}) collective-permute-start(bf16[512,1024]{1,0:T(8,128)(2,1)S(1)} %collective-permute-done.25.refs_6_), channel_id=1, source_target_pairs={{0,1},{1,0},{2,3},{3,2},{4,5},{5,4},{6,7},{7,6},{8,9},{9,8},{10,11... | collective-permute-start | bytes 3145736 | tf_op jit(solution)/shard_map/ppermute | solution.py:726
  143.0 41.6 %collective-permute-start.31 = (bf16[256,2048]{1,0:T(8,128)(2,1)}, bf16[256,2048]{1,0:T(8,128)(2,1)}, u32[]{:S(2)}, u32[]{:S(2)}) collective-permute-start(bf16[256,2048]{1,0:T(8,128)(2,1)} %collective-permute-done.29.refs_10_), channel_id=1, source_target_pairs={{0,1},{1,0},{2,3},{3,2},{4,5},{5,4},{6,7},{7,6},{8,9},{9,8},{10,11... | collective-permute-start | bytes 3145736 | tf_op jit(solution)/shard_map/ppermute | solution.py:726
  161.3 26.4 %collective-permute-start.28 = (bf16[512,1024]{1,0:T(8,128)(2,1)}, bf16[512,1024]{1,0:T(8,128)(2,1)}, u32[]{:S(2)}, u32[]{:S(2)}) collective-permute-start(bf16[512,1024]{1,0:T(8,128)(2,1)} %collective-permute-done.26.refs_7_), channel_id=1, source_target_pairs={{0,1},{1,0},{2,3},{3,2},{4,5},{5,4},{6,7},{7,6},{8,9},{9,8},{10,11... | collective-permute-start | bytes 3145736 | tf_op jit(solution)/shard_map/ppermute | solution.py:726
  161.3 26.4 %collective-permute-start.32 = (bf16[256,2048]{1,0:T(8,128)(2,1)}, bf16[256,2048]{1,0:T(8,128)(2,1)}, u32[]{:S(2)}, u32[]{:S(2)}) collective-permute-start(bf16[256,2048]{1,0:T(8,128)(2,1)} %collective-permute-done.30.refs_11_), channel_id=1, source_target_pairs={{0,1},{1,0},{2,3},{3,2},{4,5},{5,4},{6,7},{7,6},{8,9},{9,8},{10,11... | collective-permute-start | bytes 3145736 | tf_op jit(solution)/shard_map/ppermute | solution.py:726
  163.7 0.7 copy-start.8
  164.4 11.1 %all-to-all-start.2 = ((bf16[8,64,128]{2,1,0:T(8,128)(2,1)}), bf16[8,64,128]{2,1,0:T(8,128)(2,1)S(1)}, u32[]{:S(2)}, u32[]{:S(2)}) async-start(bf16[8,64,128]{2,1,0:T(8,128)(2,1)} %bitcast.26), calls=%async_computation.2 | async-start | bytes 262144 | tf_op jit(solution)/shard_map/all_to_all | solution.py:732
  168.1 15.0 %copy-start.6 = (f32[32,2048]{1,0:T(8,128)S(1)}, f32[32,2048]{1,0:T(8,128)}, u32[]{:S(2)}) copy-start(f32[32,2048]{1,0:T(8,128)} %copy-done.5) | copy-start | bytes 786436
  175.5 18.7 %copy-start = (bf16[2048,1024]{1,0:T(8,128)(2,1)S(1)}, bf16[2048,1024]{1,0:T(8,128)(2,1)}, u32[]{:S(2)}) copy-start(bf16[2048,1024]{1,0:T(8,128)(2,1)} %refs_4_.1) | copy-start | bytes 12582916
  178.1 5.0 %collective-permute-start.21 = (bf16[32,2048]{1,0:T(8,128)(2,1)S(1)}, bf16[32,2048]{1,0:T(8,128)(2,1)S(1)}, u32[]{:S(2)}, u32[]{:S(2)}) collective-permute-start(bf16[32,2048]{1,0:T(8,128)(2,1)S(1)} %get-tuple-element.45), channel_id=1, source_target_pairs={{0,2},{1,3},{2,0},{3,1},{4,6},{5,7},{6,4},{7,5},{8,10},{9,11},{10,... | collective-permute-start | bytes 393224 | tf_op jit(solution)/shard_map/ppermute | solution.py:729
  183.3 7.1 %collective-permute-start.22 = (bf16[32,2048]{1,0:T(8,128)(2,1)S(1)}, bf16[32,2048]{1,0:T(8,128)(2,1)S(1)}, u32[]{:S(2)}, u32[]{:S(2)}) collective-permute-start(bf16[32,2048]{1,0:T(8,128)(2,1)S(1)} %get-tuple-element.47.refs_0_), channel_id=1, source_target_pairs={{0,8},{4,12},{8,0},{12,4},{16,24},{20,28},{24,16},{28,20},{1,9},{5... | collective-permute-start | bytes 393224 | tf_op jit(solution)/shard_map/ppermute | solution.py:737
  183.3 10.9 %collective-permute-start.23 = (bf16[32,2048]{1,0:T(8,128)(2,1)S(1)}, bf16[32,2048]{1,0:T(8,128)(2,1)S(1)}, u32[]{:S(2)}, u32[]{:S(2)}) collective-permute-start(bf16[32,2048]{1,0:T(8,128)(2,1)S(1)} %get-tuple-element.47.refs_0_), channel_id=1, source_target_pairs={{0,16},{4,20},{8,24},{12,28},{16,0},{20,4},{24,8},{28,12},{1,17},{... | collective-permute-start | bytes 393224 | tf_op jit(solution)/shard_map/ppermute | solution.py:737
  184.6 9.6 %collective-permute-start.24 = (bf16[32,2048]{1,0:T(8,128)(2,1)S(1)}, bf16[32,2048]{1,0:T(8,128)(2,1)S(1)}, u32[]{:S(2)}, u32[]{:S(2)}) collective-permute-start(bf16[32,2048]{1,0:T(8,128)(2,1)S(1)} %get-tuple-element.47.refs_0_), channel_id=1, source_target_pairs={{0,24},{4,28},{8,16},{12,20},{16,8},{20,12},{24,0},{28,4},{1,25},{... | collective-permute-start | bytes 393224 | tf_op jit(solution)/shard_map/ppermute | solution.py:737
  201.9 7.7 %collective-permute-start.33 = (bf16[32,2048]{1,0:T(8,128)(2,1)S(1)}, bf16[32,2048]{1,0:T(8,128)(2,1)S(1)}, u32[]{:S(2)}, u32[]{:S(2)}) collective-permute-start(bf16[32,2048]{1,0:T(8,128)(2,1)S(1)} %get-tuple-element.50), channel_id=1, source_target_pairs={{0,8},{4,12},{8,0},{12,4},{16,24},{20,28},{24,16},{28,20},{1,9},{5... | collective-permute-start | bytes 393224 | tf_op jit(solution)/shard_map/ppermute | solution.py:737
  203.9 10.5 %collective-permute-start.34 = (bf16[32,2048]{1,0:T(8,128)(2,1)S(1)}, bf16[32,2048]{1,0:T(8,128)(2,1)S(1)}, u32[]{:S(2)}, u32[]{:S(2)}) collective-permute-start(bf16[32,2048]{1,0:T(8,128)(2,1)S(1)} %get-tuple-element.51), channel_id=1, source_target_pairs={{0,16},{4,20},{8,24},{12,28},{16,0},{20,4},{24,8},{28,12},{1,17},{... | collective-permute-start | bytes 393224 | tf_op jit(solution)/shard_map/ppermute | solution.py:737
  204.1 10.4 %collective-permute-start.35 = (bf16[32,2048]{1,0:T(8,128)(2,1)S(1)}, bf16[32,2048]{1,0:T(8,128)(2,1)S(1)}, u32[]{:S(2)}, u32[]{:S(2)}) collective-permute-start(bf16[32,2048]{1,0:T(8,128)(2,1)S(1)} %get-tuple-element.52), channel_id=1, source_target_pairs={{0,24},{4,28},{8,16},{12,20},{16,8},{20,12},{24,0},{28,4},{1,25},{... | collective-permute-start | bytes 393224 | tf_op jit(solution)/shard_map/ppermute | solution.py:737

commit v6 on v5

--- a/solution.py
+++ b/solution.py
@@ -250,7 +250,7 @@
             bytes_accessed=count * rows * width * 2,
             transcendentals=0,
         ),
-        compiler_params=pltpu.CompilerParams(vmem_limit_bytes=20 * MIB),
+        compiler_params=pltpu.CompilerParams(vmem_limit_bytes=12 * MIB),
         name="context_rows",
     )(ids[:, None, :], *tables, table)
 
@@ -619,17 +619,26 @@
 
 
 def gather_kernel(step, scalars_ref, *refs):
-    *block_refs, out_ref = refs
-    for distance, block_ref in enumerate(block_refs):
-        out_ref[lax.div(scalars_ref[2], step) ^ distance] = block_ref[...]
+    *block_refs, out_ref, loaded = refs
+    loads = [
+        pltpu.make_async_copy(
+            block_ref, out_ref.at[lax.div(scalars_ref[2], step) ^ distance], loaded.at[distance]
+        )
+        for distance, block_ref in enumerate(block_refs)
+    ]
+    for load in loads:
+        load.start()
+    for load in loads:
+        load.wait()
 
 
 def gather_blocks(scalars, blocks, step):
     return pl.pallas_call(
         lambda *refs: gather_kernel(step, *refs),
-        in_specs=[IN_SMEM] + [IN_VMEM] * len(blocks),
+        in_specs=[IN_SMEM] + [ANYWHERE] * len(blocks),
         out_specs=IN_VMEM,
         out_shape=jax.ShapeDtypeStruct((len(blocks), *blocks[0].shape), blocks[0].dtype),
+        scratch_shapes=[pltpu.SemaphoreType.DMA((len(blocks),))],
         compiler_params=pltpu.CompilerParams(vmem_limit_bytes=4 * MIB),
         name="gather_blocks",
     )(scalars, *blocks)
@@ -793,6 +802,7 @@
     tiles = half_blocks * pieces
     context = context_rows(own_ids.reshape(-1, step), 0, tables, embed_table, owners)
     latent = context_rows(latent_ids.reshape(-1, step), tiles, tables, embed_table, owners)
+    arrived = [arrived[0], *map(in_hbm, arrived[1:])]
     arrived = gather_blocks(scalars, arrived, 1)
     arrived_other = swap(arrived)
     pairs, queries, kept_latent = context_heads(

time: 216 us -> 217 us (level)
    unnamed x24 -> x38, local copies, waits for them, and re-layouts: 4.92 us -> 4.95 us
  transfers between devices with their start and end apart: 39 -> 39, of which waited for: 17 -> 16; matrix products, arithmetic and copies ran while one was open for 2% -> 2% of each run, Pallas kernels for 19% -> 19%
where the time goes in v6:
time: 217 us; the launch traced here: 216 us
  waiting for transfers between devices  99.4 us (46%)
  starting transfers between devices  56.5 us (26%)
  Pallas kernels  49.4 us (23%)
  local copies, waits for them, and re-layouts  7.61 us (4%)
  other arithmetic  2.36 us (1%)
    all_to_all x3, waiting for transfers between devices, exchange(): return lax.all_to_all(value, 'ctx', 0, 0, tiled=True)  38.5 us
    ppermute x19, starting transfers between devices, across(): lax.ppermute(value, 'ctx', [(i, i ^ distance) for i in range(owners)])  36.6 us
    ppermute x19, waiting for transfers between devices, across(): lax.ppermute(value, 'ctx', [(i, i ^ distance) for i in range(owners)])  33.8 us
    ppermute x5, waiting for transfers between devices, cross(): return lax.ppermute(value, 'lat', [(i, i ^ 2) for i in range(groups)])  25.2 us
    all_to_all x3, starting transfers between devices, exchange(): return lax.all_to_all(value, 'ctx', 0, 0, tiled=True)  10.4 us
    pallas_call x2, Pallas kernels, context_rows(): pl.pallas_call(lambda *refs: context_kernel(owners, first, *refs), grid=(...  10.1 us
    pallas_call x1, Pallas kernels, mlp_shares(): pl.pallas_call(mlp_kernel, in_specs=[IN_SMEM] + [IN_VMEM] * (len(blocks)...  7.65 us
    pallas_call x2, Pallas kernels, head_attention(): pl.pallas_call(lambda *refs: attention_kernel(key_tile, shifted, *refs),...  7.3 us
  transfers between devices with their start and end apart: 39, of which 16 were waited for; matrix products, arithmetic and copies ran while one was open for 2% of the time, Pallas kernels for 19%

profile of v6, /device:TPU:0, one launch (start us, length us, event | category | flops | bytes accessed | tf_op | source)
XLA Modules:
  0.0 216.3 jit_solution(4785949487777643838)
XLA Ops:
  1.2 3.0 %prepare_weights.1 = (bf16[4,128,384]{2,1,0:T(8,128)(2,1)S(1)}, bf16[4,128,384]{2,1,0:T(8,128)(2,1)S(1)}, bf16[512,1024]{1,0:T(8,128)(2,1)}) custom-call(s32[5]{0:T(128)S(1)} %stack.28.refs_0_.scalars_ref, bf16[256,512]{1,0:T(8,128)(2,1)} %query_hbm.1, bf16[2,256,512]{2,1,0:T(8,128)(2,1)} %pair_hbm.1, bf16[2048,1024]{1,0:T(8,128)(2,1)} %refs_4_.1), custom_call_target="tpu_custom_call" | custom-call | tf_op jit(solution)/shard_map/prepare_weights/pallas_call | solution.py:406
  4.4 3.0 %collective-permute-start = (s32[1,4,128]{2,1,0:T(4,128)S(1)}, s32[1,4,128]{2,1,0:T(4,128)S(1)}, u32[]{:S(2)}, u32[]{:S(2)}) collective-permute-start(s32[1,4,128]{2,1,0:T(4,128)S(1)} %bitcast.32), channel_id=1, source_target_pairs={{0,4},{4,0},{8,12},{12,8},{16,20},{20,16},{24,28},{28,24},{1,5},{5... | collective-permute-start | bytes 6152 | tf_op jit(solution)/shard_map/ppermute | solution.py:746
  7.3 1.5 collective-permute-start.16
  9.1 1.9 collective-permute-done.4.theirs_ref
  11.1 0.7 order_blocks.1
  11.8 5.0 %collective-permute-start.10 = (bf16[128,384]{1,0:T(8,128)(2,1)S(1)}, bf16[128,384]{1,0:T(8,128)(2,1)S(1)}, u32[]{:S(2)}, u32[]{:S(2)}) collective-permute-start(bf16[128,384]{1,0:T(8,128)(2,1)S(1)} %get-tuple-element.37), channel_id=1, source_target_pairs={{0,24},{4,28},{8,16},{12,20},{16,8},{20,12},{24,0},{28,4},{1,25},{... | collective-permute-start | bytes 294920 | tf_op jit(solution)/shard_map/ppermute | solution.py:746
  16.8 1.1 collective-permute-start.11
  18.4 1.6 collective-permute-done.10.refs_7_
  20.0 3.7 %collective-permute-start.6 = (bf16[128,384]{1,0:T(8,128)(2,1)S(1)}, bf16[128,384]{1,0:T(8,128)(2,1)S(1)}, u32[]{:S(2)}, u32[]{:S(2)}) collective-permute-start(bf16[128,384]{1,0:T(8,128)(2,1)S(1)} %get-tuple-element.33), channel_id=1, source_target_pairs={{0,8},{4,12},{8,0},{12,4},{16,24},{20,28},{24,16},{28,20},{1,9},{5... | collective-permute-start | bytes 294920 | tf_op jit(solution)/shard_map/ppermute | solution.py:746
  23.7 0.5 collective-permute-done.11.refs_8_
  24.2 2.6 %collective-permute-start.7 = (bf16[128,384]{1,0:T(8,128)(2,1)S(1)}, bf16[128,384]{1,0:T(8,128)(2,1)S(1)}, u32[]{:S(2)}, u32[]{:S(2)}) collective-permute-start(bf16[128,384]{1,0:T(8,128)(2,1)S(1)} %get-tuple-element.34), channel_id=1, source_target_pairs={{0,12},{4,8},{8,4},{12,0},{16,28},{20,24},{24,20},{28,16},{1,13},{... | collective-permute-start | bytes 294920 | tf_op jit(solution)/shard_map/ppermute | solution.py:746
  26.8 0.8 collective-permute-start.1
  27.7 3.2 %collective-permute-start.8 = (bf16[128,384]{1,0:T(8,128)(2,1)S(1)}, bf16[128,384]{1,0:T(8,128)(2,1)S(1)}, u32[]{:S(2)}, u32[]{:S(2)}) collective-permute-start(bf16[128,384]{1,0:T(8,128)(2,1)S(1)} %get-tuple-element.35), channel_id=1, source_target_pairs={{0,16},{4,20},{8,24},{12,28},{16,0},{20,4},{24,8},{28,12},{1,17},{... | collective-permute-start | bytes 294920 | tf_op jit(solution)/shard_map/ppermute | solution.py:746
  30.8 3.5 %collective-permute-start.9 = (bf16[128,384]{1,0:T(8,128)(2,1)S(1)}, bf16[128,384]{1,0:T(8,128)(2,1)S(1)}, u32[]{:S(2)}, u32[]{:S(2)}) collective-permute-start(bf16[128,384]{1,0:T(8,128)(2,1)S(1)} %get-tuple-element.36), channel_id=1, source_target_pairs={{0,20},{4,16},{8,28},{12,24},{16,4},{20,0},{24,12},{28,8},{1,21},{... | collective-permute-start | bytes 294920 | tf_op jit(solution)/shard_map/ppermute | solution.py:746
  34.4 3.3 %collective-permute-done.8.refs_5_ = bf16[128,384]{1,0:T(8,128)(2,1)S(1)} collective-permute-done((bf16[128,384]{1,0:T(8,128)(2,1)S(1)}, bf16[128,384]{1,0:T(8,128)(2,1)S(1)}, u32[]{:S(2)}, u32[]{:S(2)}) %collective-permute-start.8) | collective-permute-done | bytes 98336 | tf_op jit(solution)/shard_map/ppermute | solution.py:746
  37.7 2.2 collective-permute-done.9.refs_6_
  39.8 2.2 %collective-permute-start.3 = (s32[2,4,128]{2,1,0:T(4,128)S(1)}, s32[2,4,128]{2,1,0:T(4,128)S(1)}, u32[]{:S(2)}, u32[]{:S(2)}) collective-permute-start(s32[2,4,128]{2,1,0:T(4,128)S(1)} %pad_add_fusion.refs_1_), channel_id=1, source_target_pairs={{0,24},{4,28},{8,16},{12,20},{16,8},{20,12},{24,0},{28,4},{1,25},{... | collective-permute-start | bytes 12296 | tf_op jit(solution)/shard_map/ppermute | solution.py:746
  42.1 1.9 gather_blocks.3.refs_3_
  44.1 1.4 fusion.4
  45.6 0.6 collective-permute-start.15
  46.1 0.6 gather_blocks.2
  46.9 7.7 %context_rows.2.refs_1_ = bf16[2048,2048]{1,0:T(8,128)(2,1)S(1)} custom-call(s32[8,1,256]{2,1,0:T(1,128)S(1)} %bitcast.28, f32[16,2048]{1,0:T(8,128)S(1)} %get-tuple-element.63.refs_1_, f32[16,2048]{1,0:T(8,128)S(1)} %get-tuple-element.64.refs_2_, f32[16,2048]{1,0:T(8,128)S(1)} %get-tuple-element.61.refs_3_, f32[16,2048]{1,0:T(8,128)S(1)} %get-tuple-element.62.refs_4_, ...), custom_call_target="tpu_custom_call" | custom-call | flops 2147483648 | bytes 8388608 | tf_op jit(solution)/shard_map/context_rows/pallas_call | solution.py:240
  54.6 2.4 %context_rows.3.refs_2_ = bf16[512,2048]{1,0:T(8,128)(2,1)S(1)} custom-call(s32[2,1,256]{2,1,0:T(1,128)S(1)} %broadcast_in_dim.30.refs_0_, f32[16,2048]{1,0:T(8,128)S(1)} %get-tuple-element.63.refs_1_, f32[16,2048]{1,0:T(8,128)S(1)} %get-tuple-element.64.refs_2_, f32[16,2048]{1,0:T(8,128)S(1)} %get-tuple-element.61.refs_3_, ...), custom_call_target="tpu_custom_call" | custom-call | flops 536870912 | bytes 2097152 | tf_op jit(solution)/shard_map/context_rows/pallas_call | solution.py:240
  57.1 4.0 %context_heads.1 = (bf16[2048,256]{1,0:T(8,128)(2,1)}, bf16[8,2,32,128]{3,2,1,0:T(8,128)(2,1)S(1)}, bf16[64,2048]{1,0:T(8,128)(2,1)S(1)}) custom-call(s32[5]{0:T(128)S(1)} %stack.28.refs_0_.scalars_ref, bf16[2048,2048]{1,0:T(8,128)(2,1)S(1)} %context_rows.2.refs_1_, bf16[512,2048]{1,0:T(8,128)(2,1)S(1)} %context_rows.3.refs_2_, ...), custom_call_target="tpu_custom_call" | custom-call | flops 2684354560 | bytes 8388608 | tf_op jit(solution)/shard_map/context_heads/pallas_call | solution.py:572
  61.2 0.7 copy-done.3
  62.3 0.6 collective-permute-start.25
  63.0 2.4 %constant_dynamic-slice_fusion = bf16[256,2048]{1,0:T(8,128)(2,1)} fusion(bf16[1024,2048]{1,0:T(8,128)(2,1)} %refs_5_.1, s32[]{:T(128)S(6)} %select_n.97), kind=kLoop, calls=%fused_computation.37 | loop fusion | bytes 2097156 | tf_op jit(solution)/shard_map/dynamic_slice | solution.py:750
  65.3 1.0 copy-done.9
  66.3 1.4 collective-permute-start.29
  67.7 1.2 copy-done.10
  68.9 5.4 %head_attention.2 = bf16[8,2,32,128]{3,2,1,0:T(8,128)(2,1)S(1)} custom-call(s32[5]{0:T(128)S(1)} %stack.28.refs_0_.scalars_ref, bf16[8,2,32,128]{3,2,1,0:T(8,128)(2,1)S(1)} %get-tuple-element.39.refs_1_, bf16[1,4,512,256]{3,2,1,0:T(8,128)(2,1)} %bitcast.9.refs_2_, bf16[1,4,512,256]{3,2,1,0:T(8,128)(2,1)S(1)} %bitcast.29), custom_call_target="tpu_custom_call" | custom-call | flops 2147483648 | bytes 2097152 | tf_op jit(solution)/shard_map/head_attention/pallas_call | solution.py:301
  74.3 0.6 copy-done.7
  75.0 3.6 %all-to-all-start = ((bf16[8,64,128]{2,1,0:T(8,128)(2,1)}), bf16[8,64,128]{2,1,0:T(8,128)(2,1)S(1)}, u32[]{:S(2)}, u32[]{:S(2)}) async-start(bf16[8,64,128]{2,1,0:T(8,128)(2,1)} %bitcast.25), calls=%async_computation | async-start | bytes 262144 | tf_op jit(solution)/shard_map/all_to_all | solution.py:741
  78.5 11.1 %collective-permute-done.25.refs_6_ = bf16[512,1024]{1,0:T(8,128)(2,1)S(1)} collective-permute-done((bf16[512,1024]{1,0:T(8,128)(2,1)}, bf16[512,1024]{1,0:T(8,128)(2,1)S(1)}, u32[]{:S(2)}, u32[]{:S(2)}) %collective-permute-start.25) | collective-permute-done | bytes 1048608 | tf_op jit(solution)/shard_map/ppermute | solution.py:746
  89.6 21.9 %all-to-all-done.heads_ref = bf16[8,64,128]{2,1,0:T(8,128)(2,1)S(1)} async-done(((bf16[8,64,128]{2,1,0:T(8,128)(2,1)}), bf16[8,64,128]{2,1,0:T(8,128)(2,1)S(1)}, u32[]{:S(2)}, u32[]{:S(2)}) %all-to-all-start) | async-done | bytes 131104 | tf_op jit(solution)/shard_map/all_to_all | solution.py:741
  111.5 1.5 collective-permute-start.14
  113.0 3.4 %collective-permute-done.14.came_ref = bf16[8,64,128]{2,1,0:T(8,128)(2,1)S(1)} collective-permute-done((bf16[8,64,128]{2,1,0:T(8,128)(2,1)S(1)}, bf16[8,64,128]{2,1,0:T(8,128)(2,1)S(1)}, u32[]{:S(2)}, u32[]{:S(2)}) %collective-permute-start.14) | collective-permute-done | bytes 131104 | tf_op jit(solution)/shard_map/ppermute | solution.py:738
  116.5 1.5 collective-permute-start.26
  118.0 4.6 %stream_rows.1 = (f32[32,2048]{1,0:T(8,128)S(1)}, bf16[64,2048]{1,0:T(8,128)(2,1)S(1)}) custom-call(s32[5]{0:T(128)S(1)} %stack.28.refs_0_.scalars_ref, bf16[8,64,128]{2,1,0:T(8,128)(2,1)S(1)} %all-to-all-done.heads_ref, bf16[8,64,128]{2,1,0:T(8,128)(2,1)S(1)} %collective-permute-done.14.came_ref, bf16[64,2048]{1,0:T(8,128)(2,1)S(1)} %copy-done.4, ...), custom_call_target="tpu_custom_call" | custom-call | flops 536870912 | bytes 8388608 | tf_op jit(solution)/shard_map/stream_rows/pallas_call | solution.py:350
  122.7 0.7 copy-done.5
  123.4 6.7 %triple_heads.1 = bf16[8,64,384]{2,1,0:T(8,128)(2,1)} custom-call(s32[5]{0:T(128)S(1)} %stack.28.refs_0_.scalars_ref, bf16[64,2048]{1,0:T(8,128)(2,1)S(1)} %get-tuple-element.43.refs_1_, bf16[3,2048,512]{2,1,0:T(8,128)(2,1)} %refs_2_.1, bf16[3,2048,512]{2,1,0:T(8,128)(2,1)} %collective-permute-done.18.refs_3_), custom_call_target="tpu_custom_call" | custom-call | flops 805306368 | bytes 12582912 | tf_op jit(solution)/shard_map/triple_heads/pallas_call | solution.py:489
  130.1 3.5 %all-to-all-start.1 = ((bf16[8,64,384]{2,1,0:T(8,128)(2,1)}), bf16[8,64,384]{2,1,0:T(8,128)(2,1)S(1)}, u32[]{:S(2)}, u32[]{:S(2)}) async-start(bf16[8,64,384]{2,1,0:T(8,128)(2,1)} %triple_heads.1), calls=%async_computation.1 | async-start | bytes 786432 | tf_op jit(solution)/shard_map/all_to_all | solution.py:741
  133.5 0.6 collective-permute-start.30
  134.1 9.3 %all-to-all-done.1 = bf16[8,64,384]{2,1,0:T(8,128)(2,1)S(1)} async-done(((bf16[8,64,384]{2,1,0:T(8,128)(2,1)}), bf16[8,64,384]{2,1,0:T(8,128)(2,1)S(1)}, u32[]{:S(2)}, u32[]{:S(2)}) %all-to-all-start.1) | async-done | bytes 393248 | tf_op jit(solution)/shard_map/all_to_all | solution.py:741
  143.4 0.5 collective-permute-start.27
  143.9 18.3 %collective-permute-done.30.refs_11_ = bf16[256,2048]{1,0:T(8,128)(2,1)} collective-permute-done((bf16[256,2048]{1,0:T(8,128)(2,1)}, bf16[256,2048]{1,0:T(8,128)(2,1)}, u32[]{:S(2)}, u32[]{:S(2)}) %collective-permute-start.30) | collective-permute-done | bytes 1048608 | tf_op jit(solution)/shard_map/ppermute | solution.py:738
  162.2 0.5 collective-permute-start.32
  162.8 1.9 head_attention.3
  164.7 0.6 copy-done.8
  165.4 3.4 %all-to-all-start.2 = ((bf16[8,64,128]{2,1,0:T(8,128)(2,1)}), bf16[8,64,128]{2,1,0:T(8,128)(2,1)S(1)}, u32[]{:S(2)}, u32[]{:S(2)}) async-start(bf16[8,64,128]{2,1,0:T(8,128)(2,1)} %bitcast.26), calls=%async_computation.2 | async-start | bytes 262144 | tf_op jit(solution)/shard_map/all_to_all | solution.py:741
  168.8 7.3 %all-to-all-done.2.heads_ref = bf16[8,64,128]{2,1,0:T(8,128)(2,1)S(1)} async-done(((bf16[8,64,128]{2,1,0:T(8,128)(2,1)}), bf16[8,64,128]{2,1,0:T(8,128)(2,1)S(1)}, u32[]{:S(2)}, u32[]{:S(2)}) %all-to-all-start.2) | async-done | bytes 131104 | tf_op jit(solution)/shard_map/all_to_all | solution.py:741
  176.1 2.6 %project_rows.1 = (f32[32,2048]{1,0:T(8,128)S(1)}, bf16[32,2048]{1,0:T(8,128)(2,1)S(1)}) custom-call(s32[5]{0:T(128)S(1)} %stack.28.refs_0_.scalars_ref, bf16[8,64,128]{2,1,0:T(8,128)(2,1)S(1)} %all-to-all-done.2.heads_ref, bf16[512,2048]{1,0:T(8,128)(2,1)S(1)} %copy-done.2, bf16[512,2048]{1,0:T(8,128)(2,1)} %collective-permute-done.20.theirs_ref), custom_call_target="tpu_custom_call" | custom-call | flops 268435456 | bytes 4194304 | tf_op jit(solution)/shard_map/project_rows/pallas_call | solution.py:442
  178.7 1.6 collective-permute-start.21
  180.3 3.4 %collective-permute-done.21.came_ref = bf16[32,2048]{1,0:T(8,128)(2,1)S(1)} collective-permute-done((bf16[32,2048]{1,0:T(8,128)(2,1)S(1)}, bf16[32,2048]{1,0:T(8,128)(2,1)S(1)}, u32[]{:S(2)}, u32[]{:S(2)}) %collective-permute-start.21) | collective-permute-done | bytes 131104 | tf_op jit(solution)/shard_map/ppermute | solution.py:738
  184.0 1.0 collective-permute-start.23
  185.0 3.3 %collective-permute-start.24 = (bf16[32,2048]{1,0:T(8,128)(2,1)S(1)}, bf16[32,2048]{1,0:T(8,128)(2,1)S(1)}, u32[]{:S(2)}, u32[]{:S(2)}) collective-permute-start(bf16[32,2048]{1,0:T(8,128)(2,1)S(1)} %get-tuple-element.47.refs_0_), channel_id=1, source_target_pairs={{0,24},{4,28},{8,16},{12,20},{16,8},{20,12},{24,0},{28,4},{1,25},{... | collective-permute-start | bytes 393224 | tf_op jit(solution)/shard_map/ppermute | solution.py:746
  188.4 2.7 %collective-permute-done.22.refs_1_ = bf16[32,2048]{1,0:T(8,128)(2,1)S(1)} collective-permute-done((bf16[32,2048]{1,0:T(8,128)(2,1)S(1)}, bf16[32,2048]{1,0:T(8,128)(2,1)S(1)}, u32[]{:S(2)}, u32[]{:S(2)}) %collective-permute-start.22) | collective-permute-done | bytes 131104 | tf_op jit(solution)/shard_map/ppermute | solution.py:746
  191.0 4.0 %collective-permute-done.23.refs_2_ = bf16[32,2048]{1,0:T(8,128)(2,1)S(1)} collective-permute-done((bf16[32,2048]{1,0:T(8,128)(2,1)S(1)}, bf16[32,2048]{1,0:T(8,128)(2,1)S(1)}, u32[]{:S(2)}, u32[]{:S(2)}) %collective-permute-start.23) | collective-permute-done | bytes 131104 | tf_op jit(solution)/shard_map/ppermute | solution.py:746
  195.0 7.7 %mlp_shares.1 = (f32[32,2048]{1,0:T(8,128)S(1)}, bf16[32,2048]{1,0:T(8,128)(2,1)S(1)}, bf16[32,2048]{1,0:T(8,128)(2,1)S(1)}, bf16[32,2048]{1,0:T(8,128)(2,1)S(1)}) custom-call(s32[5]{0:T(128)S(1)} %stack.28.refs_0_.scalars_ref, bf16[32,2048]{1,0:T(8,128)(2,1)S(1)} %get-tuple-element.47.refs_0_, bf16[32,2048]{1,0:T(8,128)(2,1)S(1)} %collective-permute-done.22.refs_1_, ...), custom_call_target="tpu_custom_call" | custom-call | flops 2147483648 | bytes 16777216 | tf_op jit(solution)/shard_map/mlp_shares/pallas_call | solution.py:683
  202.7 2.0 collective-permute-start.33
  205.1 2.1 collective-permute-start.35
  207.2 1.4 collective-permute-done.33
  208.6 6.9 %collective-permute-done.34 = bf16[32,2048]{1,0:T(8,128)(2,1)S(1)} collective-permute-done((bf16[32,2048]{1,0:T(8,128)(2,1)S(1)}, bf16[32,2048]{1,0:T(8,128)(2,1)S(1)}, u32[]{:S(2)}, u32[]{:S(2)}) %collective-permute-start.34) | collective-permute-done | bytes 131104 | tf_op jit(solution)/shard_map/ppermute | solution.py:746
  215.6 0.7 fusion.3
  (87 shorter events, 2.9 us)
Async XLA Ops:
  0.0 123.4 %collective-permute-start.18 = (bf16[3,2048,512]{2,1,0:T(8,128)(2,1)}, bf16[3,2048,512]{2,1,0:T(8,128)(2,1)}, u32[]{:S(2)}, u32[]{:S(2)}) collective-permute-start(bf16[3,2048,512]{2,1,0:T(8,128)(2,1)} %refs_2_.1), channel_id=1, source_target_pairs={{0,1},{1,0},{2,3},{3,2},{4,5},{5,4},{6,7},{7,6},{8,9},{9,8},{10,11... | collective-permute-start | bytes 18874376 | tf_op jit(solution)/shard_map/ppermute | solution.py:735
  1.2 3.1 %copy-start.18 = (s32[512]{0:T(512)S(1)}, s32[512]{0:T(512)}, u32[]{:S(2)}) copy-start(s32[512]{0:T(512)} %param.10) | copy-start | bytes 6148
  4.3 42.6 %copy-start.1 = (bf16[256,2048]{1,0:T(8,128)(2,1)S(1)}, bf16[256,2048]{1,0:T(8,128)(2,1)}, u32[]{:S(2)}) copy-start(bf16[256,2048]{1,0:T(8,128)(2,1)} %refs_7_.3) | copy-start | bytes 3145732
  4.3 6.8 %collective-permute-start.4 = (bf16[4,128,384]{2,1,0:T(8,128)(2,1)S(1)}, bf16[4,128,384]{2,1,0:T(8,128)(2,1)S(1)}, u32[]{:S(2)}, u32[]{:S(2)}) collective-permute-start(bf16[4,128,384]{2,1,0:T(8,128)(2,1)S(1)} %get-tuple-element.30), channel_id=1, source_target_pairs={{0,1},{1,0},{2,3},{3,2},{4,5},{5,4},{6,7},{7,6},{8,9},{9,8},{10,11... | collective-permute-start | bytes 1179656 | tf_op jit(solution)/shard_map/ppermute | solution.py:735
  4.4 13.6 %collective-permute-start = (s32[1,4,128]{2,1,0:T(4,128)S(1)}, s32[1,4,128]{2,1,0:T(4,128)S(1)}, u32[]{:S(2)}, u32[]{:S(2)}) collective-permute-start(s32[1,4,128]{2,1,0:T(4,128)S(1)} %bitcast.32), channel_id=1, source_target_pairs={{0,4},{4,0},{8,12},{12,8},{16,20},{20,16},{24,28},{28,24},{1,5},{5... | collective-permute-start | bytes 6152 | tf_op jit(solution)/shard_map/ppermute | solution.py:746
  7.3 49.7 %collective-permute-start.16 = (bf16[512,2048]{1,0:T(8,128)(2,1)}, bf16[512,2048]{1,0:T(8,128)(2,1)}, u32[]{:S(2)}, u32[]{:S(2)}) collective-permute-start(bf16[512,2048]{1,0:T(8,128)(2,1)} %refs_0_.1), channel_id=1, source_target_pairs={{0,2},{1,3},{2,0},{3,1},{4,6},{5,7},{6,4},{7,5},{8,10},{9,11},{10,... | collective-permute-start | bytes 6291464 | tf_op jit(solution)/shard_map/ppermute | solution.py:738
  11.8 8.3 %collective-permute-start.10 = (bf16[128,384]{1,0:T(8,128)(2,1)S(1)}, bf16[128,384]{1,0:T(8,128)(2,1)S(1)}, u32[]{:S(2)}, u32[]{:S(2)}) collective-permute-start(bf16[128,384]{1,0:T(8,128)(2,1)S(1)} %get-tuple-element.37), channel_id=1, source_target_pairs={{0,24},{4,28},{8,16},{12,20},{16,8},{20,12},{24,0},{28,4},{1,25},{... | collective-permute-start | bytes 294920 | tf_op jit(solution)/shard_map/ppermute | solution.py:746
  16.8 7.5 %collective-permute-start.11 = (bf16[128,384]{1,0:T(8,128)(2,1)S(1)}, bf16[128,384]{1,0:T(8,128)(2,1)S(1)}, u32[]{:S(2)}, u32[]{:S(2)}) collective-permute-start(bf16[128,384]{1,0:T(8,128)(2,1)S(1)} %get-tuple-element.38), channel_id=1, source_target_pairs={{0,28},{4,24},{8,20},{12,16},{16,12},{20,8},{24,4},{28,0},{1,29},{... | collective-permute-start | bytes 294920 | tf_op jit(solution)/shard_map/ppermute | solution.py:746
  17.9 8.9 %collective-permute-start.5 = (bf16[128,384]{1,0:T(8,128)(2,1)S(1)}, bf16[128,384]{1,0:T(8,128)(2,1)S(1)}, u32[]{:S(2)}, u32[]{:S(2)}) collective-permute-start(bf16[128,384]{1,0:T(8,128)(2,1)S(1)} %get-tuple-element.32), channel_id=1, source_target_pairs={{0,4},{4,0},{8,12},{12,8},{16,20},{20,16},{24,28},{28,24},{1,5},{5... | collective-permute-start | bytes 294920 | tf_op jit(solution)/shard_map/ppermute | solution.py:746
  20.0 22.0 %copy-start.11 = (bf16[128,384]{1,0:T(8,128)(2,1)}, bf16[128,384]{1,0:T(8,128)(2,1)S(1)}, u32[]{:S(2)}) copy-start(bf16[128,384]{1,0:T(8,128)(2,1)S(1)} %collective-permute-done.10.refs_7_) | copy-start | bytes 294916
  20.0 7.7 %collective-permute-start.6 = (bf16[128,384]{1,0:T(8,128)(2,1)S(1)}, bf16[128,384]{1,0:T(8,128)(2,1)S(1)}, u32[]{:S(2)}, u32[]{:S(2)}) collective-permute-start(bf16[128,384]{1,0:T(8,128)(2,1)S(1)} %get-tuple-element.33), channel_id=1, source_target_pairs={{0,8},{4,12},{8,0},{12,4},{16,24},{20,28},{24,16},{28,20},{1,9},{5... | collective-permute-start | bytes 294920 | tf_op jit(solution)/shard_map/ppermute | solution.py:746
  24.2 17.8 %copy-start.12 = (bf16[128,384]{1,0:T(8,128)(2,1)}, bf16[128,384]{1,0:T(8,128)(2,1)S(1)}, u32[]{:S(2)}) copy-start(bf16[128,384]{1,0:T(8,128)(2,1)S(1)} %collective-permute-done.11.refs_8_) | copy-start | bytes 294916
  24.2 6.6 %collective-permute-start.7 = (bf16[128,384]{1,0:T(8,128)(2,1)S(1)}, bf16[128,384]{1,0:T(8,128)(2,1)S(1)}, u32[]{:S(2)}, u32[]{:S(2)}) collective-permute-start(bf16[128,384]{1,0:T(8,128)(2,1)S(1)} %get-tuple-element.34), channel_id=1, source_target_pairs={{0,12},{4,8},{8,4},{12,0},{16,28},{20,24},{24,20},{28,16},{1,13},{... | collective-permute-start | bytes 294920 | tf_op jit(solution)/shard_map/ppermute | solution.py:746
  26.8 15.2 %copy-start.13 = (bf16[128,384]{1,0:T(8,128)(2,1)}, bf16[128,384]{1,0:T(8,128)(2,1)S(1)}, u32[]{:S(2)}) copy-start(bf16[128,384]{1,0:T(8,128)(2,1)S(1)} %collective-permute-done.5.refs_2_) | copy-start | bytes 294916
  26.8 17.2 %collective-permute-start.1 = (s32[2,4,128]{2,1,0:T(4,128)S(1)}, s32[2,4,128]{2,1,0:T(4,128)S(1)}, u32[]{:S(2)}, u32[]{:S(2)}) collective-permute-start(s32[2,4,128]{2,1,0:T(4,128)S(1)} %pad_add_fusion.refs_1_), channel_id=1, source_target_pairs={{0,8},{4,12},{8,0},{12,4},{16,24},{20,28},{24,16},{28,20},{1,9},{5... | collective-permute-start | bytes 12296 | tf_op jit(solution)/shard_map/ppermute | solution.py:746
  27.7 14.4 %copy-start.14 = (bf16[128,384]{1,0:T(8,128)(2,1)}, bf16[128,384]{1,0:T(8,128)(2,1)S(1)}, u32[]{:S(2)}) copy-start(bf16[128,384]{1,0:T(8,128)(2,1)S(1)} %collective-permute-done.6.refs_3_) | copy-start | bytes 294916
  27.7 10.0 %collective-permute-start.8 = (bf16[128,384]{1,0:T(8,128)(2,1)S(1)}, bf16[128,384]{1,0:T(8,128)(2,1)S(1)}, u32[]{:S(2)}, u32[]{:S(2)}) collective-permute-start(bf16[128,384]{1,0:T(8,128)(2,1)S(1)} %get-tuple-element.35), channel_id=1, source_target_pairs={{0,16},{4,20},{8,24},{12,28},{16,0},{20,4},{24,8},{28,12},{1,17},{... | collective-permute-start | bytes 294920 | tf_op jit(solution)/shard_map/ppermute | solution.py:746
  30.8 11.2 %copy-start.15 = (bf16[128,384]{1,0:T(8,128)(2,1)}, bf16[128,384]{1,0:T(8,128)(2,1)S(1)}, u32[]{:S(2)}) copy-start(bf16[128,384]{1,0:T(8,128)(2,1)S(1)} %collective-permute-done.7.refs_4_) | copy-start | bytes 294916
  30.8 9.0 %collective-permute-start.9 = (bf16[128,384]{1,0:T(8,128)(2,1)S(1)}, bf16[128,384]{1,0:T(8,128)(2,1)S(1)}, u32[]{:S(2)}, u32[]{:S(2)}) collective-permute-start(bf16[128,384]{1,0:T(8,128)(2,1)S(1)} %get-tuple-element.36), channel_id=1, source_target_pairs={{0,20},{4,16},{8,28},{12,24},{16,4},{20,0},{24,12},{28,8},{1,21},{... | collective-permute-start | bytes 294920 | tf_op jit(solution)/shard_map/ppermute | solution.py:746
  37.6 4.4 %copy-start.16 = (bf16[128,384]{1,0:T(8,128)(2,1)}, bf16[128,384]{1,0:T(8,128)(2,1)S(1)}, u32[]{:S(2)}) copy-start(bf16[128,384]{1,0:T(8,128)(2,1)S(1)} %collective-permute-done.8.refs_5_) | copy-start | bytes 294916
  37.6 7.9 %collective-permute-start.2 = (s32[2,4,128]{2,1,0:T(4,128)S(1)}, s32[2,4,128]{2,1,0:T(4,128)S(1)}, u32[]{:S(2)}, u32[]{:S(2)}) collective-permute-start(s32[2,4,128]{2,1,0:T(4,128)S(1)} %pad_add_fusion.refs_1_), channel_id=1, source_target_pairs={{0,16},{4,20},{8,24},{12,28},{16,0},{20,4},{24,8},{28,12},{1,17},{... | collective-permute-start | bytes 12296 | tf_op jit(solution)/shard_map/ppermute | solution.py:746
  39.8 2.3 %copy-start.17 = (bf16[128,384]{1,0:T(8,128)(2,1)}, bf16[128,384]{1,0:T(8,128)(2,1)S(1)}, u32[]{:S(2)}) copy-start(bf16[128,384]{1,0:T(8,128)(2,1)S(1)} %collective-permute-done.9.refs_6_) | copy-start | bytes 294916
  39.8 6.3 %collective-permute-start.3 = (s32[2,4,128]{2,1,0:T(4,128)S(1)}, s32[2,4,128]{2,1,0:T(4,128)S(1)}, u32[]{:S(2)}, u32[]{:S(2)}) collective-permute-start(s32[2,4,128]{2,1,0:T(4,128)S(1)} %pad_add_fusion.refs_1_), channel_id=1, source_target_pairs={{0,24},{4,28},{8,16},{12,20},{16,8},{20,12},{24,0},{28,4},{1,25},{... | collective-permute-start | bytes 12296 | tf_op jit(solution)/shard_map/ppermute | solution.py:746
  44.0 13.1 %collective-permute-start.12 = (bf16[8,128,384]{2,1,0:T(8,128)(2,1)S(1)}, bf16[8,128,384]{2,1,0:T(8,128)(2,1)S(1)}, u32[]{:S(2)}, u32[]{:S(2)}) collective-permute-start(bf16[8,128,384]{2,1,0:T(8,128)(2,1)S(1)} %gather_blocks.3.refs_3_), channel_id=1, source_target_pairs={{0,1},{1,0},{2,3},{3,2},{4,5},{5,4},{6,7},{7,6},{8,9},{9,8},{10,11... | collective-permute-start | bytes 2359304 | tf_op jit(solution)/shard_map/ppermute | solution.py:735
  45.6 67.5 %collective-permute-start.15 = (bf16[512,2048]{1,0:T(8,128)(2,1)}, bf16[512,2048]{1,0:T(8,128)(2,1)}, u32[]{:S(2)}, u32[]{:S(2)}) collective-permute-start(bf16[512,2048]{1,0:T(8,128)(2,1)} %refs_0_.1), channel_id=1, source_target_pairs={{0,1},{1,0},{2,3},{3,2},{4,5},{5,4},{6,7},{7,6},{8,9},{9,8},{10,11... | collective-permute-start | bytes 6291464 | tf_op jit(solution)/shard_map/ppermute | solution.py:735
  57.0 61.0 %collective-permute-start.17 = (bf16[512,2048]{1,0:T(8,128)(2,1)}, bf16[512,2048]{1,0:T(8,128)(2,1)}, u32[]{:S(2)}, u32[]{:S(2)}) collective-permute-start(bf16[512,2048]{1,0:T(8,128)(2,1)} %collective-permute-done.16.refs_2_), channel_id=1, source_target_pairs={{0,1},{1,0},{2,3},{3,2},{4,5},{5,4},{6,7},{7,6},{8,9},{9,8},{10,11... | collective-permute-start | bytes 6291464 | tf_op jit(solution)/shard_map/ppermute | solution.py:735
  61.2 0.7 copy-start.3
  61.9 3.5 %collective-permute-start.13 = (bf16[2048,256]{1,0:T(8,128)(2,1)}, bf16[2048,256]{1,0:T(8,128)(2,1)S(1)}, u32[]{:S(2)}, u32[]{:S(2)}) collective-permute-start(bf16[2048,256]{1,0:T(8,128)(2,1)} %get-tuple-element.40), channel_id=1, source_target_pairs={{0,1},{1,0},{2,3},{3,2},{4,5},{5,4},{6,7},{7,6},{8,9},{9,8},{10,11... | collective-permute-start | bytes 3145736 | tf_op jit(solution)/shard_map/ppermute | solution.py:735
  62.3 27.3 %collective-permute-start.25 = (bf16[512,1024]{1,0:T(8,128)(2,1)}, bf16[512,1024]{1,0:T(8,128)(2,1)S(1)}, u32[]{:S(2)}, u32[]{:S(2)}) collective-permute-start(bf16[512,1024]{1,0:T(8,128)(2,1)} %get-tuple-element.48), channel_id=1, source_target_pairs={{0,4},{4,0},{8,12},{12,8},{16,20},{20,16},{24,28},{28,24},{1,5},{5... | collective-permute-start | bytes 3145736 | tf_op jit(solution)/shard_map/ppermute | solution.py:746
  65.3 1.0 copy-start.9
  66.3 67.2 %collective-permute-start.29 = (bf16[256,2048]{1,0:T(8,128)(2,1)}, bf16[256,2048]{1,0:T(8,128)(2,1)}, u32[]{:S(2)}, u32[]{:S(2)}) collective-permute-start(bf16[256,2048]{1,0:T(8,128)(2,1)} %constant_dynamic-slice_fusion), channel_id=1, source_target_pairs={{0,4},{4,0},{8,12},{12,8},{16,20},{20,16},{24,28},{28,24},{1,5},{5... | collective-permute-start | bytes 3145736 | tf_op jit(solution)/shard_map/ppermute | solution.py:746
  67.7 1.2 copy-start.10
  68.9 44.1 %copy-start.2 = (bf16[512,2048]{1,0:T(8,128)(2,1)S(1)}, bf16[512,2048]{1,0:T(8,128)(2,1)}, u32[]{:S(2)}) copy-start(bf16[512,2048]{1,0:T(8,128)(2,1)} %mine_ref.1) | copy-start | bytes 6291460
  68.9 49.1 %copy-start.4 = (bf16[64,2048]{1,0:T(8,128)(2,1)S(1)}, bf16[64,2048]{1,0:T(8,128)(2,1)}, u32[]{:S(2)}) copy-start(bf16[64,2048]{1,0:T(8,128)(2,1)} %copy-done.3) | copy-start | bytes 786436
  74.3 0.7 copy-start.7
  75.0 36.5 %all-to-all-start = ((bf16[8,64,128]{2,1,0:T(8,128)(2,1)}), bf16[8,64,128]{2,1,0:T(8,128)(2,1)S(1)}, u32[]{:S(2)}, u32[]{:S(2)}) async-start(bf16[8,64,128]{2,1,0:T(8,128)(2,1)} %bitcast.25), calls=%async_computation | async-start | bytes 262144 | tf_op jit(solution)/shard_map/all_to_all | solution.py:741
  111.5 5.0 %collective-permute-start.14 = (bf16[8,64,128]{2,1,0:T(8,128)(2,1)S(1)}, bf16[8,64,128]{2,1,0:T(8,128)(2,1)S(1)}, u32[]{:S(2)}, u32[]{:S(2)}) collective-permute-start(bf16[8,64,128]{2,1,0:T(8,128)(2,1)S(1)} %all-to-all-done.heads_ref), channel_id=1, source_target_pairs={{0,2},{1,3},{2,0},{3,1},{4,6},{5,7},{6,4},{7,5},{8,10},{9,11},{10,... | collective-permute-start | bytes 393224 | tf_op jit(solution)/shard_map/ppermute | solution.py:738
  113.0 55.7 %collective-permute-start.20 = (bf16[512,2048]{1,0:T(8,128)(2,1)S(1)}, bf16[512,2048]{1,0:T(8,128)(2,1)}, u32[]{:S(2)}, u32[]{:S(2)}) collective-permute-start(bf16[512,2048]{1,0:T(8,128)(2,1)S(1)} %copy-done.2), channel_id=1, source_target_pairs={{0,1},{1,0},{2,3},{3,2},{4,5},{5,4},{6,7},{7,6},{8,9},{9,8},{10,11... | collective-permute-start | bytes 6291464 | tf_op jit(solution)/shard_map/ppermute | solution.py:735
  116.5 27.4 %collective-permute-start.26 = (bf16[512,1024]{1,0:T(8,128)(2,1)S(1)}, bf16[512,1024]{1,0:T(8,128)(2,1)}, u32[]{:S(2)}, u32[]{:S(2)}) collective-permute-start(bf16[512,1024]{1,0:T(8,128)(2,1)S(1)} %collective-permute-done.25.refs_6_), channel_id=1, source_target_pairs={{0,2},{1,3},{2,0},{3,1},{4,6},{5,7},{6,4},{7,5},{8,10},{9,11},{10,... | collective-permute-start | bytes 3145736 | tf_op jit(solution)/shard_map/ppermute | solution.py:738
  122.6 0.7 copy-start.5
  130.1 13.4 %all-to-all-start.1 = ((bf16[8,64,384]{2,1,0:T(8,128)(2,1)}), bf16[8,64,384]{2,1,0:T(8,128)(2,1)S(1)}, u32[]{:S(2)}, u32[]{:S(2)}) async-start(bf16[8,64,384]{2,1,0:T(8,128)(2,1)} %triple_heads.1), calls=%async_computation.1 | async-start | bytes 786432 | tf_op jit(solution)/shard_map/all_to_all | solution.py:741
  133.5 28.7 %collective-permute-start.30 = (bf16[256,2048]{1,0:T(8,128)(2,1)}, bf16[256,2048]{1,0:T(8,128)(2,1)}, u32[]{:S(2)}, u32[]{:S(2)}) collective-permute-start(bf16[256,2048]{1,0:T(8,128)(2,1)} %collective-permute-done.29.refs_10_), channel_id=1, source_target_pairs={{0,2},{1,3},{2,0},{3,1},{4,6},{5,7},{6,4},{7,5},{8,10},{9,11},{10,... | collective-permute-start | bytes 3145736 | tf_op jit(solution)/shard_map/ppermute | solution.py:738
  143.4 18.8 %collective-permute-start.19 = (bf16[8,2,32,384]{3,2,1,0:T(8,128)(2,1)S(1)}, bf16[8,2,32,384]{3,2,1,0:T(8,128)(2,1)S(1)}, u32[]{:S(2)}, u32[]{:S(2)}) collective-permute-start(bf16[8,2,32,384]{3,2,1,0:T(8,128)(2,1)S(1)} %bitcast.22), channel_id=1, source_target_pairs={{0,1},{1,0},{2,3},{3,2},{4,5},{5,4},{6,7},{7,6},{8,9},{9,8},{10,11... | collective-permute-start | bytes 1179656 | tf_op jit(solution)/shard_map/ppermute | solution.py:735
  143.4 40.6 %collective-permute-start.27 = (bf16[512,1024]{1,0:T(8,128)(2,1)S(1)}, bf16[512,1024]{1,0:T(8,128)(2,1)}, u32[]{:S(2)}, u32[]{:S(2)}) collective-permute-start(bf16[512,1024]{1,0:T(8,128)(2,1)S(1)} %collective-permute-done.25.refs_6_), channel_id=1, source_target_pairs={{0,1},{1,0},{2,3},{3,2},{4,5},{5,4},{6,7},{7,6},{8,9},{9,8},{10,11... | collective-permute-start | bytes 3145736 | tf_op jit(solution)/shard_map/ppermute | solution.py:735
  143.9 41.1 %collective-permute-start.31 = (bf16[256,2048]{1,0:T(8,128)(2,1)}, bf16[256,2048]{1,0:T(8,128)(2,1)}, u32[]{:S(2)}, u32[]{:S(2)}) collective-permute-start(bf16[256,2048]{1,0:T(8,128)(2,1)} %collective-permute-done.29.refs_10_), channel_id=1, source_target_pairs={{0,1},{1,0},{2,3},{3,2},{4,5},{5,4},{6,7},{7,6},{8,9},{9,8},{10,11... | collective-permute-start | bytes 3145736 | tf_op jit(solution)/shard_map/ppermute | solution.py:735
  162.2 26.1 %collective-permute-start.28 = (bf16[512,1024]{1,0:T(8,128)(2,1)}, bf16[512,1024]{1,0:T(8,128)(2,1)}, u32[]{:S(2)}, u32[]{:S(2)}) collective-permute-start(bf16[512,1024]{1,0:T(8,128)(2,1)} %collective-permute-done.26.refs_7_), channel_id=1, source_target_pairs={{0,1},{1,0},{2,3},{3,2},{4,5},{5,4},{6,7},{7,6},{8,9},{9,8},{10,11... | collective-permute-start | bytes 3145736 | tf_op jit(solution)/shard_map/ppermute | solution.py:735
  162.2 26.1 %collective-permute-start.32 = (bf16[256,2048]{1,0:T(8,128)(2,1)}, bf16[256,2048]{1,0:T(8,128)(2,1)}, u32[]{:S(2)}, u32[]{:S(2)}) collective-permute-start(bf16[256,2048]{1,0:T(8,128)(2,1)} %collective-permute-done.30.refs_11_), channel_id=1, source_target_pairs={{0,1},{1,0},{2,3},{3,2},{4,5},{5,4},{6,7},{7,6},{8,9},{9,8},{10,11... | collective-permute-start | bytes 3145736 | tf_op jit(solution)/shard_map/ppermute | solution.py:735
  164.7 0.7 copy-start.8
  165.4 10.7 %all-to-all-start.2 = ((bf16[8,64,128]{2,1,0:T(8,128)(2,1)}), bf16[8,64,128]{2,1,0:T(8,128)(2,1)S(1)}, u32[]{:S(2)}, u32[]{:S(2)}) async-start(bf16[8,64,128]{2,1,0:T(8,128)(2,1)} %bitcast.26), calls=%async_computation.2 | async-start | bytes 262144 | tf_op jit(solution)/shard_map/all_to_all | solution.py:741
  168.7 15.0 %copy-start.6 = (f32[32,2048]{1,0:T(8,128)S(1)}, f32[32,2048]{1,0:T(8,128)}, u32[]{:S(2)}) copy-start(f32[32,2048]{1,0:T(8,128)} %copy-done.5) | copy-start | bytes 786436
  176.1 18.9 %copy-start = (bf16[2048,1024]{1,0:T(8,128)(2,1)S(1)}, bf16[2048,1024]{1,0:T(8,128)(2,1)}, u32[]{:S(2)}) copy-start(bf16[2048,1024]{1,0:T(8,128)(2,1)} %refs_4_.1) | copy-start | bytes 12582916
  178.7 5.0 %collective-permute-start.21 = (bf16[32,2048]{1,0:T(8,128)(2,1)S(1)}, bf16[32,2048]{1,0:T(8,128)(2,1)S(1)}, u32[]{:S(2)}, u32[]{:S(2)}) collective-permute-start(bf16[32,2048]{1,0:T(8,128)(2,1)S(1)} %get-tuple-element.45), channel_id=1, source_target_pairs={{0,2},{1,3},{2,0},{3,1},{4,6},{5,7},{6,4},{7,5},{8,10},{9,11},{10,... | collective-permute-start | bytes 393224 | tf_op jit(solution)/shard_map/ppermute | solution.py:738
  183.9 7.1 %collective-permute-start.22 = (bf16[32,2048]{1,0:T(8,128)(2,1)S(1)}, bf16[32,2048]{1,0:T(8,128)(2,1)S(1)}, u32[]{:S(2)}, u32[]{:S(2)}) collective-permute-start(bf16[32,2048]{1,0:T(8,128)(2,1)S(1)} %get-tuple-element.47.refs_0_), channel_id=1, source_target_pairs={{0,8},{4,12},{8,0},{12,4},{16,24},{20,28},{24,16},{28,20},{1,9},{5... | collective-permute-start | bytes 393224 | tf_op jit(solution)/shard_map/ppermute | solution.py:746
  184.0 11.0 %collective-permute-start.23 = (bf16[32,2048]{1,0:T(8,128)(2,1)S(1)}, bf16[32,2048]{1,0:T(8,128)(2,1)S(1)}, u32[]{:S(2)}, u32[]{:S(2)}) collective-permute-start(bf16[32,2048]{1,0:T(8,128)(2,1)S(1)} %get-tuple-element.47.refs_0_), channel_id=1, source_target_pairs={{0,16},{4,20},{8,24},{12,28},{16,0},{20,4},{24,8},{28,12},{1,17},{... | collective-permute-start | bytes 393224 | tf_op jit(solution)/shard_map/ppermute | solution.py:746
  185.0 10.0 %collective-permute-start.24 = (bf16[32,2048]{1,0:T(8,128)(2,1)S(1)}, bf16[32,2048]{1,0:T(8,128)(2,1)S(1)}, u32[]{:S(2)}, u32[]{:S(2)}) collective-permute-start(bf16[32,2048]{1,0:T(8,128)(2,1)S(1)} %get-tuple-element.47.refs_0_), channel_id=1, source_target_pairs={{0,24},{4,28},{8,16},{12,20},{16,8},{20,12},{24,0},{28,4},{1,25},{... | collective-permute-start | bytes 393224 | tf_op jit(solution)/shard_map/ppermute | solution.py:746
  202.7 5.9 %collective-permute-start.33 = (bf16[32,2048]{1,0:T(8,128)(2,1)S(1)}, bf16[32,2048]{1,0:T(8,128)(2,1)S(1)}, u32[]{:S(2)}, u32[]{:S(2)}) collective-permute-start(bf16[32,2048]{1,0:T(8,128)(2,1)S(1)} %get-tuple-element.50), channel_id=1, source_target_pairs={{0,8},{4,12},{8,0},{12,4},{16,24},{20,28},{24,16},{28,20},{1,9},{5... | collective-permute-start | bytes 393224 | tf_op jit(solution)/shard_map/ppermute | solution.py:746
  204.7 10.8 %collective-permute-start.34 = (bf16[32,2048]{1,0:T(8,128)(2,1)S(1)}, bf16[32,2048]{1,0:T(8,128)(2,1)S(1)}, u32[]{:S(2)}, u32[]{:S(2)}) collective-permute-start(bf16[32,2048]{1,0:T(8,128)(2,1)S(1)} %get-tuple-element.51), channel_id=1, source_target_pairs={{0,16},{4,20},{8,24},{12,28},{16,0},{20,4},{24,8},{28,12},{1,17},{... | collective-permute-start | bytes 393224 | tf_op jit(solution)/shard_map/ppermute | solution.py:746
  205.1 10.5 %collective-permute-start.35 = (bf16[32,2048]{1,0:T(8,128)(2,1)S(1)}, bf16[32,2048]{1,0:T(8,128)(2,1)S(1)}, u32[]{:S(2)}, u32[]{:S(2)}) collective-permute-start(bf16[32,2048]{1,0:T(8,128)(2,1)S(1)} %get-tuple-element.52), channel_id=1, source_target_pairs={{0,24},{4,28},{8,16},{12,20},{16,8},{20,12},{24,0},{28,4},{1,25},{... | collective-permute-start | bytes 393224 | tf_op jit(solution)/shard_map/ppermute | solution.py:746
